TPU v7x, 256 devices: a whole 4x4x8 slice. The times are simulated.
256 devices in a mesh: lat: 64 (over x, y_hi, z), lon: 4 (over y_lo, core).
Axes of the slice: x: 4, y: 4 (y_hi: 2, y_lo: 2; y = y_hi * 2 + y_lo), z: 8, core: 2. Of those that a mesh axis runs over, the one named last changes fastest.
Arguments:
- tracer: float32 [32, 1536, 1152], P(None, 'lat', 'lon'), may hold values from -6 to 6
- wind_u: float32 [32, 1536, 1152], P(None, 'lat', 'lon'), may hold values from -2.5 to 2.5
- wind_v: float32 [32, 1536, 1152], P(None, 'lat', 'lon'), may hold values from -2.5 to 2.5
- ocean_temp: float32 [4, 2048, 3584], P(None, 'lat', 'lon'), may hold values from -6 to 6
- land_mask: int32 [2048, 3584], P('lat', 'lon'), may hold values 0 or 1
- remap_rows: int32 [2048, 3584], P('lat', 'lon'), may hold values from 0 to 1535, as said below
- remap_cols: int32 [2048, 3584], P('lat', 'lon'), may hold values from 0 to 1151, as said below
- polar_rows: int32 [192], replicated, may hold values from 0 to 1535, as said below
Outputs:
- tracer_out: float32 [32, 1536, 1152], P(None, 'lat', 'lon')
- ocean_out: float32 [4, 2048, 3584], P(None, 'lat', 'lon')
Inputs may be any that keep to these rules, and one draw needn't show every extreme that they name: `remap_rows`: for an ocean cell in row block b of 32 rows, an atmosphere row from b * 24 - 1 to (b + 1) * 24, within the grid. `remap_cols`: for an ocean cell in column block c of 896 columns, an atmosphere column from c * 288 - 1 to (c + 1) * 288, modulo 1152. `polar_rows`: distinct rows, each among the 192 rows nearest either pole.
All inputs are finite; a program needn't handle non-finite values. No bound on the sum of `land_mask` on one device may be relied on, other than what follows from the above.
Results may differ from a plain program's by a relative error of at most 0.0001.
Values sent between devices are 32-bit elements; how exact they have to be, the bound alone decides.
No kernel may reach another device: no remote copies, remote signals or barrier semaphores. Data moves between devices by JAX's collectives and lax.ppermute only.
A program may use at most 128 MiB of HBM per device.

v0:
```python
import math

import jax
import jax.numpy as jnp
from jax import lax
from jax.sharding import PartitionSpec as P

STEPS = 2
OSTEPS = 2


advect_coef = 0.2
diffuse_coef = 0.1
flux_coef = 0.25
ocean_diffuse = 0.15
vertical_mix = 0.2
highest = lax.Precision.HIGHEST


def padded_2(shard, sides, width, wrap):
    for axis, dim in sides:
        count, length = (lax.axis_size(axis), shard.shape[dim])
        up = [(i, (i + 1) % count) for i in range(count if wrap else count - 1)]
        down = [(j, i) for i, j in up]
        last = lax.slice_in_dim(shard, length - width, length, axis=dim)
        first = lax.slice_in_dim(shard, 0, width, axis=dim)
        before = lax.ppermute(last, axis, up)
        after = lax.ppermute(first, axis, down)
        shard = jnp.concatenate([before, shard, after], axis=dim)
    return shard


def damp_table(row_index, polar_rows, wave_numbers, lat_total, band_rows, lon_total):
    latitude_cos = jnp.sin(math.pi * (row_index.astype(jnp.float32) + 0.5) / lat_total)
    ratio = latitude_cos / math.sin(math.pi * band_rows / lat_total)
    wave_sine = jnp.sin(math.pi * wave_numbers / lon_total)
    safe_sine = jnp.where(wave_numbers > 0.5, wave_sine, 1.0)
    damping = jnp.where(
        wave_numbers[None, :] > 0.5, jnp.minimum(1.0, ratio[:, None] / safe_sine[None, :]), 1.0
    )
    listed = jnp.any(row_index[:, None] == polar_rows[None, :], axis=1)
    return jnp.where(listed[:, None], damping, 1.0)


def make_basis(lon_total):
    half_circle = lon_total // 2
    points = jnp.arange(lon_total, dtype=jnp.int32)
    cos_waves = jnp.arange(half_circle + 1, dtype=jnp.int32)
    sin_waves = jnp.arange(1, half_circle, dtype=jnp.int32)
    cos_phase = points[:, None] * cos_waves[None, :] % lon_total
    sin_phase = points[:, None] * sin_waves[None, :] % lon_total
    basis = jnp.concatenate(
        [
            jnp.cos(2.0 * math.pi * cos_phase.astype(jnp.float32) / lon_total),
            jnp.sin(2.0 * math.pi * sin_phase.astype(jnp.float32) / lon_total),
        ],
        axis=1,
    )
    waves_all = jnp.concatenate([cos_waves, sin_waves])
    wave_numbers = waves_all.astype(jnp.float32)
    weight = jnp.where(
        (waves_all == 0) | (waves_all == half_circle), 1.0 / lon_total, 2.0 / lon_total
    )
    return (basis, wave_numbers, weight)


def rim(field):
    wider = padded_2(field, (("lat", 1),), 1, False)
    return padded_2(wider, (("lon", 2),), 1, True)


def atmos_step(tracer_now, wind_u, wind_v):
    padded = rim(tracer_now)
    east_side = padded[:, 1:-1, 2:]
    west_side = padded[:, 1:-1, :-2]
    north_side = padded[:, 2:, 1:-1]
    south_side = padded[:, :-2, 1:-1]
    advect = wind_u * (east_side - west_side) + wind_v * (north_side - south_side)
    spread_sum = east_side + west_side + north_side + south_side - 4.0 * tracer_now
    return tracer_now - advect_coef * advect + diffuse_coef * spread_sum


def back_project(scaled, target_basis):
    return lax.dot_general(
        scaled,
        target_basis,
        (((1,), (1,)), ((), ())),
        precision=highest,
        preferred_element_type=jnp.float32,
    )


def ocean_step(temp, sea, air_temp, air_speed):
    top_level = temp[0] + sea * flux_coef * air_speed * (air_temp - temp[0])
    temp = jnp.concatenate([top_level[None], temp[1:]], axis=0)
    padded = rim(jnp.concatenate([temp, sea[None]], axis=0))
    level_count = temp.shape[0]
    temp_rim = padded[:level_count]
    sea_rim = padded[level_count]
    lateral = sea * (
        sea_rim[1:-1, 2:] * (temp_rim[:, 1:-1, 2:] - temp)
        + sea_rim[1:-1, :-2] * (temp_rim[:, 1:-1, :-2] - temp)
        + sea_rim[2:, 1:-1] * (temp_rim[:, 2:, 1:-1] - temp)
        + sea_rim[:-2, 1:-1] * (temp_rim[:, :-2, 1:-1] - temp)
    )
    temp = temp + ocean_diffuse * lateral
    upper = jnp.concatenate([temp[:1], temp[:-1]], axis=0)
    lower = jnp.concatenate([temp[1:], temp[-1:]], axis=0)
    return temp + vertical_mix * sea * (upper + lower - 2.0 * temp)


def per_device(tracer, wind_u, wind_v, ocean_temp, land_mask, remap_rows, remap_cols, polar_rows):
    levels, row_count, lon_local = tracer.shape
    lat_devices = lax.axis_size("lat")
    lon_devices = lax.axis_size("lon")
    lat_total = row_count * lat_devices
    lon_total = lon_local * lon_devices
    band_devices = lat_devices // 8
    band_rows = band_devices * row_count
    lat_place = lax.axis_index("lat")
    lon_place = lax.axis_index("lon")
    basis, wave_numbers, weight = make_basis(lon_total)
    own_basis = lax.dynamic_slice_in_dim(basis, lon_place * lon_local, lon_local, 0)
    own_rows = lat_place * row_count + jnp.arange(row_count, dtype=jnp.int32)
    line_count = levels * row_count
    tracer_now = tracer
    for step_index in range(STEPS):
        tracer_now = atmos_step(tracer_now, wind_u, wind_v)
        row_weights = (
            damp_table(own_rows, polar_rows, wave_numbers, lat_total, band_rows, lon_total)
            * weight[None, :]
        )
        lines = tracer_now.reshape(line_count, lon_local)
        coeffs = jnp.dot(
            lax.all_gather(lines, "lon", axis=1, tiled=True),
            basis,
            precision=highest,
            preferred_element_type=jnp.float32,
        )
        scaled = (coeffs.reshape(levels, row_count, lon_total) * row_weights[None]).reshape(
            line_count, lon_total
        )
        tracer_now = back_project(scaled, own_basis).reshape(levels, row_count, lon_local)
    bottom = jnp.stack(
        [tracer_now[levels - 1], jnp.abs(wind_u[levels - 1]) + jnp.abs(wind_v[levels - 1]) + 0.5]
    )
    bottom_rim = rim(bottom)
    local_row = remap_rows - lat_place * row_count + 1
    local_col = (remap_cols - lon_place * lon_local + 1) % lon_total
    flat_index = local_row * (lon_local + 2) + local_col
    picked = jnp.take(bottom_rim.reshape(2, -1), flat_index, axis=1)
    air_temp = picked[0]
    air_speed = picked[1]
    sea = land_mask.astype(jnp.float32)
    temp = ocean_temp
    for step_index in range(OSTEPS):
        temp = ocean_step(temp, sea, air_temp, air_speed)
    return (tracer_now, temp)


def solution(mesh):
    in_specs = (
        P(None, "lat", "lon"),
        P(None, "lat", "lon"),
        P(None, "lat", "lon"),
        P(None, "lat", "lon"),
        P("lat", "lon"),
        P("lat", "lon"),
        P("lat", "lon"),
        P(),
    )
    out_specs = (P(None, "lat", "lon"), P(None, "lat", "lon"))
    return jax.shard_map(
        per_device, mesh=mesh, in_specs=in_specs, out_specs=out_specs, check_vma=False
    )
```

profile of v0, /device:TPU:3, one launch (start us, length us, event | category | flops | bytes accessed | tf_op | source)
XLA Modules:
  0.0 390.3 jit_solution(18377480665657922847)
XLA Ops:
  7.2 1.3 fusion.94
  8.5 3.7 collective-permute-start
  12.2 8.5 %collective-permute-start.1 = (f32[32,1,288]{2,1,0:T(1,128)S(1)}, f32[32,1,288]{2,1,0:T(1,128)S(1)}, u32[]{:S(2)}, u32[]{:S(2)}) collective-permute-start(f32[32,1,288]{2,1,0:T(1,128)S(1)} %get-tuple-element.13), channel_id=1, source_target_pairs={{4,0},{8,4},{12,8},{16,12},{20,16},{24,20},{28,24},{32,28},{36,32}... | collective-permute-start | bytes 110600 | tf_op jit(solution)/shard_map/ppermute | solution.py:28
  20.7 1.1 collective-permute-done.1
  21.8 1.4 pad_maximum_fusion.34
  23.3 1.6 collective-permute-start.2
  25.2 11.8 %collective-permute-done.2 = f32[32,26,1]{2,1,0:T(8,128)S(1)} collective-permute-done((f32[32,26,1]{2,1,0:T(8,128)S(1)}, f32[32,26,1]{2,1,0:T(8,128)S(1)}, u32[]{:S(2)}, u32[]{:S(2)}) %collective-permute-start.2) | collective-permute-done | bytes 3360 | tf_op jit(solution)/shard_map/ppermute | solution.py:28
  37.1 2.8 multiply_add_fusion.1
  39.8 1.3 copy.30
  41.8 11.0 %fusion.2 = f32[1152,577]{1,0:T(8,128)S(1)} fusion(), kind=kLoop, calls=%fused_computation.10 | loop fusion | flops 5982336 | bytes 2658816 | tf_op jit(solution)/shard_map/cos | solution.py:54
  52.9 12.6 %fusion.5 = f32[1152,575]{1,0:T(8,128)} fusion(s32[575]{0:T(1024)S(1)} %iota_add_fusion), kind=kLoop, calls=%fused_computation.13 | loop fusion | flops 5961600 | bytes 2651900 | tf_op jit(solution)/shard_map/sin | solution.py:55
  65.6 21.0 %all-gather.3.cloned.1.call-done = f32[768,1152]{0,1:T(8,128)} async-done(((f32[768,288]{0,1:T(8,128)}), f32[768,1152]{0,1:T(8,128)}) %all-gather.3.cloned.1.call-update) | async-done | bytes 3538960 | tf_op jit(solution)/shard_map/all_gather | solution.py:135
  86.5 21.0 %bitcast_multiply_fusion.1 = f32[768,1152]{1,0:T(8,128)S(1)} fusion(f32[768,1152]{0,1:T(8,128)} %all-gather.3.cloned.1.call-done, f32[1152,575]{1,0:T(8,128)} %fusion.5, f32[1152,577]{1,0:T(8,128)S(1)} %fusion.2, f32[24,1152]{1,0:T(8,128)S(1)} %fusion.87), kind=kOutput, calls=%fused_computation.5 | convolution fusion | flops 12232802304 | bytes 12496896 | tf_op jit(solution)/shard_map/dot_general | solution.py:134
  107.5 6.2 %fusion.13 = f32[32,24,288]{2,1,0:T(8,128)S(1)} fusion(f32[32,24,1152]{2,1,0:T(8,128)S(1)} %bitcast.57, s32[]{:T(128)S(6)} %select_n.72, f32[1152,577]{1,0:T(8,128)S(1)} %fusion.2, f32[1152,575]{1,0:T(8,128)S(1)} %copy-done), kind=kOutput, calls=%fused_computation.23 | convolution fusion | flops 3057979392 | bytes 9732100 | tf_op jit(solution)/shard_map/dot_general | solution.py:84
  113.8 3.3 collective-permute-start.4
  117.2 6.6 %collective-permute-start.5 = (f32[32,1,288]{2,1,0:T(1,128)S(1)}, f32[32,1,288]{2,1,0:T(1,128)S(1)}, u32[]{:S(2)}, u32[]{:S(2)}) collective-permute-start(f32[32,1,288]{2,1,0:T(1,128)S(1)} %get-tuple-element.11), channel_id=1, source_target_pairs={{4,0},{8,4},{12,8},{16,12},{20,16},{24,20},{28,24},{32,28},{36,32}... | collective-permute-start | bytes 110600 | tf_op jit(solution)/shard_map/ppermute | solution.py:28
  124.0 0.9 collective-permute-done.5
  125.2 1.3 collective-permute-start.6
  126.5 1.0 collective-permute-start.7
  127.5 12.6 %collective-permute-done.6 = f32[32,26,1]{2,1,0:T(8,128)S(1)} collective-permute-done((f32[32,26,1]{2,1,0:T(8,128)S(1)}, f32[32,26,1]{2,1,0:T(8,128)S(1)}, u32[]{:S(2)}, u32[]{:S(2)}) %collective-permute-start.6) | collective-permute-done | bytes 3360 | tf_op jit(solution)/shard_map/ppermute | solution.py:28
  140.0 2.5 multiply_add_fusion
  142.6 2.5 copy.31
  145.4 1.1 compare_and_fusion
  147.2 0.9 broadcast_clamp_fusion
  148.1 41.0 %all-gather.5.cloned.1.call-done = f32[768,1152]{0,1:T(8,128)} async-done(((f32[768,288]{0,1:T(8,128)}), f32[768,1152]{0,1:T(8,128)}) %all-gather.5.cloned.1.call-update) | async-done | bytes 3538960 | tf_op jit(solution)/shard_map/all_gather | solution.py:135
  189.1 21.0 %bitcast_multiply_fusion = f32[768,1152]{1,0:T(8,128)S(1)} fusion(f32[768,1152]{0,1:T(8,128)} %all-gather.5.cloned.1.call-done, f32[1152,575]{1,0:T(8,128)} %fusion.5, f32[1152,577]{1,0:T(8,128)S(1)} %fusion.2, f32[24,1152]{1,0:T(8,128)S(1)} %fusion.87), kind=kOutput, calls=%fused_computation.4 | convolution fusion | flops 12232802304 | bytes 12496896 | tf_op jit(solution)/shard_map/dot_general | solution.py:134
  210.0 4.1 %fusion.90 = f32[768,288]{0,1:T(8,128)S(1)} fusion(f32[768,1152]{1,0:T(8,128)S(1)} %bitcast_multiply_fusion, s32[]{:T(128)S(6)} %select_n.72, f32[1152,577]{1,0:T(8,128)S(1)} %fusion.2, f32[1152,575]{1,0:T(8,128)S(1)} %copy-done.1), kind=kOutput, calls=%fused_computation.184 | convolution fusion | flops 3057979392 | bytes 9732100 | tf_op jit(solution)/shard_map/dot_general | solution.py:84
  214.1 0.9 copy-done.6
  215.3 3.3 collective-permute-start.8
  218.6 6.6 %collective-permute-start.9 = (f32[2,1,288]{1,2,0:T(8,128)S(1)}, f32[2,1,288]{1,2,0:T(8,128)S(1)}, u32[]{:S(2)}, u32[]{:S(2)}) collective-permute-start(f32[2,1,288]{1,2,0:T(8,128)S(1)} %get-tuple-element.31), channel_id=1, source_target_pairs={{4,0},{8,4},{12,8},{16,12},{20,16},{24,20},{28,24},{32,28},{36,32}... | collective-permute-start | bytes 6920 | tf_op jit(solution)/shard_map/ppermute | solution.py:28
  225.4 5.3 %collective-permute-done.8 = f32[2,1,288]{1,2,0:T(8,128)S(1)} collective-permute-done((f32[2,1,288]{1,2,0:T(8,128)S(1)}, f32[2,1,288]{1,2,0:T(8,128)S(1)}, u32[]{:S(2)}, u32[]{:S(2)}) %collective-permute-start.8) | collective-permute-done | bytes 2336 | tf_op jit(solution)/shard_map/ppermute | solution.py:27
  231.9 1.2 collective-permute-start.10
  233.2 0.9 collective-permute-done.10
  234.1 2.3 collective-permute-done.11
  236.8 2.7 copy.39
  239.5 97.5 %gather_fusion = f32[28672,2]{1,0:T(8,128)} fusion(f32[2,7540]{0,1:T(8,128)} %copy.39, s32[28672]{0:T(1024)S(1)} %broadcast_clamp_fusion), kind=kCustom, calls=%fused_computation | custom fusion | bytes 573440 | tf_op jit(solution)/shard_map/jit(_take)/gather | solution.py:151
  336.9 9.0 %copy.40 = f32[32,896,2]{1,0,2:T(8,128)S(1)} copy(f32[32,896,2]{2,1,0:T(8,128)} %bitcast.56) | data formatting | bytes 458752 | tf_op jit(solution)/shard_map/jit(_take)/gather | solution.py:151
  346.1 1.9 collective-permute-start.12
  348.0 9.2 %collective-permute-start.13 = (f32[5,1,896]{2,1,0:T(1,128)S(1)}, f32[5,1,896]{2,1,0:T(1,128)S(1)}, u32[]{:S(2)}, u32[]{:S(2)}) collective-permute-start(f32[5,1,896]{2,1,0:T(1,128)S(1)} %get-tuple-element.20), channel_id=1, source_target_pairs={{4,0},{8,4},{12,8},{16,12},{20,16},{24,20},{28,24},{32,28},{36,32}... | collective-permute-start | bytes 53768 | tf_op jit(solution)/shard_map/ppermute | solution.py:28
  357.3 0.9 collective-permute-done.13
  358.9 1.4 collective-permute-done.14
  360.3 2.7 collective-permute-done.15
  364.6 2.1 collective-permute-start.16
  366.6 9.0 %collective-permute-start.17 = (f32[5,1,896]{2,1,0:T(1,128)S(1)}, f32[5,1,896]{2,1,0:T(1,128)S(1)}, u32[]{:S(2)}, u32[]{:S(2)}) collective-permute-start(f32[5,1,896]{2,1,0:T(1,128)S(1)} %get-tuple-element.18), channel_id=1, source_target_pairs={{4,0},{8,4},{12,8},{16,12},{20,16},{24,20},{28,24},{32,28},{36,32}... | collective-permute-start | bytes 53768 | tf_op jit(solution)/shard_map/ppermute | solution.py:28
  375.6 0.9 collective-permute-done.17
  377.2 1.4 copy.32
  378.7 2.4 collective-permute-done.19
  382.0 1.3 fusion.68
  (92 shorter events, 8.8 us)
Async XLA Ops:
  7.2 79.3 %all-gather.3.cloned.1.call-start = ((), (), s32[]{:S(2)}) async-start(), calls=%async_computation | async-start | bytes 4423680 | tf_op jit(solution)/shard_map/all_gather | solution.py:135
  7.2 29.9 %copy-start.3 = (f32[32,24,288]{2,1,0:T(8,128)S(1)}, f32[32,24,288]{2,1,0:T(8,128)}, u32[]{:S(2)}) copy-start(f32[32,24,288]{2,1,0:T(8,128)} %param.9) | copy-start | bytes 2654212
  8.5 28.6 %copy-start.2 = (f32[32,24,288]{2,1,0:T(8,128)S(1)}, f32[32,24,288]{2,1,0:T(8,128)}, u32[]{:S(2)}) copy-start(f32[32,24,288]{2,1,0:T(8,128)} %param.8) | copy-start | bytes 2654212
  8.5 12.2 %collective-permute-start = (f32[32,1,288]{2,1,0:T(1,128)S(1)}, f32[32,1,288]{2,1,0:T(1,128)S(1)}, u32[]{:S(2)}, u32[]{:S(2)}) collective-permute-start(f32[32,1,288]{2,1,0:T(1,128)S(1)} %get-tuple-element.12), channel_id=1, source_target_pairs={{0,4},{4,8},{8,12},{12,16},{16,20},{20,24},{24,28},{28,32},{32,36}... | collective-permute-start | bytes 110600 | tf_op jit(solution)/shard_map/ppermute | solution.py:27
  12.2 9.6 %collective-permute-start.1 = (f32[32,1,288]{2,1,0:T(1,128)S(1)}, f32[32,1,288]{2,1,0:T(1,128)S(1)}, u32[]{:S(2)}, u32[]{:S(2)}) collective-permute-start(f32[32,1,288]{2,1,0:T(1,128)S(1)} %get-tuple-element.13), channel_id=1, source_target_pairs={{4,0},{8,4},{12,8},{16,12},{20,16},{24,20},{28,24},{32,28},{36,32}... | collective-permute-start | bytes 110600 | tf_op jit(solution)/shard_map/ppermute | solution.py:28
  23.3 13.8 %collective-permute-start.2 = (f32[32,26,1]{2,1,0:T(8,128)S(1)}, f32[32,26,1]{2,1,0:T(8,128)S(1)}, u32[]{:S(2)}, u32[]{:S(2)}) collective-permute-start(f32[32,26,1]{2,1,0:T(8,128)S(1)} %get-tuple-element.9), channel_id=1, source_target_pairs={{1,0},{2,1},{3,2},{0,3},{5,4},{6,5},{7,6},{4,7},{9,8},{10,9},{11,1... | collective-permute-start | bytes 9992 | tf_op jit(solution)/shard_map/ppermute | solution.py:28
  24.9 12.2 %collective-permute-start.3 = (f32[32,26,1]{2,1,0:T(8,128)S(1)}, f32[32,26,1]{2,1,0:T(8,128)S(1)}, u32[]{:S(2)}, u32[]{:S(2)}) collective-permute-start(f32[32,26,1]{2,1,0:T(8,128)S(1)} %get-tuple-element.8), channel_id=1, source_target_pairs={{0,1},{1,2},{2,3},{3,0},{4,5},{5,6},{6,7},{7,4},{8,9},{9,10},{10,1... | collective-permute-start | bytes 9992 | tf_op jit(solution)/shard_map/ppermute | solution.py:27
  39.8 1.8 copy-start.10
  41.1 147.9 %all-gather.5.cloned.1.call-start = ((), (), s32[]{:S(2)}) async-start(), calls=%async_computation.1 | async-start | bytes 4423680 | tf_op jit(solution)/shard_map/all_gather | solution.py:135
  86.5 21.0 %copy-start = (f32[1152,575]{1,0:T(8,128)S(1)}, f32[1152,575]{1,0:T(8,128)}, u32[]{:S(2)}) copy-start(f32[1152,575]{1,0:T(8,128)} %fusion.5) | copy-start | bytes 7948804
  113.7 26.3 %copy-start.5 = (f32[32,24,288]{2,1,0:T(8,128)S(1)}, f32[32,24,288]{2,1,0:T(8,128)}, u32[]{:S(2)}) copy-start(f32[32,24,288]{2,1,0:T(8,128)} %param.10) | copy-start | bytes 2654212
  113.8 26.2 %copy-start.4 = (f32[32,24,288]{2,1,0:T(8,128)S(1)}, f32[32,24,288]{2,1,0:T(8,128)}, u32[]{:S(2)}) copy-start(f32[32,24,288]{2,1,0:T(8,128)} %param.9) | copy-start | bytes 2654212
  113.8 10.2 %collective-permute-start.4 = (f32[32,1,288]{2,1,0:T(1,128)S(1)}, f32[32,1,288]{2,1,0:T(1,128)S(1)}, u32[]{:S(2)}, u32[]{:S(2)}) collective-permute-start(f32[32,1,288]{2,1,0:T(1,128)S(1)} %get-tuple-element.10), channel_id=1, source_target_pairs={{0,4},{4,8},{8,12},{12,16},{16,20},{20,24},{24,28},{28,32},{32,36}... | collective-permute-start | bytes 110600 | tf_op jit(solution)/shard_map/ppermute | solution.py:27
  117.2 7.8 %collective-permute-start.5 = (f32[32,1,288]{2,1,0:T(1,128)S(1)}, f32[32,1,288]{2,1,0:T(1,128)S(1)}, u32[]{:S(2)}, u32[]{:S(2)}) collective-permute-start(f32[32,1,288]{2,1,0:T(1,128)S(1)} %get-tuple-element.11), channel_id=1, source_target_pairs={{4,0},{8,4},{12,8},{16,12},{20,16},{24,20},{28,24},{32,28},{36,32}... | collective-permute-start | bytes 110600 | tf_op jit(solution)/shard_map/ppermute | solution.py:28
  125.2 14.8 %collective-permute-start.6 = (f32[32,26,1]{2,1,0:T(8,128)S(1)}, f32[32,26,1]{2,1,0:T(8,128)S(1)}, u32[]{:S(2)}, u32[]{:S(2)}) collective-permute-start(f32[32,26,1]{2,1,0:T(8,128)S(1)} %get-tuple-element.7), channel_id=1, source_target_pairs={{1,0},{2,1},{3,2},{0,3},{5,4},{6,5},{7,6},{4,7},{9,8},{10,9},{11,1... | collective-permute-start | bytes 9992 | tf_op jit(solution)/shard_map/ppermute | solution.py:28
  126.5 13.5 %collective-permute-start.7 = (f32[32,26,1]{2,1,0:T(8,128)S(1)}, f32[32,26,1]{2,1,0:T(8,128)S(1)}, u32[]{:S(2)}, u32[]{:S(2)}) collective-permute-start(f32[32,26,1]{2,1,0:T(8,128)S(1)} %get-tuple-element.6), channel_id=1, source_target_pairs={{0,1},{1,2},{2,3},{3,0},{4,5},{5,6},{6,7},{7,4},{8,9},{9,10},{10,1... | collective-permute-start | bytes 9992 | tf_op jit(solution)/shard_map/ppermute | solution.py:27
  142.6 2.6 slice-start
  142.6 2.7 slice-start.1
  189.1 21.0 %copy-start.1 = (f32[1152,575]{1,0:T(8,128)S(1)}, f32[1152,575]{1,0:T(8,128)}, u32[]{:S(2)}) copy-start(f32[1152,575]{1,0:T(8,128)} %fusion.5) | copy-start | bytes 7948804
  214.1 0.9 copy-start.6
  215.1 18.0 %copy-start.8 = (s32[32,896]{1,0:T(8,128)S(1)}, s32[32,896]{1,0:T(8,128)}, u32[]{:S(2)}) copy-start(s32[32,896]{1,0:T(8,128)} %param.12) | copy-start | bytes 344068
  215.3 17.9 %copy-start.9 = (f32[4,32,896]{2,1,0:T(8,128)S(1)}, f32[4,32,896]{2,1,0:T(8,128)}, u32[]{:S(2)}) copy-start(f32[4,32,896]{2,1,0:T(8,128)} %param.11) | copy-start | bytes 1376260
  215.3 15.4 %collective-permute-start.8 = (f32[2,1,288]{1,2,0:T(8,128)S(1)}, f32[2,1,288]{1,2,0:T(8,128)S(1)}, u32[]{:S(2)}, u32[]{:S(2)}) collective-permute-start(f32[2,1,288]{1,2,0:T(8,128)S(1)} %get-tuple-element.30), channel_id=1, source_target_pairs={{0,4},{4,8},{8,12},{12,16},{16,20},{20,24},{24,28},{28,32},{32,36}... | collective-permute-start | bytes 6920 | tf_op jit(solution)/shard_map/ppermute | solution.py:27
  218.6 13.0 %collective-permute-start.9 = (f32[2,1,288]{1,2,0:T(8,128)S(1)}, f32[2,1,288]{1,2,0:T(8,128)S(1)}, u32[]{:S(2)}, u32[]{:S(2)}) collective-permute-start(f32[2,1,288]{1,2,0:T(8,128)S(1)} %get-tuple-element.31), channel_id=1, source_target_pairs={{4,0},{8,4},{12,8},{16,12},{20,16},{24,20},{28,24},{32,28},{36,32}... | collective-permute-start | bytes 6920 | tf_op jit(solution)/shard_map/ppermute | solution.py:28
  231.9 2.2 collective-permute-start.10
  233.1 3.3 collective-permute-start.11
  346.1 11.2 %collective-permute-start.12 = (f32[5,1,896]{2,1,0:T(1,128)S(1)}, f32[5,1,896]{2,1,0:T(1,128)S(1)}, u32[]{:S(2)}, u32[]{:S(2)}) collective-permute-start(f32[5,1,896]{2,1,0:T(1,128)S(1)} %get-tuple-element.21), channel_id=1, source_target_pairs={{0,4},{4,8},{8,12},{12,16},{16,20},{20,24},{24,28},{28,32},{32,36}... | collective-permute-start | bytes 53768 | tf_op jit(solution)/shard_map/ppermute | solution.py:27
  348.0 10.1 %collective-permute-start.13 = (f32[5,1,896]{2,1,0:T(1,128)S(1)}, f32[5,1,896]{2,1,0:T(1,128)S(1)}, u32[]{:S(2)}, u32[]{:S(2)}) collective-permute-start(f32[5,1,896]{2,1,0:T(1,128)S(1)} %get-tuple-element.20), channel_id=1, source_target_pairs={{4,0},{8,4},{12,8},{16,12},{20,16},{24,20},{28,24},{32,28},{36,32}... | collective-permute-start | bytes 53768 | tf_op jit(solution)/shard_map/ppermute | solution.py:28
  358.3 2.0 collective-permute-start.14
  358.6 4.3 %collective-permute-start.15 = (f32[5,34,1]{2,1,0:T(8,128)S(1)}, f32[5,34,1]{2,1,0:T(8,128)S(1)}, u32[]{:S(2)}, u32[]{:S(2)}) collective-permute-start(f32[5,34,1]{2,1,0:T(8,128)S(1)} %get-tuple-element.16), channel_id=1, source_target_pairs={{1,0},{2,1},{3,2},{0,3},{5,4},{6,5},{7,6},{4,7},{9,8},{10,9},{11,1... | collective-permute-start | bytes 2048 | tf_op jit(solution)/shard_map/ppermute | solution.py:28
  364.5 12.7 %copy-start.7 = (f32[768,288]{0,1:T(8,128)S(1)}, f32[768,288]{0,1:T(8,128)}, u32[]{:S(2)}) copy-start(f32[768,288]{0,1:T(8,128)} %copy-done.6) | copy-start | bytes 2654212
  364.6 11.0 %collective-permute-start.16 = (f32[5,1,896]{2,1,0:T(1,128)S(1)}, f32[5,1,896]{2,1,0:T(1,128)S(1)}, u32[]{:S(2)}, u32[]{:S(2)}) collective-permute-start(f32[5,1,896]{2,1,0:T(1,128)S(1)} %get-tuple-element.19), channel_id=1, source_target_pairs={{0,4},{4,8},{8,12},{12,16},{16,20},{20,24},{24,28},{28,32},{32,36}... | collective-permute-start | bytes 53768 | tf_op jit(solution)/shard_map/ppermute | solution.py:27
  366.6 9.8 %collective-permute-start.17 = (f32[5,1,896]{2,1,0:T(1,128)S(1)}, f32[5,1,896]{2,1,0:T(1,128)S(1)}, u32[]{:S(2)}, u32[]{:S(2)}) collective-permute-start(f32[5,1,896]{2,1,0:T(1,128)S(1)} %get-tuple-element.18), channel_id=1, source_target_pairs={{4,0},{8,4},{12,8},{16,12},{20,16},{24,20},{28,24},{32,28},{36,32}... | collective-permute-start | bytes 53768 | tf_op jit(solution)/shard_map/ppermute | solution.py:28
  376.6 2.1 collective-permute-start.18
  377.0 4.1 %collective-permute-start.19 = (f32[5,34,1]{2,1,0:T(8,128)S(1)}, f32[5,34,1]{2,1,0:T(8,128)S(1)}, u32[]{:S(2)}, u32[]{:S(2)}) collective-permute-start(f32[5,34,1]{2,1,0:T(8,128)S(1)} %get-tuple-element.14), channel_id=1, source_target_pairs={{1,0},{2,1},{3,2},{0,3},{5,4},{6,5},{7,6},{4,7},{9,8},{10,9},{11,1... | collective-permute-start | bytes 2048 | tf_op jit(solution)/shard_map/ppermute | solution.py:28
Sparse Core Ops, SparseCore 0:
  41.2 45.2 all-gather.2
  145.3 43.7 all-gather.4
where the time goes:
time: 394 us; the launch traced here: 390 us
  local copies, waits for them, and re-layouts  119 us (30%)
  waiting for transfers between devices  106 us (27%)
  starting transfers between devices  61 us (15%)
  matrix products  52.2 us (13%)
  other arithmetic  37 us (9%)
  between operations  14.9 us (4%)
    gather x2, local copies, waits for them, and re-layouts, per_device(): picked = jnp.take(bottom_rim.reshape(2, -1), flat_index, axis=1)  106 us
    all_gather x2, waiting for transfers between devices, per_device(): lax.all_gather(lines, 'lon', axis=1, tiled=True)  61.9 us
    ppermute x10, starting transfers between devices, padded_2(): after = lax.ppermute(first, axis, down)  43.2 us
    dot_general x2, matrix products, per_device(): jnp.dot(lax.all_gather(lines, 'lon', axis=1, tiled=True), basis, precisio...  41.9 us
    ppermute x10, waiting for transfers between devices, padded_2(): after = lax.ppermute(first, axis, down)  36.3 us
    ppermute x10, starting transfers between devices, padded_2(): before = lax.ppermute(last, axis, up)  17.6 us
    sin x1, other arithmetic, make_basis(): jnp.sin(2.0 * math.pi * sin_phase.astype(jnp.float32) / lon_total)  12.6 us
    cos x1, other arithmetic, make_basis(): jnp.cos(2.0 * math.pi * cos_phase.astype(jnp.float32) / lon_total)  11 us
  transfers between devices with their start and end apart: 22, of which 17 were waited for; matrix products, arithmetic and copies ran while one was open for 7% of the time, Pallas kernels for 0%

commit v1 on v0

v1 whole, which is shorter than its diff:
```python
import math

import jax
import jax.numpy as jnp
import numpy as np
from jax import lax
from jax.experimental import pallas as pl
from jax.experimental.pallas import tpu as pltpu
from jax.sharding import PartitionSpec as P


f32 = jnp.float32
bf16 = jnp.bfloat16
LEV, ROWS, COLS, LONS = 32, 24, 288, 4
NLON = COLS * LONS
LB = LEV // LONS
HALF = NLON // 2
OLEV, OROWS, OCOLS = 4, 32, 896
WROWS, WCOLS = 40, 1024
WIN = 32
FT = 54 * 8

advect_coef = 0.2
diffuse_coef = 0.1
flux_coef = 0.25
ocean_diffuse = 0.15
vertical_mix = 0.2


def call(kernel, out_shape, smem=0, n_in=0, n_any=0, scratch=(), cost=None, mib=24):
    specs = [pl.BlockSpec(memory_space=pltpu.SMEM)] * smem + [pl.BlockSpec(memory_space=pltpu.VMEM)] * n_in
    specs += [pl.BlockSpec(memory_space=pl.ANY)] * n_any
    return pl.pallas_call(
        kernel,
        out_shape=out_shape,
        in_specs=specs,
        scratch_shapes=scratch,
        cost_estimate=cost,
        compiler_params=pltpu.CompilerParams(vmem_limit_bytes=mib << 20),
    )


def cost(us):
    return pl.CostEstimate(flops=0, transcendentals=0, bytes_accessed=int(us * 3.0e6))


def sds(*shape, dtype=f32):
    return jax.ShapeDtypeStruct(shape, dtype)


LEVEL_AT, OCEAN_AT, SEA_AT, LAT_WIRE = 288, 312, 368, 384
WIND_AT, STRIP_AT, RIM_WIRE = 144, 360, 400
TILES = OCOLS // 128


def pack_kernel(place, q_in, u_in, v_in, t_in, mask_in, a0, a1, a2, a3, b0, b1, b2, b3, up, down, mid, q, u, v, t, mask, sems):
    copies = [
        [
            pltpu.make_async_copy(source.at[pl.ds(LB * i, LB)], target.at[pl.ds(LB * i, LB)], sems.at[f, i])
            for i in range(LONS)
        ]
        for f, (source, target) in enumerate(((q_in, q), (u_in, u), (v_in, v)))
    ]
    copies.append([pltpu.make_async_copy(t_in, t, sems.at[3, 0]), pltpu.make_async_copy(mask_in, mask, sems.at[3, 1])])
    for group in copies:
        for copy in group:
            copy.start()
    first_wires, second_wires = (a0, a1, a2, a3), (b0, b1, b2, b3)
    for f, field in enumerate((q, u, v)):
        for copy in copies[f]:
            copy.wait()
        for s in range(LONS):
            wire, base = (first_wires[s], 0) if f == 0 else (second_wires[s], (f - 1) * FT)
            first = (place[0] + s) % LONS * LB
            for l in range(LB):
                for c in range(2):
                    wire[pl.ds(base + c * 192 + l, ROWS, stride=8), :] = field[first + l, :, c * 128 : c * 128 + 128]
                wire[pl.ds(base + 384 + l, 6, stride=8), :] = jnp.concatenate(
                    [field[first + l, 6 * i : 6 * i + 6, 256:288] for i in range(4)], axis=1
                )
    for copy in copies[3]:
        copy.wait()
    for s in range(LONS):
        first = (place[0] + s) % LONS * LB
        for l in range(LB):
            for out, rows in ((up, (22, 23, 23, 23)), (down, (0, 1, 0, 0))):
                rems = []
                for i, (field, r) in enumerate(zip((q, q, u, v), rows)):
                    for c in range(2):
                        out[pl.ds(s * 72 + c * 32 + i * 8 + l, 1), :] = field[
                            first + l, r : r + 1, c * 128 : c * 128 + 128
                        ]
                    rems.append(field[first + l, r : r + 1, 256:288])
                out[pl.ds(s * 72 + 64 + l, 1), :] = jnp.concatenate(rems, axis=1)
    for out, a, b, o in ((up, ROWS - 3, ROWS - 2, OROWS - 2), (down, 0, 0, 0)):
        for at, field, r, n in ((0, q, a, 3), (3, u, b, 2), (5, v, b, 2)):
            for c in range(2):
                out[LEVEL_AT + 8 * c + at : LEVEL_AT + 8 * c + at + n, :] = field[
                    LEV - 1, r : r + n, c * 128 : c * 128 + 128
                ]
            out[LEVEL_AT + 16 + at : LEVEL_AT + 16 + at + n, 0:32] = field[LEV - 1, r : r + n, 256:288]
        for c in range(TILES):
            for l in range(OLEV):
                out[OCEAN_AT + 8 * c + 2 * l : OCEAN_AT + 8 * c + 2 * l + 2, :] = t[
                    l, o : o + 2, c * 128 : c * 128 + 128
                ]
            out[SEA_AT + 2 * c : SEA_AT + 2 * c + 2, :] = mask[o : o + 2, c * 128 : c * 128 + 128].astype(f32)
    for f, field in enumerate((q, u, v)):
        mid[f, :, :] = field[LEV - 1, :, :]


def join_kernel(before, after, mid, t, mask, w0, w1, w2, w3, win):
    wires = (w0, w1, w2, w3)
    for s, wire in enumerate(wires):
        wire[0:72, :] = before[s * 72 : s * 72 + 72, :]
        wire[72:144, :] = after[s * 72 : s * 72 + 72, :]
    for f, (at, n) in enumerate(((0, 3), (3, 2), (5, 2))):
        win[...] = jnp.zeros((WIN, 384), f32)
        win[4 : 4 + ROWS, 0:COLS] = mid[f, :, :]
        for c in range(3):
            rows = LEVEL_AT + 8 * c + at
            width = 128 if c < 2 else 32
            win[4 - n : 4, c * 128 : c * 128 + width] = before[rows : rows + n, 0:width]
            win[4 + ROWS : 4 + ROWS + n, c * 128 : c * 128 + width] = after[rows : rows + n, 0:width]
        rem = jnp.concatenate([win[8 * i : 8 * i + 8, 256:288] for i in range(4)], axis=1)
        for wire in wires:
            base = WIND_AT + f * 72
            wire[base : base + 32, :] = win[:, 0:128]
            wire[base + 32 : base + 64, :] = win[:, 128:256]
            wire[base + 64 : base + 72, :] = rem
    pad = 128 - 2 * (OLEV + 1)
    for wire, col in ((w3, 0), (w1, OCOLS - 2)):
        tile, lane = col // 128, col % 128
        own = [t[l, :, col : col + 2] for l in range(OLEV)] + [mask[:, col : col + 2].astype(f32)]
        wire[STRIP_AT : STRIP_AT + OROWS, :] = jnp.concatenate(own + [jnp.zeros((OROWS, pad), f32)], axis=1)
        wire[STRIP_AT + OROWS : STRIP_AT + WROWS, :] = jnp.zeros((WROWS - OROWS, 128), f32)
        for near, row in ((after, OROWS), (before, WROWS - 2)):
            base = OCEAN_AT + 8 * tile
            far = [near[base + 2 * l : base + 2 * l + 2, lane : lane + 2] for l in range(OLEV)]
            far.append(near[SEA_AT + 2 * tile : SEA_AT + 2 * tile + 2, lane : lane + 2])
            wire[STRIP_AT + row : STRIP_AT + row + 2, :] = jnp.concatenate(far + [jnp.zeros((2, pad), f32)], axis=1)


def unpack_kernel(place, w0, w1, w2, w3, out):
    for s, wire in enumerate((w0, w1, w2, w3)):
        first = (place[0] + LONS - s) % LONS * LB
        for l in range(LB):
            for c in range(2):
                out[first + l, :, c * 128 : c * 128 + 128] = wire[pl.ds(c * 192 + l, ROWS, stride=8), :]
            rem = wire[pl.ds(384 + l, 6, stride=8), :]
            for i in range(4):
                out[first + l, 6 * i : 6 * i + 6, 256:288] = rem[:, 32 * i : 32 * i + 32]


def wave_tables():
    slots = np.arange(NLON)[None, :]
    wave = np.where(slots <= HALF, slots, slots - HALF)
    coarse = (32 * np.arange(36)[:, None] * wave) % NLON * (2 * np.pi / NLON)
    fine = (np.arange(32)[:, None] * wave) % NLON * (2 * np.pi / NLON)
    with_cos = np.where(slots <= HALF, np.cos(coarse), np.sin(coarse))
    with_sin = np.where(slots <= HALF, -np.sin(coarse), np.cos(coarse))
    return tuple(a.astype(np.float32) for a in (with_cos, with_sin, np.cos(fine), np.sin(fine)))


def basis_kernel(with_cos, with_sin, cosine, sine, hi, lo):
    def body(a, carry):
        row = pl.multiple_of(a * 32, 32)
        for h in (0, 16):
            value = with_cos[pl.ds(a, 1), :] * cosine[h : h + 16, :] + with_sin[pl.ds(a, 1), :] * sine[h : h + 16, :]
            top = value.astype(bf16)
            hi[pl.ds(row + h, 16), :] = top
            lo[pl.ds(row + h, 16), :] = (value - top.astype(f32)).astype(bf16)
        return carry

    lax.fori_loop(0, 36, body, 0)


def split(x):
    top = x.astype(bf16)
    return top, (x - top.astype(f32)).astype(bf16)


def product(x, hi, lo, back=False):
    top, rest = split(x)
    lines = x.shape[0]
    dims = (((1,), (1 if back else 0,)), ((), ()))

    def dot(a, b):
        return lax.dot_general(a, b[...], dims, preferred_element_type=f32)

    both = dot(jnp.concatenate([top, rest], axis=0), hi)
    return both[:lines] + both[lines:] + dot(top, lo)


def advance(q, north, south, u, v):
    east = pltpu.roll(q, NLON - 1, 1)
    west = pltpu.roll(q, 1, 1)
    advect = u * (east - west) + v * (north - south)
    spread = east + west + north + south - 4.0 * q
    return q - advect_coef * advect + diffuse_coef * spread


def bottom_kernel(w0, w1, w2, w3, damp, bh, bl, heat, speed):
    def circle(f):
        base, parts = WIND_AT + f * 72, []
        for w in (w0, w1, w2, w3):
            parts += [w[base : base + 32, :], w[base + 32 : base + 64, :]]
            parts.append(
                jnp.concatenate([w[base + 64 : base + 72, 32 * i : 32 * i + 32] for i in range(4)], axis=0)
            )
        return jnp.concatenate(parts, axis=1)

    q, u, v = circle(0), circle(1), circle(2)
    wind = jnp.abs(u) + jnp.abs(v) + 0.5
    for _ in range(2):
        q = advance(q, pltpu.roll(q, WIN - 1, 0), pltpu.roll(q, 1, 0), u, v)
        q = product(product(q, bh, bl) * damp[...], bh, bl, back=True)
    for out, field in ((heat, q), (speed, wind)):
        lane = lax.broadcasted_iota(jnp.int32, (WIN, 128), 1)
        out[:, 0:256] = field[:, 0:256]
        out[:, 256:384] = jnp.where(lane < 64, field[:, 256:384], field[:, NLON - 128 : NLON])


def bulk_kernel(m0, m1, m2, m3, n0, n1, n2, n3, h0, h1, h2, h3, damp, bh, bl, after, o0, o1, o2, o3, qs, us, vs, xs):
    halos = (h0, h1, h2, h3)

    def main_slab(f, r):
        parts = []
        for w in (m0, m1, m2, m3) if f == 0 else (n0, n1, n2, n3):
            base = max(f - 1, 0) * FT
            parts.append(w[base + r * 8 : base + r * 8 + 8, :])
            parts.append(w[base + 192 + r * 8 : base + 200 + r * 8, :])
            g, i = r % 6, r // 6
            parts.append(w[base + 384 + g * 8 : base + 392 + g * 8, 32 * i : 32 * i + 32])
        return jnp.concatenate(parts, axis=1)

    def halo_slab(side, i):
        parts = []
        for h in halos:
            base = side * 72
            parts.append(h[base + i * 8 : base + i * 8 + 8, :])
            parts.append(h[base + 32 + i * 8 : base + 40 + i * 8, :])
            parts.append(h[base + 64 : base + 72, 32 * i : 32 * i + 32])
        return jnp.concatenate(parts, axis=1)

    def put(ref, slot, value):
        ref[slot * 8 : slot * 8 + 8, :] = value

    for r in range(ROWS):
        put(qs, r + 2, main_slab(0, r))
        put(us, r + 1, main_slab(1, r))
        put(vs, r + 1, main_slab(2, r))
    put(qs, 0, halo_slab(0, 0))
    put(qs, 1, halo_slab(0, 1))
    put(us, 0, halo_slab(0, 2))
    put(vs, 0, halo_slab(0, 3))
    put(qs, 26, halo_slab(1, 0))
    put(qs, 27, halo_slab(1, 1))
    put(us, 25, halo_slab(1, 2))
    put(vs, 25, halo_slab(1, 3))

    def at(ref, slot):
        return ref[pl.ds(pl.multiple_of(slot * 8, 8), 8), :]

    def scale(count, first):
        def body(r, carry):
            xs[pl.ds(pl.multiple_of(r * 8, 8), 8), :] = at(xs, r) * damp[pl.ds(r + first, 1), :]
            return carry

        lax.fori_loop(0, count, body, 0)

    def first(r, carry):
        xs[pl.ds(pl.multiple_of(r * 8, 8), 8), :] = advance(
            at(qs, r + 1), at(qs, r + 2), at(qs, r), at(us, r), at(vs, r)
        )
        return carry

    lax.fori_loop(0, ROWS + 2, first, 0)
    xs[...] = product(xs[...], bh, bl)
    scale(ROWS + 2, 3)
    qs[0:208, :] = product(xs[...], bh, bl, back=True)

    def second(r, carry):
        xs[pl.ds(pl.multiple_of(r * 8, 8), 8), :] = advance(
            at(qs, r + 1), at(qs, r + 2), at(qs, r), at(us, r + 1), at(vs, r + 1)
        )
        return carry

    lax.fori_loop(0, ROWS, second, 0)
    xs[0:192, :] = product(xs[0:192, :], bh, bl)
    scale(ROWS, 4)
    xs[0:192, :] = product(xs[0:192, :], bh, bl, back=True)
    for p, out in enumerate((o0, o1, o2, o3)):
        for g in range(6):
            rems = []
            for r in range(g, ROWS, 6):
                piece = xs[r * 8 : r * 8 + 8, p * COLS : p * COLS + COLS]
                out[r * 8 : r * 8 + 8, :] = piece[:, 0:128]
                out[192 + r * 8 : 200 + r * 8, :] = piece[:, 128:256]
                rems.append(piece[:, 256:288])
            out[384 + g * 8 : 392 + g * 8, :] = jnp.concatenate(rems, axis=1)


def pick_kernel(place, rows, cols, heat, speed, air_heat, air_speed, up, down):
    def body(k, carry):
        start = pl.multiple_of(k * 8, 8)
        for c in range(TILES):
            row = rows[pl.ds(start, 8), c * 128 : c * 128 + 128] - place[1] * ROWS + 4
            col = cols[pl.ds(start, 8), c * 128 : c * 128 + 128] - place[0] * COLS
            col = jnp.where(col < 0, col + NLON, col)
            col = jnp.where(col > COLS, col - (NLON - 384), col)
            key = row * 4 + (col >> 7)
            lane = col & 127
            got_heat = jnp.zeros((8, 128), f32)
            got_speed = jnp.zeros((8, 128), f32)
            for w in range(3, 29):
                for b in range(3):
                    mine = key == w * 4 + b
                    line_heat = jnp.broadcast_to(heat[w : w + 1, b * 128 : b * 128 + 128], (8, 128))
                    line_speed = jnp.broadcast_to(speed[w : w + 1, b * 128 : b * 128 + 128], (8, 128))
                    got_heat = jnp.where(mine, jnp.take_along_axis(line_heat, lane, axis=1), got_heat)
                    got_speed = jnp.where(mine, jnp.take_along_axis(line_speed, lane, axis=1), got_speed)
            air_heat[pl.ds(start, 8), c * 128 : c * 128 + 128] = got_heat
            air_speed[pl.ds(start, 8), c * 128 : c * 128 + 128] = got_speed
        return carry

    lax.fori_loop(0, OROWS // 8, body, 0)
    for f, field in enumerate((air_heat, air_speed)):
        up[2 * f : 2 * f + 2, :] = field[OROWS - 2 : OROWS, :]
        down[2 * f : 2 * f + 2, :] = field[0:2, :]


def ring_kernel(heat, speed, before, after, behind, east, west):
    for out, col in ((east, 0), (west, OCOLS - 2)):
        out[0:OROWS, :] = jnp.concatenate([heat[:, col : col + 2], speed[:, col : col + 2]], axis=1)
        out[OROWS:WROWS, :] = jnp.zeros((WROWS - OROWS, 4), f32)
        for near, row in ((after, OROWS), (before, WROWS - 2)):
            out[row : row + 2, :] = jnp.concatenate([near[0:2, col : col + 2], near[2:4, col : col + 2]], axis=1)


def ocean_kernel(t, mask, heat, speed, before, after, east, west, air_before, air_after, air_east, air_west, out, win):
    gap = jnp.zeros((WROWS, 124), f32)
    strip = slice(STRIP_AT, STRIP_AT + WROWS)

    def window(field, slot, above, below, right, left):
        win[slot, OROWS:WROWS, :] = jnp.zeros((WROWS - OROWS, WCOLS), f32)
        win[slot, 0:OROWS, 0:OCOLS] = field
        for c in range(TILES):
            win[slot, OROWS : OROWS + 2, c * 128 : c * 128 + 128] = below(c)
            win[slot, WROWS - 2 : WROWS, c * 128 : c * 128 + 128] = above(c)
        win[slot, :, OCOLS:WCOLS] = jnp.concatenate([right, gap, left], axis=1)
        return win[slot]

    def sea_rows(wire):
        return lambda c: wire[SEA_AT + 2 * c : SEA_AT + 2 * c + 2, :]

    def level_rows(wire, l):
        return lambda c: wire[OCEAN_AT + 8 * c + 2 * l : OCEAN_AT + 8 * c + 2 * l + 2, :]

    def air_rows(wire, f):
        return lambda c: wire[2 * f : 2 * f + 2, c * 128 : c * 128 + 128]

    temps = [
        window(
            t[l], l, level_rows(before, l), level_rows(after, l),
            east[strip, 2 * l : 2 * l + 2], west[strip, 2 * l : 2 * l + 2],
        )
        for l in range(OLEV)
    ]
    sea = window(mask[...].astype(f32), 4, sea_rows(before), sea_rows(after), east[strip, 8:10], west[strip, 8:10])
    air = [
        window(
            field[...], 5 + f, air_rows(air_before, f), air_rows(air_after, f),
            air_east[:, 2 * f : 2 * f + 2], air_west[:, 2 * f : 2 * f + 2],
        )
        for f, field in enumerate((heat, speed))
    ]

    def beside(field):
        return (
            pltpu.roll(field, WCOLS - 1, 1),
            pltpu.roll(field, 1, 1),
            pltpu.roll(field, WROWS - 1, 0),
            pltpu.roll(field, 1, 0),
        )

    seas = beside(sea)
    rate = sea * flux_coef * air[1]
    for _ in range(2):
        temps[0] = temps[0] + rate * (air[0] - temps[0])
        moved = []
        for field in temps:
            total = jnp.zeros_like(field)
            for near_sea, near in zip(seas, beside(field)):
                total = total + near_sea * (near - field)
            moved.append(field + ocean_diffuse * (sea * total))
        temps = [
            moved[l]
            + vertical_mix * sea * (moved[max(l - 1, 0)] + moved[min(l + 1, OLEV - 1)] - 2.0 * moved[l])
            for l in range(OLEV)
        ]
    for l in range(OLEV):
        out[l, :, :] = temps[l][0:OROWS, 0:OCOLS]


def damp_window(lat_place, polar_rows, lat_total, band_rows):
    slots = np.arange(NLON)
    waves = np.where(slots < HALF, slots, np.where(slots == HALF, HALF, slots - HALF))
    weight = np.where((slots == 0) | (slots == HALF), 1.0, 2.0) / NLON
    sine = np.where(waves > 0, np.sin(np.pi * waves / NLON), 1.0)
    row_index = lat_place * ROWS - 4 + jnp.arange(WIN, dtype=jnp.int32)
    latitude_cos = jnp.sin(math.pi * (row_index.astype(f32) + 0.5) / lat_total)
    ratio = latitude_cos / math.sin(math.pi * band_rows / lat_total)
    damping = jnp.minimum(1.0, ratio[:, None] / sine.astype(np.float32)[None, :])
    damping = jnp.where(waves[None, :] > 0, damping, 1.0)
    listed = jnp.any(row_index[:, None] == polar_rows[None, :], axis=1)
    inside = (row_index >= 0) & (row_index < lat_total)
    table = jnp.where(listed[:, None], damping, 1.0) * weight.astype(np.float32)[None, :]
    return jnp.where(inside[:, None], table, 0.0)


def per_device(tracer, wind_u, wind_v, ocean_temp, land_mask, remap_rows, remap_cols, polar_rows):
    lat_devices = lax.axis_size("lat")
    lat_place, lon_place = lax.axis_index("lat"), lax.axis_index("lon")
    place = jnp.stack([lon_place, lat_place]).astype(jnp.int32)
    north = [(i, i + 1) for i in range(lat_devices - 1)]
    south = [(j, i) for i, j in north]

    def along(x, s):
        return lax.ppermute(x, "lon", [(i, (i + s) % LONS) for i in range(LONS)])

    def across(to_north, to_south):
        before = lax.ppermute(to_north, "lat", north)
        return before, lax.ppermute(to_south, "lat", south)

    packed = call(
        pack_kernel,
        [sds(FT, 128)] * 4 + [sds(2 * FT, 128)] * 4 + [sds(LAT_WIRE, 128)] * 2 + [sds(3, ROWS, COLS)],
        smem=1,
        n_any=5,
        scratch=[pltpu.VMEM((LEV, ROWS, COLS), f32)] * 3
        + [
            pltpu.VMEM((OLEV, OROWS, OCOLS), f32),
            pltpu.VMEM((OROWS, OCOLS), jnp.int32),
            pltpu.SemaphoreType.DMA((4, LONS)),
        ],
        cost=cost(5),
        mib=60,
    )(place, tracer, wind_u, wind_v, ocean_temp, land_mask)
    mains, winds, mid = packed[:4], packed[4:8], packed[10]
    pieces = [mains[0]] + [along(mains[s], s) for s in (3, 2, 1)]
    before, after = across(packed[8], packed[9])

    basis = call(basis_kernel, [sds(NLON, NLON, dtype=bf16)] * 2, n_in=4, cost=cost(3))(*wave_tables())
    damp = damp_window(lat_place, polar_rows, ROWS * lat_devices, lat_devices // 8 * ROWS)
    joined = call(
        join_kernel,
        [sds(RIM_WIRE if s in (1, 3) else STRIP_AT, 128) for s in range(LONS)],
        n_in=5,
        scratch=[pltpu.VMEM((WIN, 384), f32)],
        cost=cost(2),
    )(before, after, mid, ocean_temp, land_mask)
    rims = [joined[0]] + [along(joined[s], s) for s in (3, 2, 1)]
    blows = [winds[0]] + [along(winds[s], s) for s in (3, 2, 1)]

    heat, speed = call(bottom_kernel, [sds(WIN, 384)] * 2, n_in=7, cost=cost(8))(*rims, damp, *basis)
    air_heat, air_speed, air_up, air_down = call(
        pick_kernel, [sds(OROWS, OCOLS)] * 2 + [sds(4, OCOLS)] * 2, smem=1, n_in=4, cost=cost(7)
    )(place, remap_rows, remap_cols, heat, speed)
    air_before, air_after = across(air_up, air_down)

    lines = (ROWS + 4) * LB
    outs = call(
        bulk_kernel,
        [sds(FT, 128)] * 4,
        n_in=15,
        n_any=1,
        scratch=[pltpu.VMEM((lines, NLON), f32)] + [pltpu.VMEM((lines - 16, NLON), f32)] * 3,
        cost=cost(18),
        mib=36,
    )(*pieces, *blows, *rims, damp, *basis, air_up)
    back = [outs[0]] + [along(outs[s], s) for s in (1, 2, 3)]

    east, west = call(ring_kernel, [sds(WROWS, 4)] * 2, n_in=4, n_any=1, cost=cost(1))(
        air_heat, air_speed, air_before, air_after, outs[0]
    )
    air_east, air_west = along(east, LONS - 1), along(west, 1)
    ocean_out = call(
        ocean_kernel, sds(OLEV, OROWS, OCOLS), n_in=12, scratch=[pltpu.VMEM((7, WROWS, WCOLS), f32)], cost=cost(3)
    )(
        ocean_temp, land_mask, air_heat, air_speed, before, after, rims[1], rims[3],
        air_before, air_after, air_east, air_west,
    )
    tracer_out = call(unpack_kernel, sds(LEV, ROWS, COLS), smem=1, n_in=4, cost=cost(2))(place, *back)
    return tracer_out, ocean_out


def solution(mesh):
    band = P(None, "lat", "lon")
    cells = P("lat", "lon")
    return jax.shard_map(
        per_device,
        mesh=mesh,
        in_specs=(band, band, band, band, cells, cells, cells, P()),
        out_specs=(band, band),
        check_vma=False,
    )
```

time: 394 us -> 102 us (0.26)
  local copies, waits for them, and re-layouts: 119 us -> 1.01 us
  waiting for transfers between devices: 106 us -> 23.5 us
  matrix products: 52.2 us -> 0 us
  Pallas kernels: 0 us -> 36.4 us
  other arithmetic: 37 us -> 0.91 us
  starting transfers between devices: 61 us -> 38.7 us
  between operations: 14.9 us -> 0.95 us
    gather x2 -> x0, local copies, waits for them, and re-layouts: 106 us -> none  [per_device(): picked = jnp.take(bottom_rim.reshape(2, -1), flat_index, axis=1)]
    all_gather x2 -> x0, waiting for transfers between devices: 61.9 us -> none  [per_device(): lax.all_gather(lines, 'lon', axis=1, tiled=True)]
    dot_general x4 -> x0, matrix products: 52.2 us -> none  [the longest x2 41.9 us: per_device(): jnp.dot(lax.all_gather(lines, 'lon', axis=1, tiled=True), basis, precisio...]
    pallas_call x0 -> x9, Pallas kernels: none -> 36.4 us  [the longest x1 15.6 us: per_device(): call(bulk_kernel, [sds(FT, 128)] * 4, n_in=15, n_any=1, scratch=[pltpu.VM...]
    ppermute x20 -> x18, starting transfers between devices: 60.8 us -> 38.7 us  [the longest x14 16.7 us: along(): return lax.ppermute(x, 'lon', [(i, (i + s) % LONS) for i in range(LONS)])]
    ppermute x20 -> x18, waiting for transfers between devices: 44.3 us -> 23.5 us  [the longest x14 14.1 us: along(): return lax.ppermute(x, 'lon', [(i, (i + s) % LONS) for i in range(LONS)])]
    sin x1 -> x0, other arithmetic: 12.6 us -> none  [make_basis(): jnp.sin(2.0 * math.pi * sin_phase.astype(jnp.float32) / lon_total)]
    cos x1 -> x0, other arithmetic: 11 us -> none  [make_basis(): jnp.cos(2.0 * math.pi * cos_phase.astype(jnp.float32) / lon_total)]
  transfers between devices with their start and end apart: 22 -> 18, of which waited for: 17 -> 7; matrix products, arithmetic and copies ran while one was open for 7% -> 0% of each run, Pallas kernels for 0% -> 14%
where the time goes in v1:
time: 102 us; the launch traced here: 101 us
  starting transfers between devices  38.7 us (38%)
  Pallas kernels  36.4 us (36%)
  waiting for transfers between devices  23.5 us (23%)
    ppermute x14, starting transfers between devices, along(): return lax.ppermute(x, 'lon', [(i, (i + s) % LONS) for i in range(LONS)])  16.7 us
    ppermute x2, starting transfers between devices, across(): return (before, lax.ppermute(to_south, 'lat', south))  16.4 us
    pallas_call x1, Pallas kernels, per_device(): call(bulk_kernel, [sds(FT, 128)] * 4, n_in=15, n_any=1, scratch=[pltpu.VM...  15.6 us
    ppermute x14, waiting for transfers between devices, along(): return lax.ppermute(x, 'lon', [(i, (i + s) % LONS) for i in range(LONS)])  14.1 us
    ppermute x2, waiting for transfers between devices, across(): before = lax.ppermute(to_north, 'lat', north)  8.42 us
    pallas_call x1, Pallas kernels, per_device(): call(pick_kernel, [sds(OROWS, OCOLS)] * 2 + [sds(4, OCOLS)] * 2, smem=1,...  5.64 us
    ppermute x2, starting transfers between devices, across(): before = lax.ppermute(to_north, 'lat', north)  5.6 us
    pallas_call x1, Pallas kernels, per_device(): call(pack_kernel, [sds(FT, 128)] * 4 + [sds(2 * FT, 128)] * 4 + [sds(LAT_...  5.07 us
  transfers between devices with their start and end apart: 18, of which 7 were waited for; matrix products, arithmetic and copies ran while one was open for 0% of the time, Pallas kernels for 14%

profile of v1, /device:TPU:3, one launch (start us, length us, event | category | flops | bytes accessed | tf_op | source)
XLA Modules:
  0.0 101.5 jit_solution(16078293862848907143)
XLA Ops:
  0.6 0.6 pad_add_fusion.place
  1.2 0.0 copy-start.13
  1.2 0.0 copy-start.14
  1.2 5.1 %shard_map.158 = (f32[432,128]{1,0:T(8,128)}, f32[432,128]{1,0:T(8,128)}, f32[432,128]{1,0:T(8,128)}, f32[432,128]{1,0:T(8,128)}, f32[864,128]{1,0:T(8,128)}, /*...) custom-call(s32[2]{0:T(128)} %pad_add_fusion.place, ...), custom_call_target="tpu_custom_call" | custom-call | bytes 15000000 | tf_op jit(solution)/shard_map/pallas_call | solution.py:436
  6.3 0.0 copy-start.4
  6.3 0.0 copy-start.5
  6.4 0.0 copy-start.6
  6.4 0.0 copy-start.7
  6.4 3.7 %collective-permute-start.6 = (f32[384,128]{1,0:T(8,128)}, f32[384,128]{1,0:T(8,128)S(1)}, u32[]{:S(2)}, u32[]{:S(2)}) collective-permute-start(f32[384,128]{1,0:T(8,128)} %get-tuple-element.39), channel_id=1, source_target_pairs={{0,4},{4,8},{8,12},{12,16},{16,20},{20,24},{24,28},{28,32},{32,36}... | collective-permute-start | bytes 589832 | tf_op jit(solution)/shard_map/ppermute | solution.py:433
  10.1 8.5 %collective-permute-start.7 = (f32[384,128]{1,0:T(8,128)}, f32[384,128]{1,0:T(8,128)S(1)}, u32[]{:S(2)}, u32[]{:S(2)}) collective-permute-start(f32[384,128]{1,0:T(8,128)} %get-tuple-element.40), channel_id=1, source_target_pairs={{4,0},{8,4},{12,8},{16,12},{20,16},{24,20},{28,24},{32,28},{36,32}... | collective-permute-start | bytes 589832 | tf_op jit(solution)/shard_map/ppermute | solution.py:434
  18.5 1.0 %collective-permute-start = (f32[432,128]{1,0:T(8,128)}, f32[432,128]{1,0:T(8,128)S(1)}, u32[]{:S(2)}, u32[]{:S(2)}) collective-permute-start(f32[432,128]{1,0:T(8,128)} %get-tuple-element.32), channel_id=1, source_target_pairs={{0,3},{1,0},{2,1},{3,2},{4,7},{5,4},{6,5},{7,6},{8,11},{9,8},{10,9... | collective-permute-start | bytes 663560 | tf_op jit(solution)/shard_map/ppermute | solution.py:430
  19.6 0.4 collective-permute-start.1
  20.0 1.4 %collective-permute-done.6.before = f32[384,128]{1,0:T(8,128)S(1)} collective-permute-done((f32[384,128]{1,0:T(8,128)}, f32[384,128]{1,0:T(8,128)S(1)}, u32[]{:S(2)}, u32[]{:S(2)}) %collective-permute-start.6) | collective-permute-done | bytes 196640 | tf_op jit(solution)/shard_map/ppermute | solution.py:433
  21.4 1.0 collective-permute-done.7.after
  22.4 0.9 copy-done.10
  23.3 0.2 shard_map.159
  23.5 0.5 collective-permute-start.9
  24.0 1.8 %collective-permute-start.8 = (f32[400,128]{1,0:T(8,128)S(1)}, f32[400,128]{1,0:T(8,128)S(1)}, u32[]{:S(2)}, u32[]{:S(2)}) collective-permute-start(f32[400,128]{1,0:T(8,128)S(1)} %get-tuple-element.43), channel_id=1, source_target_pairs={{0,3},{1,0},{2,1},{3,2},{4,7},{5,4},{6,5},{7,6},{8,11},{9,8},{10,9... | collective-permute-start | bytes 614408 | tf_op jit(solution)/shard_map/ppermute | solution.py:430
  25.8 1.0 collective-permute-start.10
  26.8 0.2 compare_reduce_fusion
  26.9 0.0 collective-permute-done.m1
  26.9 0.6 collective-permute-start.2
  27.5 3.6 %collective-permute-done.9.w2.h2 = f32[360,128]{1,0:T(8,128)S(1)} collective-permute-done((f32[360,128]{1,0:T(8,128)S(1)}, f32[360,128]{1,0:T(8,128)S(1)}, u32[]{:S(2)}, u32[]{:S(2)}) %collective-permute-start.9) | collective-permute-done | bytes 184352 | tf_op jit(solution)/shard_map/ppermute | solution.py:430
  31.2 4.4 %collective-permute-start.3 = (f32[864,128]{1,0:T(8,128)}, f32[864,128]{1,0:T(8,128)S(1)}, u32[]{:S(2)}, u32[]{:S(2)}) collective-permute-start(f32[864,128]{1,0:T(8,128)} %get-tuple-element.36), channel_id=1, source_target_pairs={{0,3},{1,0},{2,1},{3,2},{4,7},{5,4},{6,5},{7,6},{8,11},{9,8},{10,9... | collective-permute-start | bytes 1327112 | tf_op jit(solution)/shard_map/ppermute | solution.py:430
  35.5 4.0 %collective-permute-done.8.w1.h1.east = f32[400,128]{1,0:T(8,128)S(1)} collective-permute-done((f32[400,128]{1,0:T(8,128)S(1)}, f32[400,128]{1,0:T(8,128)S(1)}, u32[]{:S(2)}, u32[]{:S(2)}) %collective-permute-start.8) | collective-permute-done | bytes 204832 | tf_op jit(solution)/shard_map/ppermute | solution.py:430
  39.5 0.7 collective-permute-start.4
  40.3 0.0 collective-permute-start.5
  40.3 0.1 fusion.3.damp
  40.5 1.5 %shard_map.160 = (bf16[1152,1152]{1,0:T(8,128)(2,1)S(1)}, bf16[1152,1152]{1,0:T(8,128)(2,1)S(1)}) custom-call(f32[36,1152]{1,0:T(8,128)S(1)} %copy-done.5, f32[36,1152]{1,0:T(8,128)S(1)} %copy-done.4, f32[32,1152]{1,0:T(8,128)S(1)} %copy-done.7, f32[32,1152]{1,0:T(8,128)S(1)} %copy-done.6), custom_call_target="tpu_custom_call" | custom-call | bytes 9000000 | tf_op jit(solution)/shard_map/pallas_call | solution.py:454
  41.9 0.0 copy-start.8
  42.0 0.0 copy-start.9
  42.0 0.0 copy-start.2
  42.0 4.5 %shard_map.161 = (f32[32,384]{1,0:T(8,128)S(1)}, f32[32,384]{1,0:T(8,128)S(1)}) custom-call(f32[360,128]{1,0:T(8,128)S(1)} %get-tuple-element.42.w0.h0, f32[400,128]{1,0:T(8,128)S(1)} %collective-permute-done.8.w1.h1.east, f32[360,128]{1,0:T(8,128)S(1)} %collective-permute-done.9.w2.h2, f32[400,128]{1,0:T(8,128)S(1)} %collective-permute-done.10.w3.h3.west, ...), custom_call_target="tpu_custom_call" | custom-call | bytes 24000000 | tf_op jit(solution)/shard_map/pallas_call | solution.py:466
  46.5 0.0 copy-done.8
  46.6 5.6 %shard_map.162 = (f32[32,896]{1,0:T(8,128)S(1)}, f32[32,896]{1,0:T(8,128)S(1)}, f32[4,896]{1,0:T(4,128)S(1)}, f32[4,896]{1,0:T(4,128)S(1)}) custom-call(s32[2]{0:T(128)S(1)} %copy-done.11, s32[32,896]{1,0:T(8,128)S(1)} %copy-done.8, s32[32,896]{1,0:T(8,128)S(1)} %copy-done.9, f32[32,384]{1,0:T(8,128)S(1)} %get-tuple-element.48.heat, ...), custom_call_target="tpu_custom_call" | custom-call | bytes 21000000 | tf_op jit(solution)/shard_map/pallas_call | solution.py:467
  52.3 5.1 %collective-permute-done.5.n3 = f32[864,128]{1,0:T(8,128)S(1)} collective-permute-done((f32[864,128]{1,0:T(8,128)}, f32[864,128]{1,0:T(8,128)S(1)}, u32[]{:S(2)}, u32[]{:S(2)}) %collective-permute-start.5) | collective-permute-done | bytes 442400 | tf_op jit(solution)/shard_map/ppermute | solution.py:430
  57.4 15.6 %shard_map.163 = (f32[432,128]{1,0:T(8,128)S(1)}, f32[432,128]{1,0:T(8,128)S(1)}, f32[432,128]{1,0:T(8,128)S(1)}, f32[432,128]{1,0:T(8,128)S(1)}) custom-call(f32[432,128]{1,0:T(8,128)S(1)} %copy-done.3, f32[432,128]{1,0:T(8,128)S(1)} %collective-permute-done.m1, f32[432,128]{1,0:T(8,128)S(1)} %collective-permute-done.1.m2, ...), custom_call_target="tpu_custom_call" | custom-call | bytes 54000000 | tf_op jit(solution)/shard_map/pallas_call | solution.py:473
  72.9 2.7 %collective-permute-start.11 = (f32[432,128]{1,0:T(8,128)S(1)}, f32[432,128]{1,0:T(8,128)S(1)}, u32[]{:S(2)}, u32[]{:S(2)}) collective-permute-start(f32[432,128]{1,0:T(8,128)S(1)} %get-tuple-element.52), channel_id=1, source_target_pairs={{0,1},{1,2},{2,3},{3,0},{4,5},{5,6},{6,7},{7,4},{8,9},{9,10},{10,1... | collective-permute-start | bytes 663560 | tf_op jit(solution)/shard_map/ppermute | solution.py:430
  75.6 0.9 collective-permute-start.12
  76.5 7.9 %collective-permute-start.15 = (f32[4,896]{1,0:T(4,128)S(1)}, f32[4,896]{1,0:T(4,128)S(1)}, u32[]{:S(2)}, u32[]{:S(2)}) collective-permute-start(f32[4,896]{1,0:T(4,128)S(1)} %get-tuple-element.57), channel_id=1, source_target_pairs={{4,0},{8,4},{12,8},{16,12},{20,16},{24,20},{28,24},{32,28},{36,32}... | collective-permute-start | bytes 43016 | tf_op jit(solution)/shard_map/ppermute | solution.py:434
  84.5 1.9 %collective-permute-start.14 = (f32[4,896]{1,0:T(4,128)S(1)}, f32[4,896]{1,0:T(4,128)S(1)}, u32[]{:S(2)}, u32[]{:S(2)}) collective-permute-start(f32[4,896]{1,0:T(4,128)S(1)} %get-tuple-element.50.after), channel_id=1, source_target_pairs={{0,4},{4,8},{8,12},{12,16},{16,20},{20,24},{24,28},{28,32},{32,36}... | collective-permute-start | bytes 43016 | tf_op jit(solution)/shard_map/ppermute | solution.py:433
  86.4 7.0 %collective-permute-done.14.before.air_before = f32[4,896]{1,0:T(4,128)S(1)} collective-permute-done((f32[4,896]{1,0:T(4,128)S(1)}, f32[4,896]{1,0:T(4,128)S(1)}, u32[]{:S(2)}, u32[]{:S(2)}) %collective-permute-start.14) | collective-permute-done | bytes 14368 | tf_op jit(solution)/shard_map/ppermute | solution.py:433
  93.4 0.1 shard_map.165
  93.5 1.9 %collective-permute-start.16 = (f32[40,4]{1,0:T(8,128)S(1)}, f32[40,4]{1,0:T(8,128)S(1)}, u32[]{:S(2)}, u32[]{:S(2)}) collective-permute-start(f32[40,4]{1,0:T(8,128)S(1)} %get-tuple-element.58), channel_id=1, source_target_pairs={{0,3},{1,0},{2,1},{3,2},{4,7},{5,4},{6,5},{7,6},{8,11},{9,8},{10,9... | collective-permute-start | bytes 1928 | tf_op jit(solution)/shard_map/ppermute | solution.py:430
  95.4 0.8 collective-permute-start.17
  96.3 1.4 %collective-permute-done.16.air_east = f32[40,4]{1,0:T(8,128)S(1)} collective-permute-done((f32[40,4]{1,0:T(8,128)S(1)}, f32[40,4]{1,0:T(8,128)S(1)}, u32[]{:S(2)}, u32[]{:S(2)}) %collective-permute-start.16) | collective-permute-done | bytes 672 | tf_op jit(solution)/shard_map/ppermute | solution.py:430
  97.6 2.0 %shard_map.166 = f32[4,32,896]{2,1,0:T(8,128)} custom-call(f32[4,32,896]{2,1,0:T(8,128)S(1)} %copy-done, s32[32,896]{1,0:T(8,128)S(1)} %copy-done.1, f32[32,896]{1,0:T(8,128)S(1)} %get-tuple-element.55.heat, f32[32,896]{1,0:T(8,128)S(1)} %get-tuple-element.56.speed, f32[384,128]{1,0:T(8,128)S(1)} %collective-permute-done.6.before, ...), custom_call_target="tpu_custom_call" | custom-call | bytes 9000000 | tf_op jit(solution)/shard_map/pallas_call | solution.py:488
  99.7 1.8 %shard_map.164 = f32[32,24,288]{2,1,0:T(8,128)} custom-call(s32[2]{0:T(128)S(1)} %copy-done.11, f32[432,128]{1,0:T(8,128)S(1)} %get-tuple-element.51.w0.behind, f32[432,128]{1,0:T(8,128)S(1)} %collective-permute-done.11.w1, f32[432,128]{1,0:T(8,128)S(1)} %collective-permute-done.12.w2, f32[432,128]{1,0:T(8,128)S(1)} %collective-permute-done.13.w3), custom_call_target="tpu_custom_call" | custom-call | bytes 6000000 | tf_op jit(solution)/shard_map/pallas_call | solution.py:494
  (35 shorter events, 0.1 us)
Async XLA Ops:
  1.2 21.2 %copy-start = (f32[4,32,896]{2,1,0:T(8,128)S(1)}, f32[4,32,896]{2,1,0:T(8,128)}, u32[]{:S(2)}) copy-start(f32[4,32,896]{2,1,0:T(8,128)} %t.3) | copy-start | bytes 1376260
  1.2 21.2 %copy-start.1 = (s32[32,896]{1,0:T(8,128)S(1)}, s32[32,896]{1,0:T(8,128)}, u32[]{:S(2)}) copy-start(s32[32,896]{1,0:T(8,128)} %mask.3) | copy-start | bytes 344068
  1.2 25.5 %copy-start.15 = (s32[192]{0:T(256)S(1)}, s32[192]{0:T(256)}, u32[]{:S(2)}) copy-start(s32[192]{0:T(256)} %param.22) | copy-start | bytes 2308
  1.2 39.1 %copy-start.12 = (f32[1152]{0:T(1024)S(1)}, f32[1152]{0:T(1024)}, u32[]{:S(2)}) copy-start(f32[1152]{0:T(1024)} %constant.66) | copy-start | bytes 13828
  1.2 39.1 %copy-start.13 = (f32[1152]{0:T(1024)S(1)}, f32[1152]{0:T(1024)}, u32[]{:S(2)}) copy-start(f32[1152]{0:T(1024)} %constant.65) | copy-start | bytes 13828
  1.2 39.1 %copy-start.14 = (pred[1152]{0:T(1024)(128)(4,1)S(1)}, pred[1152]{0:T(1024)(128)(4,1)}, u32[]{:S(2)}) copy-start(pred[1152]{0:T(1024)(128)(4,1)} %constant.63) | copy-start | bytes 3460
  6.3 34.1 %copy-start.4 = (f32[36,1152]{1,0:T(8,128)S(1)}, f32[36,1152]{1,0:T(8,128)}, u32[]{:S(2)}) copy-start(f32[36,1152]{1,0:T(8,128)} %constant.50.clone.with_sin) | copy-start | bytes 497668
  6.3 34.1 %copy-start.5 = (f32[36,1152]{1,0:T(8,128)S(1)}, f32[36,1152]{1,0:T(8,128)}, u32[]{:S(2)}) copy-start(f32[36,1152]{1,0:T(8,128)} %constant.49.clone.with_cos) | copy-start | bytes 497668
  6.4 34.1 %copy-start.6 = (f32[32,1152]{1,0:T(8,128)S(1)}, f32[32,1152]{1,0:T(8,128)}, u32[]{:S(2)}) copy-start(f32[32,1152]{1,0:T(8,128)} %constant.52.clone.sine) | copy-start | bytes 442372
  6.4 34.1 %copy-start.7 = (f32[32,1152]{1,0:T(8,128)S(1)}, f32[32,1152]{1,0:T(8,128)}, u32[]{:S(2)}) copy-start(f32[32,1152]{1,0:T(8,128)} %constant.51.clone.cosine) | copy-start | bytes 442372
  6.4 15.0 %collective-permute-start.6 = (f32[384,128]{1,0:T(8,128)}, f32[384,128]{1,0:T(8,128)S(1)}, u32[]{:S(2)}, u32[]{:S(2)}) collective-permute-start(f32[384,128]{1,0:T(8,128)} %get-tuple-element.39), channel_id=1, source_target_pairs={{0,4},{4,8},{8,12},{12,16},{16,20},{20,24},{24,28},{28,32},{32,36}... | collective-permute-start | bytes 589832 | tf_op jit(solution)/shard_map/ppermute | solution.py:433
  10.1 12.3 %collective-permute-start.7 = (f32[384,128]{1,0:T(8,128)}, f32[384,128]{1,0:T(8,128)S(1)}, u32[]{:S(2)}, u32[]{:S(2)}) collective-permute-start(f32[384,128]{1,0:T(8,128)} %get-tuple-element.40), channel_id=1, source_target_pairs={{4,0},{8,4},{12,8},{16,12},{20,16},{24,20},{28,24},{32,28},{36,32}... | collective-permute-start | bytes 589832 | tf_op jit(solution)/shard_map/ppermute | solution.py:434
  18.5 8.4 %collective-permute-start = (f32[432,128]{1,0:T(8,128)}, f32[432,128]{1,0:T(8,128)S(1)}, u32[]{:S(2)}, u32[]{:S(2)}) collective-permute-start(f32[432,128]{1,0:T(8,128)} %get-tuple-element.32), channel_id=1, source_target_pairs={{0,3},{1,0},{2,1},{3,2},{4,7},{5,4},{6,5},{7,6},{8,11},{9,8},{10,9... | collective-permute-start | bytes 663560 | tf_op jit(solution)/shard_map/ppermute | solution.py:430
  19.6 32.7 %collective-permute-start.1 = (f32[432,128]{1,0:T(8,128)}, f32[432,128]{1,0:T(8,128)S(1)}, u32[]{:S(2)}, u32[]{:S(2)}) collective-permute-start(f32[432,128]{1,0:T(8,128)} %get-tuple-element.33), channel_id=1, source_target_pairs={{0,2},{1,3},{2,0},{3,1},{4,6},{5,7},{6,4},{7,5},{8,10},{9,11},{10,... | collective-permute-start | bytes 663560 | tf_op jit(solution)/shard_map/ppermute | solution.py:430
  22.4 0.9 copy-start.10
  23.5 7.7 %collective-permute-start.9 = (f32[360,128]{1,0:T(8,128)S(1)}, f32[360,128]{1,0:T(8,128)S(1)}, u32[]{:S(2)}, u32[]{:S(2)}) collective-permute-start(f32[360,128]{1,0:T(8,128)S(1)} %get-tuple-element.44), channel_id=1, source_target_pairs={{0,2},{1,3},{2,0},{3,1},{4,6},{5,7},{6,4},{7,5},{8,10},{9,11},{10,... | collective-permute-start | bytes 552968 | tf_op jit(solution)/shard_map/ppermute | solution.py:430
  24.0 15.5 %collective-permute-start.8 = (f32[400,128]{1,0:T(8,128)S(1)}, f32[400,128]{1,0:T(8,128)S(1)}, u32[]{:S(2)}, u32[]{:S(2)}) collective-permute-start(f32[400,128]{1,0:T(8,128)S(1)} %get-tuple-element.43), channel_id=1, source_target_pairs={{0,3},{1,0},{2,1},{3,2},{4,7},{5,4},{6,5},{7,6},{8,11},{9,8},{10,9... | collective-permute-start | bytes 614408 | tf_op jit(solution)/shard_map/ppermute | solution.py:430
  25.8 14.5 %collective-permute-start.10 = (f32[400,128]{1,0:T(8,128)S(1)}, f32[400,128]{1,0:T(8,128)S(1)}, u32[]{:S(2)}, u32[]{:S(2)}) collective-permute-start(f32[400,128]{1,0:T(8,128)S(1)} %get-tuple-element.45), channel_id=1, source_target_pairs={{0,1},{1,2},{2,3},{3,0},{4,5},{5,6},{6,7},{7,4},{8,9},{9,10},{10,1... | collective-permute-start | bytes 614408 | tf_op jit(solution)/shard_map/ppermute | solution.py:430
  26.9 25.3 %collective-permute-start.2 = (f32[432,128]{1,0:T(8,128)}, f32[432,128]{1,0:T(8,128)S(1)}, u32[]{:S(2)}, u32[]{:S(2)}) collective-permute-start(f32[432,128]{1,0:T(8,128)} %get-tuple-element.34), channel_id=1, source_target_pairs={{0,1},{1,2},{2,3},{3,0},{4,5},{5,6},{6,7},{7,4},{8,9},{9,10},{10,1... | collective-permute-start | bytes 663560 | tf_op jit(solution)/shard_map/ppermute | solution.py:430
  31.2 21.1 %collective-permute-start.3 = (f32[864,128]{1,0:T(8,128)}, f32[864,128]{1,0:T(8,128)S(1)}, u32[]{:S(2)}, u32[]{:S(2)}) collective-permute-start(f32[864,128]{1,0:T(8,128)} %get-tuple-element.36), channel_id=1, source_target_pairs={{0,3},{1,0},{2,1},{3,2},{4,7},{5,4},{6,5},{7,6},{8,11},{9,8},{10,9... | collective-permute-start | bytes 1327112 | tf_op jit(solution)/shard_map/ppermute | solution.py:430
  39.5 12.7 %collective-permute-start.4 = (f32[864,128]{1,0:T(8,128)}, f32[864,128]{1,0:T(8,128)S(1)}, u32[]{:S(2)}, u32[]{:S(2)}) collective-permute-start(f32[864,128]{1,0:T(8,128)} %get-tuple-element.37), channel_id=1, source_target_pairs={{0,2},{1,3},{2,0},{3,1},{4,6},{5,7},{6,4},{7,5},{8,10},{9,11},{10,... | collective-permute-start | bytes 1327112 | tf_op jit(solution)/shard_map/ppermute | solution.py:430
  40.3 17.1 %collective-permute-start.5 = (f32[864,128]{1,0:T(8,128)}, f32[864,128]{1,0:T(8,128)S(1)}, u32[]{:S(2)}, u32[]{:S(2)}) collective-permute-start(f32[864,128]{1,0:T(8,128)} %get-tuple-element.38), channel_id=1, source_target_pairs={{0,1},{1,2},{2,3},{3,0},{4,5},{5,6},{6,7},{7,4},{8,9},{9,10},{10,1... | collective-permute-start | bytes 1327112 | tf_op jit(solution)/shard_map/ppermute | solution.py:430
  41.9 4.6 %copy-start.8 = (s32[32,896]{1,0:T(8,128)S(1)}, s32[32,896]{1,0:T(8,128)}, u32[]{:S(2)}) copy-start(s32[32,896]{1,0:T(8,128)} %rows.1) | copy-start | bytes 344068
  42.0 4.6 %copy-start.9 = (s32[32,896]{1,0:T(8,128)S(1)}, s32[32,896]{1,0:T(8,128)}, u32[]{:S(2)}) copy-start(s32[32,896]{1,0:T(8,128)} %cols.1) | copy-start | bytes 344068
  42.0 4.6 %copy-start.11 = (s32[2]{0:T(128)S(1)}, s32[2]{0:T(128)}, u32[]{:S(2)}) copy-start(s32[2]{0:T(128)} %pad_add_fusion.place) | copy-start | bytes 28
  42.0 15.4 %copy-start.2 = (f32[864,128]{1,0:T(8,128)S(1)}, f32[864,128]{1,0:T(8,128)}, u32[]{:S(2)}) copy-start(f32[864,128]{1,0:T(8,128)} %get-tuple-element.35.n0) | copy-start | bytes 1327108
  42.0 15.4 %copy-start.3 = (f32[432,128]{1,0:T(8,128)S(1)}, f32[432,128]{1,0:T(8,128)}, u32[]{:S(2)}) copy-start(f32[432,128]{1,0:T(8,128)} %get-tuple-element.31.m0) | copy-start | bytes 663556
  72.9 26.7 %collective-permute-start.11 = (f32[432,128]{1,0:T(8,128)S(1)}, f32[432,128]{1,0:T(8,128)S(1)}, u32[]{:S(2)}, u32[]{:S(2)}) collective-permute-start(f32[432,128]{1,0:T(8,128)S(1)} %get-tuple-element.52), channel_id=1, source_target_pairs={{0,1},{1,2},{2,3},{3,0},{4,5},{5,6},{6,7},{7,4},{8,9},{9,10},{10,1... | collective-permute-start | bytes 663560 | tf_op jit(solution)/shard_map/ppermute | solution.py:430
  75.6 24.1 %collective-permute-start.12 = (f32[432,128]{1,0:T(8,128)S(1)}, f32[432,128]{1,0:T(8,128)S(1)}, u32[]{:S(2)}, u32[]{:S(2)}) collective-permute-start(f32[432,128]{1,0:T(8,128)S(1)} %get-tuple-element.53), channel_id=1, source_target_pairs={{0,2},{1,3},{2,0},{3,1},{4,6},{5,7},{6,4},{7,5},{8,10},{9,11},{10,... | collective-permute-start | bytes 663560 | tf_op jit(solution)/shard_map/ppermute | solution.py:430
  76.5 23.2 %collective-permute-start.13 = (f32[432,128]{1,0:T(8,128)S(1)}, f32[432,128]{1,0:T(8,128)S(1)}, u32[]{:S(2)}, u32[]{:S(2)}) collective-permute-start(f32[432,128]{1,0:T(8,128)S(1)} %get-tuple-element.54), channel_id=1, source_target_pairs={{0,3},{1,0},{2,1},{3,2},{4,7},{5,4},{6,5},{7,6},{8,11},{9,8},{10,9... | collective-permute-start | bytes 663560 | tf_op jit(solution)/shard_map/ppermute | solution.py:430
  76.5 9.9 %collective-permute-start.15 = (f32[4,896]{1,0:T(4,128)S(1)}, f32[4,896]{1,0:T(4,128)S(1)}, u32[]{:S(2)}, u32[]{:S(2)}) collective-permute-start(f32[4,896]{1,0:T(4,128)S(1)} %get-tuple-element.57), channel_id=1, source_target_pairs={{4,0},{8,4},{12,8},{16,12},{20,16},{24,20},{28,24},{32,28},{36,32}... | collective-permute-start | bytes 43016 | tf_op jit(solution)/shard_map/ppermute | solution.py:434
  84.5 9.0 %collective-permute-start.14 = (f32[4,896]{1,0:T(4,128)S(1)}, f32[4,896]{1,0:T(4,128)S(1)}, u32[]{:S(2)}, u32[]{:S(2)}) collective-permute-start(f32[4,896]{1,0:T(4,128)S(1)} %get-tuple-element.50.after), channel_id=1, source_target_pairs={{0,4},{4,8},{8,12},{12,16},{16,20},{20,24},{24,28},{28,32},{32,36}... | collective-permute-start | bytes 43016 | tf_op jit(solution)/shard_map/ppermute | solution.py:433
  93.5 4.1 %collective-permute-start.16 = (f32[40,4]{1,0:T(8,128)S(1)}, f32[40,4]{1,0:T(8,128)S(1)}, u32[]{:S(2)}, u32[]{:S(2)}) collective-permute-start(f32[40,4]{1,0:T(8,128)S(1)} %get-tuple-element.58), channel_id=1, source_target_pairs={{0,3},{1,0},{2,1},{3,2},{4,7},{5,4},{6,5},{7,6},{8,11},{9,8},{10,9... | collective-permute-start | bytes 1928 | tf_op jit(solution)/shard_map/ppermute | solution.py:430
  95.4 2.2 %collective-permute-start.17 = (f32[40,4]{1,0:T(8,128)S(1)}, f32[40,4]{1,0:T(8,128)S(1)}, u32[]{:S(2)}, u32[]{:S(2)}) collective-permute-start(f32[40,4]{1,0:T(8,128)S(1)} %get-tuple-element.59), channel_id=1, source_target_pairs={{0,1},{1,2},{2,3},{3,0},{4,5},{5,6},{6,7},{7,4},{8,9},{9,10},{10,1... | collective-permute-start | bytes 1928 | tf_op jit(solution)/shard_map/ppermute | solution.py:430

commit v2 on v1

--- a/solution.py
+++ b/solution.py
@@ -49,11 +49,26 @@
 
 
 LEVEL_AT, OCEAN_AT, SEA_AT, LAT_WIRE = 288, 312, 368, 384
-WIND_AT, STRIP_AT, RIM_WIRE = 144, 360, 400
+FIRST, SECOND = FT + 192, 2 * FT - 192
+STRIP_AT, RIM_WIRE, WINDOW = 144, 184, 216
 TILES = OCOLS // 128
 
 
-def pack_kernel(place, q_in, u_in, v_in, t_in, mask_in, a0, a1, a2, a3, b0, b1, b2, b3, up, down, mid, q, u, v, t, mask, sems):
+def wire_places(f, first, second):
+    if f == 0:
+        return ((first, 0), (first, 192), (first, 384))
+    if f == 1:
+        return ((first, FT), (second, 0), (second, 192))
+    return ((second, 240), (second, 432), (second, 624))
+
+
+def cross(place, a, b, first, second):
+    odd = jnp.full(a.shape, place[1] % 2, jnp.int32) == 1
+    first[...] = jnp.where(odd, a[...], b[...])
+    second[...] = jnp.where(odd, b[...], a[...])
+
+
+def pack_kernel(place, q_in, u_in, v_in, t_in, mask_in, a0, a1, a2, a3, b0, b1, b2, b3, x0, x1, mid, q, u, v, t, mask, up, down, sems):
     copies = [
         [
             pltpu.make_async_copy(source.at[pl.ds(LB * i, LB)], target.at[pl.ds(LB * i, LB)], sems.at[f, i])
@@ -70,12 +85,14 @@
         for copy in copies[f]:
             copy.wait()
         for s in range(LONS):
-            wire, base = (first_wires[s], 0) if f == 0 else (second_wires[s], (f - 1) * FT)
+            places = wire_places(f, first_wires[s], second_wires[s])
             first = (place[0] + s) % LONS * LB
             for l in range(LB):
                 for c in range(2):
-                    wire[pl.ds(base + c * 192 + l, ROWS, stride=8), :] = field[first + l, :, c * 128 : c * 128 + 128]
-                wire[pl.ds(base + 384 + l, 6, stride=8), :] = jnp.concatenate(
+                    wire, base = places[c]
+                    wire[pl.ds(base + l, ROWS, stride=8), :] = field[first + l, :, c * 128 : c * 128 + 128]
+                wire, base = places[2]
+                wire[pl.ds(base + l, 6, stride=8), :] = jnp.concatenate(
                     [field[first + l, 6 * i : 6 * i + 6, 256:288] for i in range(4)], axis=1
                 )
     for copy in copies[3]:
@@ -107,9 +124,11 @@
             out[SEA_AT + 2 * c : SEA_AT + 2 * c + 2, :] = mask[o : o + 2, c * 128 : c * 128 + 128].astype(f32)
     for f, field in enumerate((q, u, v)):
         mid[f, :, :] = field[LEV - 1, :, :]
-
-
-def join_kernel(before, after, mid, t, mask, w0, w1, w2, w3, win):
+    cross(place, up, down, x0, x1)
+
+
+def join_kernel(place, x0, x1, mid, t, mask, w0, w1, w2, w3, circle, before, after, win):
+    cross(place, x1, x0, before, after)
     wires = (w0, w1, w2, w3)
     for s, wire in enumerate(wires):
         wire[0:72, :] = before[s * 72 : s * 72 + 72, :]
@@ -123,11 +142,9 @@
             win[4 - n : 4, c * 128 : c * 128 + width] = before[rows : rows + n, 0:width]
             win[4 + ROWS : 4 + ROWS + n, c * 128 : c * 128 + width] = after[rows : rows + n, 0:width]
         rem = jnp.concatenate([win[8 * i : 8 * i + 8, 256:288] for i in range(4)], axis=1)
-        for wire in wires:
-            base = WIND_AT + f * 72
-            wire[base : base + 32, :] = win[:, 0:128]
-            wire[base + 32 : base + 64, :] = win[:, 128:256]
-            wire[base + 64 : base + 72, :] = rem
+        circle[f * 72 : f * 72 + 32, :] = win[:, 0:128]
+        circle[f * 72 + 32 : f * 72 + 64, :] = win[:, 128:256]
+        circle[f * 72 + 64 : f * 72 + 72, :] = rem
     pad = 128 - 2 * (OLEV + 1)
     for wire, col in ((w3, 0), (w1, OCOLS - 2)):
         tile, lane = col // 128, col % 128
@@ -202,7 +219,7 @@
 
 def bottom_kernel(w0, w1, w2, w3, damp, bh, bl, heat, speed):
     def circle(f):
-        base, parts = WIND_AT + f * 72, []
+        base, parts = f * 72, []
         for w in (w0, w1, w2, w3):
             parts += [w[base : base + 32, :], w[base + 32 : base + 64, :]]
             parts.append(
@@ -221,17 +238,17 @@
         out[:, 256:384] = jnp.where(lane < 64, field[:, 256:384], field[:, NLON - 128 : NLON])
 
 
-def bulk_kernel(m0, m1, m2, m3, n0, n1, n2, n3, h0, h1, h2, h3, damp, bh, bl, after, o0, o1, o2, o3, qs, us, vs, xs):
+def bulk_kernel(m0, m1, m2, m3, n0, n1, n2, n3, h0, h1, h2, h3, damp, bh, bl, after, far, top_out, rest_out, qs, us, vs, xs):
     halos = (h0, h1, h2, h3)
 
     def main_slab(f, r):
         parts = []
-        for w in (m0, m1, m2, m3) if f == 0 else (n0, n1, n2, n3):
-            base = max(f - 1, 0) * FT
-            parts.append(w[base + r * 8 : base + r * 8 + 8, :])
-            parts.append(w[base + 192 + r * 8 : base + 200 + r * 8, :])
+        for first, second in zip((m0, m1, m2, m3), (n0, n1, n2, n3)):
+            (w0, at0), (w1, at1), (w2, at2) = wire_places(f, first, second)
             g, i = r % 6, r // 6
-            parts.append(w[base + 384 + g * 8 : base + 392 + g * 8, 32 * i : 32 * i + 32])
+            parts.append(w0[at0 + r * 8 : at0 + r * 8 + 8, :])
+            parts.append(w1[at1 + r * 8 : at1 + r * 8 + 8, :])
+            parts.append(w2[at2 + g * 8 : at2 + g * 8 + 8, 32 * i : 32 * i + 32])
         return jnp.concatenate(parts, axis=1)
 
     def halo_slab(side, i):
@@ -289,19 +306,36 @@
     lax.fori_loop(0, ROWS, second, 0)
     xs[0:192, :] = product(xs[0:192, :], bh, bl)
     scale(ROWS, 4)
-    xs[0:192, :] = product(xs[0:192, :], bh, bl, back=True)
-    for p, out in enumerate((o0, o1, o2, o3)):
-        for g in range(6):
-            rems = []
-            for r in range(g, ROWS, 6):
-                piece = xs[r * 8 : r * 8 + 8, p * COLS : p * COLS + COLS]
-                out[r * 8 : r * 8 + 8, :] = piece[:, 0:128]
-                out[192 + r * 8 : 200 + r * 8, :] = piece[:, 128:256]
-                rems.append(piece[:, 256:288])
-            out[384 + g * 8 : 392 + g * 8, :] = jnp.concatenate(rems, axis=1)
-
-
-def pick_kernel(place, rows, cols, heat, speed, air_heat, air_speed, up, down):
+    top, rest = split(xs[0:192, :])
+    top_out[...] = top
+    rest_out[...] = rest
+    write_piece(far, project(top, rest, bh[2 * COLS : 3 * COLS, :], bl[2 * COLS : 3 * COLS, :]))
+
+
+def project(top, rest, hi, lo):
+    dims = (((1,), (1,)), ((), ()))
+    lines = top.shape[0]
+    both = lax.dot_general(jnp.concatenate([top, rest], axis=0), hi, dims, preferred_element_type=f32)
+    return both[:lines] + both[lines:] + lax.dot_general(top, lo, dims, preferred_element_type=f32)
+
+
+def write_piece(out, piece):
+    for g in range(6):
+        rems = []
+        for r in range(g, ROWS, 6):
+            out[r * 8 : r * 8 + 8, :] = piece[r * 8 : r * 8 + 8, 0:128]
+            out[192 + r * 8 : 200 + r * 8, :] = piece[r * 8 : r * 8 + 8, 128:256]
+            rems.append(piece[r * 8 : r * 8 + 8, 256:288])
+        out[384 + g * 8 : 392 + g * 8, :] = jnp.concatenate(rems, axis=1)
+
+
+def finish_kernel(top, rest, bh, bl, o0, o1, o3):
+    for out, p in ((o3, 3), (o1, 1), (o0, 0)):
+        rows = slice(p * COLS, p * COLS + COLS)
+        write_piece(out, project(top[...], rest[...], bh[rows, :], bl[rows, :]))
+
+
+def pick_kernel(place, rows, cols, heat, speed, air_heat, air_speed, x0, x1, up, down):
     def body(k, carry):
         start = pl.multiple_of(k * 8, 8)
         for c in range(TILES):
@@ -328,9 +362,11 @@
     for f, field in enumerate((air_heat, air_speed)):
         up[2 * f : 2 * f + 2, :] = field[OROWS - 2 : OROWS, :]
         down[2 * f : 2 * f + 2, :] = field[0:2, :]
-
-
-def ring_kernel(heat, speed, before, after, behind, east, west):
+    cross(place, up, down, x0, x1)
+
+
+def ring_kernel(place, heat, speed, x0, x1, behind, east, west, before, after):
+    cross(place, x1, x0, before, after)
     for out, col in ((east, 0), (west, OCOLS - 2)):
         out[0:OROWS, :] = jnp.concatenate([heat[:, col : col + 2], speed[:, col : col + 2]], axis=1)
         out[OROWS:WROWS, :] = jnp.zeros((WROWS - OROWS, 4), f32)
@@ -423,25 +459,28 @@
     lat_devices = lax.axis_size("lat")
     lat_place, lon_place = lax.axis_index("lat"), lax.axis_index("lon")
     place = jnp.stack([lon_place, lat_place]).astype(jnp.int32)
-    north = [(i, i + 1) for i in range(lat_devices - 1)]
-    south = [(j, i) for i, j in north]
+    swaps = [
+        [pair for i in range(start, lat_devices - 1, 2) for pair in ((i, i + 1), (i + 1, i))] for start in (1, 0)
+    ]
 
     def along(x, s):
         return lax.ppermute(x, "lon", [(i, (i + s) % LONS) for i in range(LONS)])
 
-    def across(to_north, to_south):
-        before = lax.ppermute(to_north, "lat", north)
-        return before, lax.ppermute(to_south, "lat", south)
+    def across(first, second):
+        got = lax.ppermute(first, "lat", swaps[0])
+        return got, lax.ppermute(second, "lat", swaps[1])
 
     packed = call(
         pack_kernel,
-        [sds(FT, 128)] * 4 + [sds(2 * FT, 128)] * 4 + [sds(LAT_WIRE, 128)] * 2 + [sds(3, ROWS, COLS)],
+        [sds(FIRST, 128)] * 4 + [sds(SECOND, 128)] * 4 + [sds(LAT_WIRE, 128)] * 2 + [sds(3, ROWS, COLS)],
         smem=1,
         n_any=5,
         scratch=[pltpu.VMEM((LEV, ROWS, COLS), f32)] * 3
         + [
             pltpu.VMEM((OLEV, OROWS, OCOLS), f32),
             pltpu.VMEM((OROWS, OCOLS), jnp.int32),
+            pltpu.VMEM((LAT_WIRE, 128), f32),
+            pltpu.VMEM((LAT_WIRE, 128), f32),
             pltpu.SemaphoreType.DMA((4, LONS)),
         ],
         cost=cost(5),
@@ -449,41 +488,49 @@
     )(place, tracer, wind_u, wind_v, ocean_temp, land_mask)
     mains, winds, mid = packed[:4], packed[4:8], packed[10]
     pieces = [mains[0]] + [along(mains[s], s) for s in (3, 2, 1)]
-    before, after = across(packed[8], packed[9])
+    near0, near1 = across(packed[8], packed[9])
 
     basis = call(basis_kernel, [sds(NLON, NLON, dtype=bf16)] * 2, n_in=4, cost=cost(3))(*wave_tables())
     damp = damp_window(lat_place, polar_rows, ROWS * lat_devices, lat_devices // 8 * ROWS)
     joined = call(
         join_kernel,
-        [sds(RIM_WIRE if s in (1, 3) else STRIP_AT, 128) for s in range(LONS)],
+        [sds(RIM_WIRE if s in (1, 3) else STRIP_AT, 128) for s in range(LONS)]
+        + [sds(WINDOW, 128)]
+        + [sds(LAT_WIRE, 128)] * 2,
+        smem=1,
         n_in=5,
         scratch=[pltpu.VMEM((WIN, 384), f32)],
         cost=cost(2),
-    )(before, after, mid, ocean_temp, land_mask)
+    )(place, near0, near1, mid, ocean_temp, land_mask)
+    before, after = joined[5:]
+    windows = [joined[4]] + [along(joined[4], s) for s in (3, 2, 1)]
     rims = [joined[0]] + [along(joined[s], s) for s in (3, 2, 1)]
     blows = [winds[0]] + [along(winds[s], s) for s in (3, 2, 1)]
 
-    heat, speed = call(bottom_kernel, [sds(WIN, 384)] * 2, n_in=7, cost=cost(8))(*rims, damp, *basis)
+    heat, speed = call(bottom_kernel, [sds(WIN, 384)] * 2, n_in=7, cost=cost(8))(*windows, damp, *basis)
     air_heat, air_speed, air_up, air_down = call(
-        pick_kernel, [sds(OROWS, OCOLS)] * 2 + [sds(4, OCOLS)] * 2, smem=1, n_in=4, cost=cost(7)
+        pick_kernel, [sds(OROWS, OCOLS)] * 2 + [sds(4, OCOLS)] * 2, smem=1, n_in=4, cost=cost(7),
+        scratch=[pltpu.VMEM((4, OCOLS), f32)] * 2,
     )(place, remap_rows, remap_cols, heat, speed)
-    air_before, air_after = across(air_up, air_down)
+    air0, air1 = across(air_up, air_down)
 
     lines = (ROWS + 4) * LB
-    outs = call(
+    far, top, rest = call(
         bulk_kernel,
-        [sds(FT, 128)] * 4,
+        [sds(FT, 128)] + [sds(ROWS * LB, NLON, dtype=bf16)] * 2,
         n_in=15,
         n_any=1,
         scratch=[pltpu.VMEM((lines, NLON), f32)] + [pltpu.VMEM((lines - 16, NLON), f32)] * 3,
-        cost=cost(18),
+        cost=cost(13),
         mib=36,
     )(*pieces, *blows, *rims, damp, *basis, air_up)
-    back = [outs[0]] + [along(outs[s], s) for s in (1, 2, 3)]
-
-    east, west = call(ring_kernel, [sds(WROWS, 4)] * 2, n_in=4, n_any=1, cost=cost(1))(
-        air_heat, air_speed, air_before, air_after, outs[0]
-    )
+    far = along(far, 2)
+    own, one, three = call(finish_kernel, [sds(FT, 128)] * 3, n_in=4, cost=cost(3))(top, rest, *basis)
+    back = [own, along(one, 1), far, along(three, 3)]
+
+    east, west, air_before, air_after = call(
+        ring_kernel, [sds(WROWS, 4)] * 2 + [sds(4, OCOLS)] * 2, smem=1, n_in=4, n_any=1, cost=cost(1)
+    )(place, air_heat, air_speed, air0, air1, top)
     air_east, air_west = along(east, LONS - 1), along(west, 1)
     ocean_out = call(
         ocean_kernel, sds(OLEV, OROWS, OCOLS), n_in=12, scratch=[pltpu.VMEM((7, WROWS, WCOLS), f32)], cost=cost(3)

time: 102 us -> 101 us (level)
  waiting for transfers between devices: 23.5 us -> 20.6 us
  Pallas kernels: 36.4 us -> 38.5 us
    ppermute x4, starting transfers between devices: 22 us -> 16.8 us  [the longest x2 16.7 us: across(): got = lax.ppermute(first, 'lat', swaps[0])]
    ppermute x14 -> x17, starting transfers between devices: 16.7 us -> 21.3 us  [along(): return lax.ppermute(x, 'lon', [(i, (i + s) % LONS) for i in range(LONS)])]
    ppermute x4, waiting for transfers between devices: 9.43 us -> 5.55 us  [the longest x2 4.55 us: across(): got = lax.ppermute(first, 'lat', swaps[0])]
    pallas_call x3 -> x4, Pallas kernels: 20.7 us -> 22.3 us  [the longest x1 14 us: per_device(): call(bulk_kernel, [sds(FT, 128)] + [sds(ROWS * LB, NLON, dtype=bf16)] * 2...]
    ppermute x14 -> x17, waiting for transfers between devices: 14.1 us -> 15 us  [along(): return lax.ppermute(x, 'lon', [(i, (i + s) % LONS) for i in range(LONS)])]
  transfers between devices with their start and end apart: 18 -> 21, of which waited for: 7 -> 9; matrix products, arithmetic and copies ran while one was open for 0% -> 0% of each run, Pallas kernels for 14% -> 15%
where the time goes in v2:
time: 101 us; the launch traced here: 100 us
  Pallas kernels  38.5 us (38%)
  starting transfers between devices  38.1 us (38%)
  waiting for transfers between devices  20.6 us (20%)
    ppermute x17, starting transfers between devices, along(): return lax.ppermute(x, 'lon', [(i, (i + s) % LONS) for i in range(LONS)])  21.3 us
    ppermute x2, starting transfers between devices, across(): got = lax.ppermute(first, 'lat', swaps[0])  16.7 us
    ppermute x17, waiting for transfers between devices, along(): return lax.ppermute(x, 'lon', [(i, (i + s) % LONS) for i in range(LONS)])  15 us
    pallas_call x1, Pallas kernels, per_device(): call(bulk_kernel, [sds(FT, 128)] + [sds(ROWS * LB, NLON, dtype=bf16)] * 2...  14 us
    pallas_call x1, Pallas kernels, per_device(): call(pick_kernel, [sds(OROWS, OCOLS)] * 2 + [sds(4, OCOLS)] * 2, smem=1,...  5.64 us
    pallas_call x1, Pallas kernels, per_device(): call(pack_kernel, [sds(FIRST, 128)] * 4 + [sds(SECOND, 128)] * 4 + [sds(L...  5.08 us
    ppermute x2, waiting for transfers between devices, across(): got = lax.ppermute(first, 'lat', swaps[0])  4.55 us
    pallas_call x1, Pallas kernels, per_device(): call(bottom_kernel, [sds(WIN, 384)] * 2, n_in=7, cost=cost(8))  4.5 us
  transfers between devices with their start and end apart: 21, of which 9 were waited for; matrix products, arithmetic and copies ran while one was open for 0% of the time, Pallas kernels for 15%

profile of v2, /device:TPU:3, one launch (start us, length us, event | category | flops | bytes accessed | tf_op | source)
XLA Modules:
  0.0 100.1 jit_solution(6059949709712617587)
XLA Ops:
  0.6 0.6 pad_add_fusion.place
  1.3 0.0 copy-start.15
  1.3 0.0 copy-start
  1.3 0.0 copy-start.1
  1.3 5.1 %shard_map.158 = (f32[624,128]{1,0:T(8,128)}, f32[624,128]{1,0:T(8,128)}, f32[624,128]{1,0:T(8,128)}, f32[624,128]{1,0:T(8,128)}, f32[672,128]{1,0:T(8,128)}, /*...) custom-call(s32[2]{0:T(128)} %pad_add_fusion.place, ...), custom_call_target="tpu_custom_call" | custom-call | bytes 15000000 | tf_op jit(solution)/shard_map/pallas_call | solution.py:473
  6.4 0.0 copy-start.12
  6.4 0.0 copy-start.13
  6.5 0.0 copy-start.14
  6.5 10.2 %collective-permute-start.6 = (f32[384,128]{1,0:T(8,128)}, f32[384,128]{1,0:T(8,128)S(1)}, u32[]{:S(2)}, u32[]{:S(2)}) collective-permute-start(f32[384,128]{1,0:T(8,128)} %get-tuple-element.46), channel_id=1, source_target_pairs={{4,8},{8,4},{12,16},{16,12},{20,24},{24,20},{28,32},{32,28},{36,40... | collective-permute-start | bytes 589832 | tf_op jit(solution)/shard_map/ppermute | solution.py:470
  16.7 0.1 collective-permute-start.7
  16.8 1.0 %collective-permute-start = (f32[624,128]{1,0:T(8,128)}, f32[624,128]{1,0:T(8,128)S(1)}, u32[]{:S(2)}, u32[]{:S(2)}) collective-permute-start(f32[624,128]{1,0:T(8,128)} %get-tuple-element.39), channel_id=1, source_target_pairs={{0,3},{1,0},{2,1},{3,2},{4,7},{5,4},{6,5},{7,6},{8,11},{9,8},{10,9... | collective-permute-start | bytes 958472 | tf_op jit(solution)/shard_map/ppermute | solution.py:467
  17.8 1.5 %shard_map.160 = (bf16[1152,1152]{1,0:T(8,128)(2,1)S(1)}, bf16[1152,1152]{1,0:T(8,128)(2,1)S(1)}) custom-call(f32[36,1152]{1,0:T(8,128)S(1)} %copy-done.5, f32[36,1152]{1,0:T(8,128)S(1)} %copy-done.4, f32[32,1152]{1,0:T(8,128)S(1)} %copy-done.7, f32[32,1152]{1,0:T(8,128)S(1)} %copy-done.6), custom_call_target="tpu_custom_call" | custom-call | bytes 9000000 | tf_op jit(solution)/shard_map/pallas_call | solution.py:493
  19.4 0.2 compare_reduce_fusion
  19.5 2.0 %collective-permute-done.6.x0 = f32[384,128]{1,0:T(8,128)S(1)} collective-permute-done((f32[384,128]{1,0:T(8,128)}, f32[384,128]{1,0:T(8,128)S(1)}, u32[]{:S(2)}, u32[]{:S(2)}) %collective-permute-start.6) | collective-permute-done | bytes 196640 | tf_op jit(solution)/shard_map/ppermute | solution.py:470
  21.5 1.0 %collective-permute-done.7.x1 = f32[384,128]{1,0:T(8,128)S(1)} collective-permute-done((f32[384,128]{1,0:T(8,128)}, f32[384,128]{1,0:T(8,128)S(1)}, u32[]{:S(2)}, u32[]{:S(2)}) %collective-permute-start.7) | collective-permute-done | bytes 196640 | tf_op jit(solution)/shard_map/ppermute | solution.py:471
  22.5 0.9 copy-done.10
  23.4 0.7 shard_map.159
  24.2 0.5 collective-permute-start.9
  24.6 2.1 %collective-permute-start.8 = (f32[184,128]{1,0:T(8,128)S(1)}, f32[184,128]{1,0:T(8,128)S(1)}, u32[]{:S(2)}, u32[]{:S(2)}) collective-permute-start(f32[184,128]{1,0:T(8,128)S(1)} %get-tuple-element.50), channel_id=1, source_target_pairs={{0,3},{1,0},{2,1},{3,2},{4,7},{5,4},{6,5},{7,6},{8,11},{9,8},{10,9... | collective-permute-start | bytes 282632 | tf_op jit(solution)/shard_map/ppermute | solution.py:467
  26.8 1.0 %collective-permute-start.13 = (f32[216,128]{1,0:T(8,128)S(1)}, f32[216,128]{1,0:T(8,128)S(1)}, u32[]{:S(2)}, u32[]{:S(2)}) collective-permute-start(f32[216,128]{1,0:T(8,128)S(1)} %get-tuple-element.55.w0), channel_id=1, source_target_pairs={{0,1},{1,2},{2,3},{3,0},{4,5},{5,6},{6,7},{7,4},{8,9},{9,10},{10,1... | collective-permute-start | bytes 331784 | tf_op jit(solution)/shard_map/ppermute | solution.py:467
  27.8 0.4 collective-permute-start.12
  28.2 2.8 %collective-permute-start.11 = (f32[216,128]{1,0:T(8,128)S(1)}, f32[216,128]{1,0:T(8,128)S(1)}, u32[]{:S(2)}, u32[]{:S(2)}) collective-permute-start(f32[216,128]{1,0:T(8,128)S(1)} %get-tuple-element.55.w0), channel_id=1, source_target_pairs={{0,3},{1,0},{2,1},{3,2},{4,7},{5,4},{6,5},{7,6},{8,11},{9,8},{10,9... | collective-permute-start | bytes 331784 | tf_op jit(solution)/shard_map/ppermute | solution.py:467
  31.0 1.3 %collective-permute-done.8.h1.east = f32[184,128]{1,0:T(8,128)S(1)} collective-permute-done((f32[184,128]{1,0:T(8,128)S(1)}, f32[184,128]{1,0:T(8,128)S(1)}, u32[]{:S(2)}, u32[]{:S(2)}) %collective-permute-start.8) | collective-permute-done | bytes 94240 | tf_op jit(solution)/shard_map/ppermute | solution.py:467
  32.3 2.7 %collective-permute-done.10.h3.west = f32[184,128]{1,0:T(8,128)S(1)} collective-permute-done((f32[184,128]{1,0:T(8,128)S(1)}, f32[184,128]{1,0:T(8,128)S(1)}, u32[]{:S(2)}, u32[]{:S(2)}) %collective-permute-start.10) | collective-permute-done | bytes 94240 | tf_op jit(solution)/shard_map/ppermute | solution.py:467
  35.0 0.5 collective-permute-start.1
  35.5 2.8 %collective-permute-start.2 = (f32[624,128]{1,0:T(8,128)}, f32[624,128]{1,0:T(8,128)S(1)}, u32[]{:S(2)}, u32[]{:S(2)}) collective-permute-start(f32[624,128]{1,0:T(8,128)} %get-tuple-element.41), channel_id=1, source_target_pairs={{0,1},{1,2},{2,3},{3,0},{4,5},{5,6},{6,7},{7,4},{8,9},{9,10},{10,1... | collective-permute-start | bytes 958472 | tf_op jit(solution)/shard_map/ppermute | solution.py:467
  38.3 1.0 %collective-permute-start.4 = (f32[672,128]{1,0:T(8,128)}, f32[672,128]{1,0:T(8,128)S(1)}, u32[]{:S(2)}, u32[]{:S(2)}) collective-permute-start(f32[672,128]{1,0:T(8,128)} %get-tuple-element.44), channel_id=1, source_target_pairs={{0,2},{1,3},{2,0},{3,1},{4,6},{5,7},{6,4},{7,5},{8,10},{9,11},{10,... | collective-permute-start | bytes 1032200 | tf_op jit(solution)/shard_map/ppermute | solution.py:467
  39.3 1.9 %collective-permute-start.5 = (f32[672,128]{1,0:T(8,128)S(1)}, f32[672,128]{1,0:T(8,128)S(1)}, u32[]{:S(2)}, u32[]{:S(2)}) collective-permute-start(f32[672,128]{1,0:T(8,128)S(1)} %copy-done.16), channel_id=1, source_target_pairs={{0,1},{1,2},{2,3},{3,0},{4,5},{5,6},{6,7},{7,4},{8,9},{9,10},{10,1... | collective-permute-start | bytes 1032200 | tf_op jit(solution)/shard_map/ppermute | solution.py:467
  41.3 0.1 fusion.3.damp
  41.4 0.0 copy-start.2
  41.4 4.5 %shard_map.161 = (f32[32,384]{1,0:T(8,128)S(1)}, f32[32,384]{1,0:T(8,128)S(1)}) custom-call(f32[216,128]{1,0:T(8,128)S(1)} %get-tuple-element.55.w0, f32[216,128]{1,0:T(8,128)S(1)} %collective-permute-done.11.w1, f32[216,128]{1,0:T(8,128)S(1)} %collective-permute-done.12.w2, f32[216,128]{1,0:T(8,128)S(1)} %collective-permute-done.13.w3, ...), custom_call_target="tpu_custom_call" | custom-call | bytes 24000000 | tf_op jit(solution)/shard_map/pallas_call | solution.py:510
  45.9 0.0 copy-done.8
  46.0 5.6 %shard_map.162 = (f32[32,896]{1,0:T(8,128)S(1)}, f32[32,896]{1,0:T(8,128)S(1)}, f32[4,896]{1,0:T(4,128)S(1)}, f32[4,896]{1,0:T(4,128)S(1)}) custom-call(s32[2]{0:T(128)S(1)} %copy-done.11, s32[32,896]{1,0:T(8,128)S(1)} %copy-done.8, s32[32,896]{1,0:T(8,128)S(1)} %copy-done.9, f32[32,384]{1,0:T(8,128)S(1)} %get-tuple-element.56.heat, ...), custom_call_target="tpu_custom_call" | custom-call | bytes 21000000 | tf_op jit(solution)/shard_map/pallas_call | solution.py:511
  51.6 2.3 %collective-permute-done.3.n1 = f32[672,128]{1,0:T(8,128)S(1)} collective-permute-done((f32[672,128]{1,0:T(8,128)}, f32[672,128]{1,0:T(8,128)S(1)}, u32[]{:S(2)}, u32[]{:S(2)}) %collective-permute-start.3) | collective-permute-done | bytes 344096 | tf_op jit(solution)/shard_map/ppermute | solution.py:467
  53.9 3.1 %collective-permute-done.4.n2 = f32[672,128]{1,0:T(8,128)S(1)} collective-permute-done((f32[672,128]{1,0:T(8,128)}, f32[672,128]{1,0:T(8,128)S(1)}, u32[]{:S(2)}, u32[]{:S(2)}) %collective-permute-start.4) | collective-permute-done | bytes 344096 | tf_op jit(solution)/shard_map/ppermute | solution.py:467
  57.0 4.2 %collective-permute-done.5.n3 = f32[672,128]{1,0:T(8,128)S(1)} collective-permute-done((f32[672,128]{1,0:T(8,128)S(1)}, f32[672,128]{1,0:T(8,128)S(1)}, u32[]{:S(2)}, u32[]{:S(2)}) %collective-permute-start.5) | collective-permute-done | bytes 344096 | tf_op jit(solution)/shard_map/ppermute | solution.py:467
  61.2 14.0 %shard_map.163 = (f32[432,128]{1,0:T(8,128)S(1)}, bf16[192,1152]{1,0:T(8,128)(2,1)S(1)}, bf16[192,1152]{1,0:T(8,128)(2,1)S(1)}) custom-call(f32[624,128]{1,0:T(8,128)S(1)} %copy-done.3, f32[624,128]{1,0:T(8,128)S(1)} %collective-permute-done.m1, f32[624,128]{1,0:T(8,128)S(1)} %collective-permute-done.1.m2, f32[624,128]{1,0:T(8,128)S(1)} %collective-permute-done.2.m3, ...), custom_call_target="tpu_custom_call" | custom-call | bytes 39000000 | tf_op jit(solution)/shard_map/pallas_call | solution.py:518
  75.3 2.6 %shard_map.164 = (f32[432,128]{1,0:T(8,128)S(1)}, f32[432,128]{1,0:T(8,128)S(1)}, f32[432,128]{1,0:T(8,128)S(1)}) custom-call(bf16[192,1152]{1,0:T(8,128)(2,1)S(1)} %get-tuple-element.59.top.behind, bf16[192,1152]{1,0:T(8,128)(2,1)S(1)} %get-tuple-element.60.rest, bf16[1152,1152]{1,0:T(8,128)(2,1)S(1)} %get-tuple-element.53.bh, ...), custom_call_target="tpu_custom_call" | custom-call | bytes 9000000 | tf_op jit(solution)/shard_map/pallas_call | solution.py:528
  77.8 2.6 %collective-permute-start.14 = (f32[432,128]{1,0:T(8,128)S(1)}, f32[432,128]{1,0:T(8,128)S(1)}, u32[]{:S(2)}, u32[]{:S(2)}) collective-permute-start(f32[432,128]{1,0:T(8,128)S(1)} %get-tuple-element.62), channel_id=1, source_target_pairs={{0,1},{1,2},{2,3},{3,0},{4,5},{5,6},{6,7},{7,4},{8,9},{9,10},{10,1... | collective-permute-start | bytes 663560 | tf_op jit(solution)/shard_map/ppermute | solution.py:467
  80.4 1.0 %collective-permute-start.15 = (f32[432,128]{1,0:T(8,128)S(1)}, f32[432,128]{1,0:T(8,128)S(1)}, u32[]{:S(2)}, u32[]{:S(2)}) collective-permute-start(f32[432,128]{1,0:T(8,128)S(1)} %get-tuple-element.63), channel_id=1, source_target_pairs={{0,2},{1,3},{2,0},{3,1},{4,6},{5,7},{6,4},{7,5},{8,10},{9,11},{10,... | collective-permute-start | bytes 663560 | tf_op jit(solution)/shard_map/ppermute | solution.py:467
  81.4 6.5 %collective-permute-start.17 = (f32[4,896]{1,0:T(4,128)S(1)}, f32[4,896]{1,0:T(4,128)S(1)}, u32[]{:S(2)}, u32[]{:S(2)}) collective-permute-start(f32[4,896]{1,0:T(4,128)S(1)} %get-tuple-element.58.after), channel_id=1, source_target_pairs={{4,8},{8,4},{12,16},{16,12},{20,24},{24,20},{28,32},{32,28},{36,40... | collective-permute-start | bytes 43016 | tf_op jit(solution)/shard_map/ppermute | solution.py:470
  87.9 2.6 %collective-permute-done.17.x0 = f32[4,896]{1,0:T(4,128)S(1)} collective-permute-done((f32[4,896]{1,0:T(4,128)S(1)}, f32[4,896]{1,0:T(4,128)S(1)}, u32[]{:S(2)}, u32[]{:S(2)}) %collective-permute-start.17) | collective-permute-done | bytes 14368 | tf_op jit(solution)/shard_map/ppermute | solution.py:470
  90.5 0.6 shard_map.166
  91.1 2.7 %collective-permute-start.19 = (f32[40,4]{1,0:T(8,128)S(1)}, f32[40,4]{1,0:T(8,128)S(1)}, u32[]{:S(2)}, u32[]{:S(2)}) collective-permute-start(f32[40,4]{1,0:T(8,128)S(1)} %get-tuple-element.72), channel_id=1, source_target_pairs={{0,3},{1,0},{2,1},{3,2},{4,7},{5,4},{6,5},{7,6},{8,11},{9,8},{10,9... | collective-permute-start | bytes 1928 | tf_op jit(solution)/shard_map/ppermute | solution.py:467
  93.9 1.0 collective-permute-start.20
  94.9 1.4 %collective-permute-done.19.air_east = f32[40,4]{1,0:T(8,128)S(1)} collective-permute-done((f32[40,4]{1,0:T(8,128)S(1)}, f32[40,4]{1,0:T(8,128)S(1)}, u32[]{:S(2)}, u32[]{:S(2)}) %collective-permute-start.19) | collective-permute-done | bytes 672 | tf_op jit(solution)/shard_map/ppermute | solution.py:467
  96.2 2.0 %shard_map.167 = f32[4,32,896]{2,1,0:T(8,128)} custom-call(f32[4,32,896]{2,1,0:T(8,128)S(1)} %copy-done, s32[32,896]{1,0:T(8,128)S(1)} %copy-done.1, f32[32,896]{1,0:T(8,128)S(1)} %get-tuple-element.65.heat, f32[32,896]{1,0:T(8,128)S(1)} %get-tuple-element.66.speed, f32[384,128]{1,0:T(8,128)S(1)} %get-tuple-element.67.before, ...), custom_call_target="tpu_custom_call" | custom-call | bytes 9000000 | tf_op jit(solution)/shard_map/pallas_call | solution.py:535
  98.3 1.8 %shard_map.165 = f32[32,24,288]{2,1,0:T(8,128)} custom-call(s32[2]{0:T(128)S(1)} %copy-done.11, f32[432,128]{1,0:T(8,128)S(1)} %get-tuple-element.61.w0, f32[432,128]{1,0:T(8,128)S(1)} %collective-permute-done.14.w1, f32[432,128]{1,0:T(8,128)S(1)} %collective-permute-done.15.w2, f32[432,128]{1,0:T(8,128)S(1)} %collective-permute-done.16.w3), custom_call_target="tpu_custom_call" | custom-call | bytes 6000000 | tf_op jit(solution)/shard_map/pallas_call | solution.py:541
  (44 shorter events, 0.2 us)
Async XLA Ops:
  1.3 16.6 %copy-start.4 = (f32[36,1152]{1,0:T(8,128)S(1)}, f32[36,1152]{1,0:T(8,128)}, u32[]{:S(2)}) copy-start(f32[36,1152]{1,0:T(8,128)} %constant.50.clone.with_sin) | copy-start | bytes 497668
  1.3 16.6 %copy-start.5 = (f32[36,1152]{1,0:T(8,128)S(1)}, f32[36,1152]{1,0:T(8,128)}, u32[]{:S(2)}) copy-start(f32[36,1152]{1,0:T(8,128)} %constant.49.clone.with_cos) | copy-start | bytes 497668
  1.3 16.6 %copy-start.6 = (f32[32,1152]{1,0:T(8,128)S(1)}, f32[32,1152]{1,0:T(8,128)}, u32[]{:S(2)}) copy-start(f32[32,1152]{1,0:T(8,128)} %constant.52.clone.sine) | copy-start | bytes 442372
  1.3 16.6 %copy-start.7 = (f32[32,1152]{1,0:T(8,128)S(1)}, f32[32,1152]{1,0:T(8,128)}, u32[]{:S(2)}) copy-start(f32[32,1152]{1,0:T(8,128)} %constant.51.clone.cosine) | copy-start | bytes 442372
  1.3 18.1 %copy-start.15 = (s32[192]{0:T(256)S(1)}, s32[192]{0:T(256)}, u32[]{:S(2)}) copy-start(s32[192]{0:T(256)} %param.22) | copy-start | bytes 2308
  1.3 21.2 %copy-start = (f32[4,32,896]{2,1,0:T(8,128)S(1)}, f32[4,32,896]{2,1,0:T(8,128)}, u32[]{:S(2)}) copy-start(f32[4,32,896]{2,1,0:T(8,128)} %t.3) | copy-start | bytes 1376260
  1.3 21.2 %copy-start.1 = (s32[32,896]{1,0:T(8,128)S(1)}, s32[32,896]{1,0:T(8,128)}, u32[]{:S(2)}) copy-start(s32[32,896]{1,0:T(8,128)} %mask.3) | copy-start | bytes 344068
  1.3 21.2 %copy-start.11 = (s32[2]{0:T(128)S(1)}, s32[2]{0:T(128)}, u32[]{:S(2)}) copy-start(s32[2]{0:T(128)} %pad_add_fusion.place) | copy-start | bytes 28
  6.4 32.9 %copy-start.16 = (f32[672,128]{1,0:T(8,128)S(1)}, f32[672,128]{1,0:T(8,128)}, u32[]{:S(2)}) copy-start(f32[672,128]{1,0:T(8,128)} %get-tuple-element.45) | copy-start | bytes 1032196
  6.4 34.8 %copy-start.12 = (f32[1152]{0:T(1024)S(1)}, f32[1152]{0:T(1024)}, u32[]{:S(2)}) copy-start(f32[1152]{0:T(1024)} %constant.66) | copy-start | bytes 13828
  6.4 34.8 %copy-start.13 = (f32[1152]{0:T(1024)S(1)}, f32[1152]{0:T(1024)}, u32[]{:S(2)}) copy-start(f32[1152]{0:T(1024)} %constant.65) | copy-start | bytes 13828
  6.5 34.8 %copy-start.14 = (pred[1152]{0:T(1024)(128)(4,1)S(1)}, pred[1152]{0:T(1024)(128)(4,1)}, u32[]{:S(2)}) copy-start(pred[1152]{0:T(1024)(128)(4,1)} %constant.63) | copy-start | bytes 3460
  6.5 15.0 %collective-permute-start.6 = (f32[384,128]{1,0:T(8,128)}, f32[384,128]{1,0:T(8,128)S(1)}, u32[]{:S(2)}, u32[]{:S(2)}) collective-permute-start(f32[384,128]{1,0:T(8,128)} %get-tuple-element.46), channel_id=1, source_target_pairs={{4,8},{8,4},{12,16},{16,12},{20,24},{24,20},{28,32},{32,28},{36,40... | collective-permute-start | bytes 589832 | tf_op jit(solution)/shard_map/ppermute | solution.py:470
  16.7 5.8 %collective-permute-start.7 = (f32[384,128]{1,0:T(8,128)}, f32[384,128]{1,0:T(8,128)S(1)}, u32[]{:S(2)}, u32[]{:S(2)}) collective-permute-start(f32[384,128]{1,0:T(8,128)} %get-tuple-element.47), channel_id=1, source_target_pairs={{0,4},{4,0},{8,12},{12,8},{16,20},{20,16},{24,28},{28,24},{32,36},... | collective-permute-start | bytes 589832 | tf_op jit(solution)/shard_map/ppermute | solution.py:471
  16.8 22.5 %collective-permute-start = (f32[624,128]{1,0:T(8,128)}, f32[624,128]{1,0:T(8,128)S(1)}, u32[]{:S(2)}, u32[]{:S(2)}) collective-permute-start(f32[624,128]{1,0:T(8,128)} %get-tuple-element.39), channel_id=1, source_target_pairs={{0,3},{1,0},{2,1},{3,2},{4,7},{5,4},{6,5},{7,6},{8,11},{9,8},{10,9... | collective-permute-start | bytes 958472 | tf_op jit(solution)/shard_map/ppermute | solution.py:467
  22.5 0.9 copy-start.10
  24.2 4.1 %collective-permute-start.9 = (f32[144,128]{1,0:T(8,128)S(1)}, f32[144,128]{1,0:T(8,128)S(1)}, u32[]{:S(2)}, u32[]{:S(2)}) collective-permute-start(f32[144,128]{1,0:T(8,128)S(1)} %get-tuple-element.51), channel_id=1, source_target_pairs={{0,2},{1,3},{2,0},{3,1},{4,6},{5,7},{6,4},{7,5},{8,10},{9,11},{10,... | collective-permute-start | bytes 221192 | tf_op jit(solution)/shard_map/ppermute | solution.py:467
  24.6 7.7 %collective-permute-start.8 = (f32[184,128]{1,0:T(8,128)S(1)}, f32[184,128]{1,0:T(8,128)S(1)}, u32[]{:S(2)}, u32[]{:S(2)}) collective-permute-start(f32[184,128]{1,0:T(8,128)S(1)} %get-tuple-element.50), channel_id=1, source_target_pairs={{0,3},{1,0},{2,1},{3,2},{4,7},{5,4},{6,5},{7,6},{8,11},{9,8},{10,9... | collective-permute-start | bytes 282632 | tf_op jit(solution)/shard_map/ppermute | solution.py:467
  26.8 8.7 %collective-permute-start.13 = (f32[216,128]{1,0:T(8,128)S(1)}, f32[216,128]{1,0:T(8,128)S(1)}, u32[]{:S(2)}, u32[]{:S(2)}) collective-permute-start(f32[216,128]{1,0:T(8,128)S(1)} %get-tuple-element.55.w0), channel_id=1, source_target_pairs={{0,1},{1,2},{2,3},{3,0},{4,5},{5,6},{6,7},{7,4},{8,9},{9,10},{10,1... | collective-permute-start | bytes 331784 | tf_op jit(solution)/shard_map/ppermute | solution.py:467
  27.8 10.4 %collective-permute-start.12 = (f32[216,128]{1,0:T(8,128)S(1)}, f32[216,128]{1,0:T(8,128)S(1)}, u32[]{:S(2)}, u32[]{:S(2)}) collective-permute-start(f32[216,128]{1,0:T(8,128)S(1)} %get-tuple-element.55.w0), channel_id=1, source_target_pairs={{0,2},{1,3},{2,0},{3,1},{4,6},{5,7},{6,4},{7,5},{8,10},{9,11},{10,... | collective-permute-start | bytes 331784 | tf_op jit(solution)/shard_map/ppermute | solution.py:467
  28.2 10.0 %collective-permute-start.11 = (f32[216,128]{1,0:T(8,128)S(1)}, f32[216,128]{1,0:T(8,128)S(1)}, u32[]{:S(2)}, u32[]{:S(2)}) collective-permute-start(f32[216,128]{1,0:T(8,128)S(1)} %get-tuple-element.55.w0), channel_id=1, source_target_pairs={{0,3},{1,0},{2,1},{3,2},{4,7},{5,4},{6,5},{7,6},{8,11},{9,8},{10,9... | collective-permute-start | bytes 331784 | tf_op jit(solution)/shard_map/ppermute | solution.py:467
  32.3 2.7 %collective-permute-start.10 = (f32[184,128]{1,0:T(8,128)S(1)}, f32[184,128]{1,0:T(8,128)S(1)}, u32[]{:S(2)}, u32[]{:S(2)}) collective-permute-start(f32[184,128]{1,0:T(8,128)S(1)} %get-tuple-element.52), channel_id=1, source_target_pairs={{0,1},{1,2},{2,3},{3,0},{4,5},{5,6},{6,7},{7,4},{8,9},{9,10},{10,1... | collective-permute-start | bytes 282632 | tf_op jit(solution)/shard_map/ppermute | solution.py:467
  35.0 16.6 %collective-permute-start.1 = (f32[624,128]{1,0:T(8,128)}, f32[624,128]{1,0:T(8,128)S(1)}, u32[]{:S(2)}, u32[]{:S(2)}) collective-permute-start(f32[624,128]{1,0:T(8,128)} %get-tuple-element.40), channel_id=1, source_target_pairs={{0,2},{1,3},{2,0},{3,1},{4,6},{5,7},{6,4},{7,5},{8,10},{9,11},{10,... | collective-permute-start | bytes 958472 | tf_op jit(solution)/shard_map/ppermute | solution.py:467
  35.5 16.1 %collective-permute-start.2 = (f32[624,128]{1,0:T(8,128)}, f32[624,128]{1,0:T(8,128)S(1)}, u32[]{:S(2)}, u32[]{:S(2)}) collective-permute-start(f32[624,128]{1,0:T(8,128)} %get-tuple-element.41), channel_id=1, source_target_pairs={{0,1},{1,2},{2,3},{3,0},{4,5},{5,6},{6,7},{7,4},{8,9},{9,10},{10,1... | collective-permute-start | bytes 958472 | tf_op jit(solution)/shard_map/ppermute | solution.py:467
  38.2 15.7 %collective-permute-start.3 = (f32[672,128]{1,0:T(8,128)}, f32[672,128]{1,0:T(8,128)S(1)}, u32[]{:S(2)}, u32[]{:S(2)}) collective-permute-start(f32[672,128]{1,0:T(8,128)} %get-tuple-element.43), channel_id=1, source_target_pairs={{0,3},{1,0},{2,1},{3,2},{4,7},{5,4},{6,5},{7,6},{8,11},{9,8},{10,9... | collective-permute-start | bytes 1032200 | tf_op jit(solution)/shard_map/ppermute | solution.py:467
  38.3 18.7 %collective-permute-start.4 = (f32[672,128]{1,0:T(8,128)}, f32[672,128]{1,0:T(8,128)S(1)}, u32[]{:S(2)}, u32[]{:S(2)}) collective-permute-start(f32[672,128]{1,0:T(8,128)} %get-tuple-element.44), channel_id=1, source_target_pairs={{0,2},{1,3},{2,0},{3,1},{4,6},{5,7},{6,4},{7,5},{8,10},{9,11},{10,... | collective-permute-start | bytes 1032200 | tf_op jit(solution)/shard_map/ppermute | solution.py:467
  39.3 21.9 %collective-permute-start.5 = (f32[672,128]{1,0:T(8,128)S(1)}, f32[672,128]{1,0:T(8,128)S(1)}, u32[]{:S(2)}, u32[]{:S(2)}) collective-permute-start(f32[672,128]{1,0:T(8,128)S(1)} %copy-done.16), channel_id=1, source_target_pairs={{0,1},{1,2},{2,3},{3,0},{4,5},{5,6},{6,7},{7,4},{8,9},{9,10},{10,1... | collective-permute-start | bytes 1032200 | tf_op jit(solution)/shard_map/ppermute | solution.py:467
  41.4 4.6 %copy-start.8 = (s32[32,896]{1,0:T(8,128)S(1)}, s32[32,896]{1,0:T(8,128)}, u32[]{:S(2)}) copy-start(s32[32,896]{1,0:T(8,128)} %rows.1) | copy-start | bytes 344068
  41.4 4.6 %copy-start.9 = (s32[32,896]{1,0:T(8,128)S(1)}, s32[32,896]{1,0:T(8,128)}, u32[]{:S(2)}) copy-start(s32[32,896]{1,0:T(8,128)} %cols.1) | copy-start | bytes 344068
  41.4 19.8 %copy-start.2 = (f32[672,128]{1,0:T(8,128)S(1)}, f32[672,128]{1,0:T(8,128)}, u32[]{:S(2)}) copy-start(f32[672,128]{1,0:T(8,128)} %get-tuple-element.42.n0) | copy-start | bytes 1032196
  41.4 19.8 %copy-start.3 = (f32[624,128]{1,0:T(8,128)S(1)}, f32[624,128]{1,0:T(8,128)}, u32[]{:S(2)}) copy-start(f32[624,128]{1,0:T(8,128)} %get-tuple-element.38.m0) | copy-start | bytes 958468
  77.8 20.4 %collective-permute-start.14 = (f32[432,128]{1,0:T(8,128)S(1)}, f32[432,128]{1,0:T(8,128)S(1)}, u32[]{:S(2)}, u32[]{:S(2)}) collective-permute-start(f32[432,128]{1,0:T(8,128)S(1)} %get-tuple-element.62), channel_id=1, source_target_pairs={{0,1},{1,2},{2,3},{3,0},{4,5},{5,6},{6,7},{7,4},{8,9},{9,10},{10,1... | collective-permute-start | bytes 663560 | tf_op jit(solution)/shard_map/ppermute | solution.py:467
  80.4 17.9 %collective-permute-start.16 = (f32[432,128]{1,0:T(8,128)S(1)}, f32[432,128]{1,0:T(8,128)S(1)}, u32[]{:S(2)}, u32[]{:S(2)}) collective-permute-start(f32[432,128]{1,0:T(8,128)S(1)} %get-tuple-element.64), channel_id=1, source_target_pairs={{0,3},{1,0},{2,1},{3,2},{4,7},{5,4},{6,5},{7,6},{8,11},{9,8},{10,9... | collective-permute-start | bytes 663560 | tf_op jit(solution)/shard_map/ppermute | solution.py:467
  80.4 17.9 %collective-permute-start.15 = (f32[432,128]{1,0:T(8,128)S(1)}, f32[432,128]{1,0:T(8,128)S(1)}, u32[]{:S(2)}, u32[]{:S(2)}) collective-permute-start(f32[432,128]{1,0:T(8,128)S(1)} %get-tuple-element.63), channel_id=1, source_target_pairs={{0,2},{1,3},{2,0},{3,1},{4,6},{5,7},{6,4},{7,5},{8,10},{9,11},{10,... | collective-permute-start | bytes 663560 | tf_op jit(solution)/shard_map/ppermute | solution.py:467
  81.4 6.5 %collective-permute-start.18 = (f32[4,896]{1,0:T(4,128)S(1)}, f32[4,896]{1,0:T(4,128)S(1)}, u32[]{:S(2)}, u32[]{:S(2)}) collective-permute-start(f32[4,896]{1,0:T(4,128)S(1)} %get-tuple-element.69), channel_id=1, source_target_pairs={{0,4},{4,0},{8,12},{12,8},{16,20},{20,16},{24,28},{28,24},{32,36},... | collective-permute-start | bytes 43016 | tf_op jit(solution)/shard_map/ppermute | solution.py:471
  81.4 9.1 %collective-permute-start.17 = (f32[4,896]{1,0:T(4,128)S(1)}, f32[4,896]{1,0:T(4,128)S(1)}, u32[]{:S(2)}, u32[]{:S(2)}) collective-permute-start(f32[4,896]{1,0:T(4,128)S(1)} %get-tuple-element.58.after), channel_id=1, source_target_pairs={{4,8},{8,4},{12,16},{16,12},{20,24},{24,20},{28,32},{32,28},{36,40... | collective-permute-start | bytes 43016 | tf_op jit(solution)/shard_map/ppermute | solution.py:470
  91.1 5.1 %collective-permute-start.19 = (f32[40,4]{1,0:T(8,128)S(1)}, f32[40,4]{1,0:T(8,128)S(1)}, u32[]{:S(2)}, u32[]{:S(2)}) collective-permute-start(f32[40,4]{1,0:T(8,128)S(1)} %get-tuple-element.72), channel_id=1, source_target_pairs={{0,3},{1,0},{2,1},{3,2},{4,7},{5,4},{6,5},{7,6},{8,11},{9,8},{10,9... | collective-permute-start | bytes 1928 | tf_op jit(solution)/shard_map/ppermute | solution.py:467
  93.9 2.4 %collective-permute-start.20 = (f32[40,4]{1,0:T(8,128)S(1)}, f32[40,4]{1,0:T(8,128)S(1)}, u32[]{:S(2)}, u32[]{:S(2)}) collective-permute-start(f32[40,4]{1,0:T(8,128)S(1)} %get-tuple-element.73), channel_id=1, source_target_pairs={{0,1},{1,2},{2,3},{3,0},{4,5},{5,6},{6,7},{7,4},{8,9},{9,10},{10,1... | collective-permute-start | bytes 1928 | tf_op jit(solution)/shard_map/ppermute | solution.py:467

commit v3 on v2

--- a/solution.py
+++ b/solution.py
@@ -27,12 +27,18 @@
 vertical_mix = 0.2
 
 
-def call(kernel, out_shape, smem=0, n_in=0, n_any=0, scratch=(), cost=None, mib=24):
+def call(kernel, out_shape, smem=0, n_in=0, n_any=0, out_any=0, n_out=0, scratch=(), cost=None, mib=24, aliases=None):
     specs = [pl.BlockSpec(memory_space=pltpu.SMEM)] * smem + [pl.BlockSpec(memory_space=pltpu.VMEM)] * n_in
     specs += [pl.BlockSpec(memory_space=pl.ANY)] * n_any
+    outs = {}
+    if out_any:
+        spaces = [pl.ANY] * out_any + [pltpu.VMEM] * (n_out - out_any)
+        outs["out_specs"] = [pl.BlockSpec(memory_space=space) for space in spaces]
     return pl.pallas_call(
         kernel,
         out_shape=out_shape,
+        **outs,
+        input_output_aliases=aliases or {},
         in_specs=specs,
         scratch_shapes=scratch,
         cost_estimate=cost,
@@ -52,6 +58,7 @@
 FIRST, SECOND = FT + 192, 2 * FT - 192
 STRIP_AT, RIM_WIRE, WINDOW = 144, 184, 216
 TILES = OCOLS // 128
+THIRD, TABLE = 40, 80
 
 
 def wire_places(f, first, second):
@@ -68,7 +75,11 @@
     second[...] = jnp.where(odd, b[...], a[...])
 
 
-def pack_kernel(place, q_in, u_in, v_in, t_in, mask_in, a0, a1, a2, a3, b0, b1, b2, b3, x0, x1, mid, q, u, v, t, mask, up, down, sems):
+def pack_kernel(
+    q_in, u_in, v_in, t_in, mask_in, a0, a1, a2, a3, b0, b1, b2, b3, x0, x1, mid,
+    q, u, v, t, mask, up, down, firsts, seconds, sems, out_sems,
+):
+    place = (lax.axis_index("lon"), lax.axis_index("lat"))
     copies = [
         [
             pltpu.make_async_copy(source.at[pl.ds(LB * i, LB)], target.at[pl.ds(LB * i, LB)], sems.at[f, i])
@@ -80,12 +91,19 @@
     for group in copies:
         for copy in group:
             copy.start()
-    first_wires, second_wires = (a0, a1, a2, a3), (b0, b1, b2, b3)
+    sends = []
+    for s, (a, b) in enumerate(zip((a0, a1, a2, a3), (b0, b1, b2, b3))):
+        sends.append(
+            (
+                pltpu.make_async_copy(firsts.at[s], a, out_sems.at[0, s]),
+                pltpu.make_async_copy(seconds.at[s], b, out_sems.at[1, s]),
+            )
+        )
     for f, field in enumerate((q, u, v)):
         for copy in copies[f]:
             copy.wait()
         for s in range(LONS):
-            places = wire_places(f, first_wires[s], second_wires[s])
+            places = wire_places(f, firsts.at[s], seconds.at[s])
             first = (place[0] + s) % LONS * LB
             for l in range(LB):
                 for c in range(2):
@@ -95,6 +113,8 @@
                 wire[pl.ds(base + l, 6, stride=8), :] = jnp.concatenate(
                     [field[first + l, 6 * i : 6 * i + 6, 256:288] for i in range(4)], axis=1
                 )
+            if f > 0:
+                sends[s][f - 1].start()
     for copy in copies[3]:
         copy.wait()
     for s in range(LONS):
@@ -125,14 +145,20 @@
     for f, field in enumerate((q, u, v)):
         mid[f, :, :] = field[LEV - 1, :, :]
     cross(place, up, down, x0, x1)
-
-
-def join_kernel(place, x0, x1, mid, t, mask, w0, w1, w2, w3, circle, before, after, win):
+    for pair in sends:
+        for copy in pair:
+            copy.wait()
+
+
+def join_kernel(place, x0, x1, t, mask, mid_in, w0, w1, w2, w3, circle, before, after, win, mid, sem):
+    copy = pltpu.make_async_copy(mid_in, mid, sem)
+    copy.start()
     cross(place, x1, x0, before, after)
     wires = (w0, w1, w2, w3)
     for s, wire in enumerate(wires):
         wire[0:72, :] = before[s * 72 : s * 72 + 72, :]
         wire[72:144, :] = after[s * 72 : s * 72 + 72, :]
+    copy.wait()
     for f, (at, n) in enumerate(((0, 3), (3, 2), (5, 2))):
         win[...] = jnp.zeros((WIN, 384), f32)
         win[4 : 4 + ROWS, 0:COLS] = mid[f, :, :]
@@ -158,15 +184,28 @@
             wire[STRIP_AT + row : STRIP_AT + row + 2, :] = jnp.concatenate(far + [jnp.zeros((2, pad), f32)], axis=1)
 
 
-def unpack_kernel(place, w0, w1, w2, w3, out):
-    for s, wire in enumerate((w0, w1, w2, w3)):
-        first = (place[0] + LONS - s) % LONS * LB
+def unpack_kernel(place, shifts, wires, out, block, sem):
+    copies = []
+    for n, (s, wire) in enumerate(zip(shifts, wires)):
         for l in range(LB):
             for c in range(2):
-                out[first + l, :, c * 128 : c * 128 + 128] = wire[pl.ds(c * 192 + l, ROWS, stride=8), :]
+                block[n, l, :, c * 128 : c * 128 + 128] = wire[pl.ds(c * 192 + l, ROWS, stride=8), :]
             rem = wire[pl.ds(384 + l, 6, stride=8), :]
             for i in range(4):
-                out[first + l, 6 * i : 6 * i + 6, 256:288] = rem[:, 32 * i : 32 * i + 32]
+                block[n, l, 6 * i : 6 * i + 6, 256:288] = rem[:, 32 * i : 32 * i + 32]
+        first = (place[0] + LONS - s) % LONS * LB
+        copies.append(pltpu.make_async_copy(block.at[n], out.at[pl.ds(first, LB)], sem.at[n]))
+        copies[-1].start()
+    for copy in copies:
+        copy.wait()
+
+
+def unpack_first(place, w0, w2, out, block, sem):
+    unpack_kernel(place, (0, 2), (w0, w2), out, block, sem)
+
+
+def unpack_second(place, w1, w3, half, out, block, sem):
+    unpack_kernel(place, (1, 3), (w1, w3), out, block, sem)
 
 
 def wave_tables():
@@ -233,9 +272,15 @@
         q = advance(q, pltpu.roll(q, WIN - 1, 0), pltpu.roll(q, 1, 0), u, v)
         q = product(product(q, bh, bl) * damp[...], bh, bl, back=True)
     for out, field in ((heat, q), (speed, wind)):
-        lane = lax.broadcasted_iota(jnp.int32, (WIN, 128), 1)
-        out[:, 0:256] = field[:, 0:256]
-        out[:, 256:384] = jnp.where(lane < 64, field[:, 256:384], field[:, NLON - 128 : NLON])
+        out[0:WIN, :] = field[:, 0:128]
+        out[WIN : 2 * WIN, :] = field[:, 128:256]
+        ends = jnp.concatenate(
+            [field[:, 256 : COLS + 1], field[:, NLON - 1 : NLON], jnp.zeros((WIN, THIRD - 34), f32)], axis=1
+        )
+        out[2 * WIN : 2 * WIN + 9, :] = jnp.concatenate(
+            [ends[3 + 9 * i : 12 + 9 * i, :] for i in range(3)] + [jnp.zeros((9, 128 - 3 * THIRD), f32)], axis=1
+        )
+        out[2 * WIN + 9 : TABLE, :] = jnp.zeros((TABLE - 2 * WIN - 9, 128), f32)
 
 
 def bulk_kernel(m0, m1, m2, m3, n0, n1, n2, n3, h0, h1, h2, h3, damp, bh, bl, after, far, top_out, rest_out, qs, us, vs, xs):
@@ -329,10 +374,14 @@
         out[384 + g * 8 : 392 + g * 8, :] = jnp.concatenate(rems, axis=1)
 
 
-def finish_kernel(top, rest, bh, bl, o0, o1, o3):
-    for out, p in ((o3, 3), (o1, 1), (o0, 0)):
+def finish_kernel(top, rest, bh, bl, o1, o3):
+    for out, p in ((o3, 3), (o1, 1)):
         rows = slice(p * COLS, p * COLS + COLS)
         write_piece(out, project(top[...], rest[...], bh[rows, :], bl[rows, :]))
+
+
+def own_kernel(top, rest, bh, bl, behind, out):
+    write_piece(out, project(top[...], rest[...], bh[0:COLS, :], bl[0:COLS, :]))
 
 
 def pick_kernel(place, rows, cols, heat, speed, air_heat, air_speed, x0, x1, up, down):
@@ -342,18 +391,19 @@
             row = rows[pl.ds(start, 8), c * 128 : c * 128 + 128] - place[1] * ROWS + 4
             col = cols[pl.ds(start, 8), c * 128 : c * 128 + 128] - place[0] * COLS
             col = jnp.where(col < 0, col + NLON, col)
-            col = jnp.where(col > COLS, col - (NLON - 384), col)
-            key = row * 4 + (col >> 7)
-            lane = col & 127
+            part = jnp.where(row >= 21, 2, jnp.where(row >= 12, 1, 0))
+            end = jnp.where(col > COLS, 33, col - 256)
+            last = col >= 256
+            key = jnp.where(last, 2 * WIN - 3 + row - 9 * part, row + WIN * (col >> 7))
+            lane = jnp.where(last, end + THIRD * part, col & 127)
             got_heat = jnp.zeros((8, 128), f32)
             got_speed = jnp.zeros((8, 128), f32)
-            for w in range(3, 29):
-                for b in range(3):
-                    mine = key == w * 4 + b
-                    line_heat = jnp.broadcast_to(heat[w : w + 1, b * 128 : b * 128 + 128], (8, 128))
-                    line_speed = jnp.broadcast_to(speed[w : w + 1, b * 128 : b * 128 + 128], (8, 128))
-                    got_heat = jnp.where(mine, jnp.take_along_axis(line_heat, lane, axis=1), got_heat)
-                    got_speed = jnp.where(mine, jnp.take_along_axis(line_speed, lane, axis=1), got_speed)
+            for n in (*range(3, 29), *range(WIN + 3, WIN + 29), *range(2 * WIN, 2 * WIN + 9)):
+                mine = key == n
+                line_heat = jnp.broadcast_to(heat[n : n + 1, :], (8, 128))
+                line_speed = jnp.broadcast_to(speed[n : n + 1, :], (8, 128))
+                got_heat = jnp.where(mine, jnp.take_along_axis(line_heat, lane, axis=1), got_heat)
+                got_speed = jnp.where(mine, jnp.take_along_axis(line_speed, lane, axis=1), got_speed)
             air_heat[pl.ds(start, 8), c * 128 : c * 128 + 128] = got_heat
             air_speed[pl.ds(start, 8), c * 128 : c * 128 + 128] = got_speed
         return carry
@@ -473,19 +523,23 @@
     packed = call(
         pack_kernel,
         [sds(FIRST, 128)] * 4 + [sds(SECOND, 128)] * 4 + [sds(LAT_WIRE, 128)] * 2 + [sds(3, ROWS, COLS)],
-        smem=1,
         n_any=5,
+        out_any=8,
+        n_out=11,
         scratch=[pltpu.VMEM((LEV, ROWS, COLS), f32)] * 3
         + [
             pltpu.VMEM((OLEV, OROWS, OCOLS), f32),
             pltpu.VMEM((OROWS, OCOLS), jnp.int32),
             pltpu.VMEM((LAT_WIRE, 128), f32),
             pltpu.VMEM((LAT_WIRE, 128), f32),
+            pltpu.VMEM((LONS, FIRST, 128), f32),
+            pltpu.VMEM((LONS, SECOND, 128), f32),
             pltpu.SemaphoreType.DMA((4, LONS)),
+            pltpu.SemaphoreType.DMA((2, LONS)),
         ],
         cost=cost(5),
         mib=60,
-    )(place, tracer, wind_u, wind_v, ocean_temp, land_mask)
+    )(tracer, wind_u, wind_v, ocean_temp, land_mask)
     mains, winds, mid = packed[:4], packed[4:8], packed[10]
     pieces = [mains[0]] + [along(mains[s], s) for s in (3, 2, 1)]
     near0, near1 = across(packed[8], packed[9])
@@ -498,16 +552,17 @@
         + [sds(WINDOW, 128)]
         + [sds(LAT_WIRE, 128)] * 2,
         smem=1,
-        n_in=5,
-        scratch=[pltpu.VMEM((WIN, 384), f32)],
+        n_in=4,
+        n_any=1,
+        scratch=[pltpu.VMEM((WIN, 384), f32), pltpu.VMEM((3, ROWS, COLS), f32), pltpu.SemaphoreType.DMA],
         cost=cost(2),
-    )(place, near0, near1, mid, ocean_temp, land_mask)
+    )(place, near0, near1, ocean_temp, land_mask, mid)
     before, after = joined[5:]
     windows = [joined[4]] + [along(joined[4], s) for s in (3, 2, 1)]
     rims = [joined[0]] + [along(joined[s], s) for s in (3, 2, 1)]
     blows = [winds[0]] + [along(winds[s], s) for s in (3, 2, 1)]
 
-    heat, speed = call(bottom_kernel, [sds(WIN, 384)] * 2, n_in=7, cost=cost(8))(*windows, damp, *basis)
+    heat, speed = call(bottom_kernel, [sds(TABLE, 128)] * 2, n_in=7, cost=cost(8))(*windows, damp, *basis)
     air_heat, air_speed, air_up, air_down = call(
         pick_kernel, [sds(OROWS, OCOLS)] * 2 + [sds(4, OCOLS)] * 2, smem=1, n_in=4, cost=cost(7),
         scratch=[pltpu.VMEM((4, OCOLS), f32)] * 2,
@@ -525,7 +580,8 @@
         mib=36,
     )(*pieces, *blows, *rims, damp, *basis, air_up)
     far = along(far, 2)
-    own, one, three = call(finish_kernel, [sds(FT, 128)] * 3, n_in=4, cost=cost(3))(top, rest, *basis)
+    one, three = call(finish_kernel, [sds(FT, 128)] * 2, n_in=4, cost=cost(2))(top, rest, *basis)
+    own = call(own_kernel, sds(FT, 128), n_in=4, n_any=1, cost=cost(1))(top, rest, *basis, one)
     back = [own, along(one, 1), far, along(three, 3)]
 
     east, west, air_before, air_after = call(
@@ -538,7 +594,14 @@
         ocean_temp, land_mask, air_heat, air_speed, before, after, rims[1], rims[3],
         air_before, air_after, air_east, air_west,
     )
-    tracer_out = call(unpack_kernel, sds(LEV, ROWS, COLS), smem=1, n_in=4, cost=cost(2))(place, *back)
+    scratch = [pltpu.VMEM((2, LB, ROWS, COLS), f32), pltpu.SemaphoreType.DMA((2,))]
+    half = call(
+        unpack_first, [sds(LEV, ROWS, COLS)], smem=1, n_in=2, out_any=1, n_out=1, scratch=scratch, cost=cost(1)
+    )(place, back[0], back[2])[0]
+    tracer_out = call(
+        unpack_second, [sds(LEV, ROWS, COLS)], smem=1, n_in=2, n_any=1, out_any=1, n_out=1, scratch=scratch,
+        cost=cost(1), aliases={3: 0},
+    )(place, back[1], back[3], half)[0]
     return tracer_out, ocean_out
 
 

time: 101 us -> 99 us (0.980)
  starting transfers between devices: 38.1 us -> 37 us
    pallas_call x3 -> x5, Pallas kernels: 8.88 us -> 10.4 us  [the longest x1 4.68 us: per_device(): call(bottom_kernel, [sds(TABLE, 128)] * 2, n_in=7, cost=cost(8))]
    pallas_call x1, Pallas kernels: 5.64 us -> 4.59 us  [per_device(): call(pick_kernel, [sds(OROWS, OCOLS)] * 2 + [sds(4, OCOLS)] * 2, smem=1,...]
    ppermute x17, starting transfers between devices: 21.3 us -> 20.3 us  [along(): return lax.ppermute(x, 'lon', [(i, (i + s) % LONS) for i in range(LONS)])]
  transfers between devices with their start and end apart: 21 -> 21, of which waited for: 9 -> 9; matrix products, arithmetic and copies ran while one was open for 0% -> 0% of each run, Pallas kernels for 15% -> 19%
where the time goes in v3:
time: 99 us; the launch traced here: 98.3 us
  Pallas kernels  38.4 us (39%)
  starting transfers between devices  37 us (37%)
  waiting for transfers between devices  20.3 us (21%)
  between operations  1.14 us (1%)
  local copies, waits for them, and re-layouts  0.99 us (1%)
    ppermute x17, starting transfers between devices, along(): return lax.ppermute(x, 'lon', [(i, (i + s) % LONS) for i in range(LONS)])  20.3 us
    ppermute x2, starting transfers between devices, across(): got = lax.ppermute(first, 'lat', swaps[0])  16.7 us
    ppermute x17, waiting for transfers between devices, along(): return lax.ppermute(x, 'lon', [(i, (i + s) % LONS) for i in range(LONS)])  14.9 us
    pallas_call x1, Pallas kernels, per_device(): call(bulk_kernel, [sds(FT, 128)] + [sds(ROWS * LB, NLON, dtype=bf16)] * 2...  14 us
    pallas_call x1, Pallas kernels, per_device(): call(bottom_kernel, [sds(TABLE, 128)] * 2, n_in=7, cost=cost(8))  4.68 us
    pallas_call x1, Pallas kernels, per_device(): call(pick_kernel, [sds(OROWS, OCOLS)] * 2 + [sds(4, OCOLS)] * 2, smem=1,...  4.59 us
    pallas_call x1, Pallas kernels, per_device(): call(pack_kernel, [sds(FIRST, 128)] * 4 + [sds(SECOND, 128)] * 4 + [sds(L...  4.39 us
    ppermute x2, waiting for transfers between devices, across(): got = lax.ppermute(first, 'lat', swaps[0])  4.36 us
  transfers between devices with their start and end apart: 21, of which 9 were waited for; matrix products, arithmetic and copies ran while one was open for 0% of the time, Pallas kernels for 19%

profile of v3, /device:TPU:3, one launch (start us, length us, event | category | flops | bytes accessed | tf_op | source)
XLA Modules:
  0.0 98.3 jit_solution(231433907331476470)
XLA Ops:
  0.6 0.0 copy-start.4
  0.6 0.0 copy-start.5
  0.7 0.0 copy-start.7
  0.7 4.4 %shard_map.158 = (f32[624,128]{1,0:T(8,128)}, f32[624,128]{1,0:T(8,128)}, f32[624,128]{1,0:T(8,128)}, f32[624,128]{1,0:T(8,128)}, f32[672,128]{1,0:T(8,128)}, /*...) custom-call(f32[32,24,288]{2,1,0:T(8,128)} %q_in.1, ...), custom_call_target="tpu_custom_call" | custom-call | bytes 15000000 | tf_op jit(solution)/shard_map/pallas_call | solution.py:523
  5.1 0.0 copy-start.11
  5.1 0.0 copy-start.12
  5.2 10.2 %collective-permute-start.6 = (f32[384,128]{1,0:T(8,128)}, f32[384,128]{1,0:T(8,128)S(1)}, u32[]{:S(2)}, u32[]{:S(2)}) collective-permute-start(f32[384,128]{1,0:T(8,128)} %get-tuple-element.45), channel_id=1, source_target_pairs={{4,8},{8,4},{12,16},{16,12},{20,24},{24,20},{28,32},{32,28},{36,40... | collective-permute-start | bytes 589832 | tf_op jit(solution)/shard_map/ppermute | solution.py:520
  15.4 0.1 collective-permute-start.7
  15.5 1.0 %collective-permute-start = (f32[624,128]{1,0:T(8,128)}, f32[624,128]{1,0:T(8,128)S(1)}, u32[]{:S(2)}, u32[]{:S(2)}) collective-permute-start(f32[624,128]{1,0:T(8,128)} %get-tuple-element.38), channel_id=1, source_target_pairs={{0,3},{1,0},{2,1},{3,2},{4,7},{5,4},{6,5},{7,6},{8,11},{9,8},{10,9... | collective-permute-start | bytes 958472 | tf_op jit(solution)/shard_map/ppermute | solution.py:517
  16.6 1.5 %shard_map.160 = (bf16[1152,1152]{1,0:T(8,128)(2,1)S(1)}, bf16[1152,1152]{1,0:T(8,128)(2,1)S(1)}) custom-call(f32[36,1152]{1,0:T(8,128)S(1)} %copy-done.5, f32[36,1152]{1,0:T(8,128)S(1)} %copy-done.4, f32[32,1152]{1,0:T(8,128)S(1)} %copy-done.7, f32[32,1152]{1,0:T(8,128)S(1)} %copy-done.6), custom_call_target="tpu_custom_call" | custom-call | bytes 9000000 | tf_op jit(solution)/shard_map/pallas_call | solution.py:547
  18.1 0.2 compare_reduce_fusion
  18.2 0.1 pad_add_fusion.place
  18.3 1.9 %collective-permute-done.6.x0 = f32[384,128]{1,0:T(8,128)S(1)} collective-permute-done((f32[384,128]{1,0:T(8,128)}, f32[384,128]{1,0:T(8,128)S(1)}, u32[]{:S(2)}, u32[]{:S(2)}) %collective-permute-start.6) | collective-permute-done | bytes 196640 | tf_op jit(solution)/shard_map/ppermute | solution.py:520
  20.2 1.0 %collective-permute-done.7.x1 = f32[384,128]{1,0:T(8,128)S(1)} collective-permute-done((f32[384,128]{1,0:T(8,128)}, f32[384,128]{1,0:T(8,128)S(1)}, u32[]{:S(2)}, u32[]{:S(2)}) %collective-permute-start.7) | collective-permute-done | bytes 196640 | tf_op jit(solution)/shard_map/ppermute | solution.py:521
  21.2 0.9 copy-done.10
  22.1 0.9 shard_map.159
  23.0 0.5 collective-permute-start.9
  23.5 2.1 %collective-permute-start.8 = (f32[184,128]{1,0:T(8,128)S(1)}, f32[184,128]{1,0:T(8,128)S(1)}, u32[]{:S(2)}, u32[]{:S(2)}) collective-permute-start(f32[184,128]{1,0:T(8,128)S(1)} %get-tuple-element.49), channel_id=1, source_target_pairs={{0,3},{1,0},{2,1},{3,2},{4,7},{5,4},{6,5},{7,6},{8,11},{9,8},{10,9... | collective-permute-start | bytes 282632 | tf_op jit(solution)/shard_map/ppermute | solution.py:517
  25.6 1.0 %collective-permute-start.13 = (f32[216,128]{1,0:T(8,128)S(1)}, f32[216,128]{1,0:T(8,128)S(1)}, u32[]{:S(2)}, u32[]{:S(2)}) collective-permute-start(f32[216,128]{1,0:T(8,128)S(1)} %get-tuple-element.54.w0), channel_id=1, source_target_pairs={{0,1},{1,2},{2,3},{3,0},{4,5},{5,6},{6,7},{7,4},{8,9},{9,10},{10,1... | collective-permute-start | bytes 331784 | tf_op jit(solution)/shard_map/ppermute | solution.py:517
  26.7 0.4 collective-permute-start.12
  27.1 2.8 %collective-permute-start.11 = (f32[216,128]{1,0:T(8,128)S(1)}, f32[216,128]{1,0:T(8,128)S(1)}, u32[]{:S(2)}, u32[]{:S(2)}) collective-permute-start(f32[216,128]{1,0:T(8,128)S(1)} %get-tuple-element.54.w0), channel_id=1, source_target_pairs={{0,3},{1,0},{2,1},{3,2},{4,7},{5,4},{6,5},{7,6},{8,11},{9,8},{10,9... | collective-permute-start | bytes 331784 | tf_op jit(solution)/shard_map/ppermute | solution.py:517
  29.8 1.3 %collective-permute-done.8.h1.east = f32[184,128]{1,0:T(8,128)S(1)} collective-permute-done((f32[184,128]{1,0:T(8,128)S(1)}, f32[184,128]{1,0:T(8,128)S(1)}, u32[]{:S(2)}, u32[]{:S(2)}) %collective-permute-start.8) | collective-permute-done | bytes 94240 | tf_op jit(solution)/shard_map/ppermute | solution.py:517
  31.2 2.7 %collective-permute-done.10.h3.west = f32[184,128]{1,0:T(8,128)S(1)} collective-permute-done((f32[184,128]{1,0:T(8,128)S(1)}, f32[184,128]{1,0:T(8,128)S(1)}, u32[]{:S(2)}, u32[]{:S(2)}) %collective-permute-start.10) | collective-permute-done | bytes 94240 | tf_op jit(solution)/shard_map/ppermute | solution.py:517
  33.9 0.5 collective-permute-start.1
  34.3 2.8 %collective-permute-start.2 = (f32[624,128]{1,0:T(8,128)S(1)}, f32[624,128]{1,0:T(8,128)S(1)}, u32[]{:S(2)}, u32[]{:S(2)}) collective-permute-start(f32[624,128]{1,0:T(8,128)S(1)} %copy-done.16), channel_id=1, source_target_pairs={{0,1},{1,2},{2,3},{3,0},{4,5},{5,6},{6,7},{7,4},{8,9},{9,10},{10,1... | collective-permute-start | bytes 958472 | tf_op jit(solution)/shard_map/ppermute | solution.py:517
  37.1 1.0 %collective-permute-start.4 = (f32[672,128]{1,0:T(8,128)}, f32[672,128]{1,0:T(8,128)S(1)}, u32[]{:S(2)}, u32[]{:S(2)}) collective-permute-start(f32[672,128]{1,0:T(8,128)} %get-tuple-element.43), channel_id=1, source_target_pairs={{0,2},{1,3},{2,0},{3,1},{4,6},{5,7},{6,4},{7,5},{8,10},{9,11},{10,... | collective-permute-start | bytes 1032200 | tf_op jit(solution)/shard_map/ppermute | solution.py:517
  38.2 1.9 %collective-permute-start.5 = (f32[672,128]{1,0:T(8,128)S(1)}, f32[672,128]{1,0:T(8,128)S(1)}, u32[]{:S(2)}, u32[]{:S(2)}) collective-permute-start(f32[672,128]{1,0:T(8,128)S(1)} %copy-done.15), channel_id=1, source_target_pairs={{0,1},{1,2},{2,3},{3,0},{4,5},{5,6},{6,7},{7,4},{8,9},{9,10},{10,1... | collective-permute-start | bytes 1032200 | tf_op jit(solution)/shard_map/ppermute | solution.py:517
  40.1 0.1 fusion.3.damp
  40.3 4.7 %shard_map.161 = (f32[80,128]{1,0:T(8,128)S(1)}, f32[80,128]{1,0:T(8,128)S(1)}) custom-call(f32[216,128]{1,0:T(8,128)S(1)} %get-tuple-element.54.w0, f32[216,128]{1,0:T(8,128)S(1)} %collective-permute-done.11.w1, f32[216,128]{1,0:T(8,128)S(1)} %collective-permute-done.12.w2, f32[216,128]{1,0:T(8,128)S(1)} %collective-permute-done.13.w3, ...), custom_call_target="tpu_custom_call" | custom-call | bytes 24000000 | tf_op jit(solution)/shard_map/pallas_call | solution.py:565
  45.0 4.6 %shard_map.162 = (f32[32,896]{1,0:T(8,128)S(1)}, f32[32,896]{1,0:T(8,128)S(1)}, f32[4,896]{1,0:T(4,128)S(1)}, f32[4,896]{1,0:T(4,128)S(1)}) custom-call(s32[2]{0:T(128)S(1)} %pad_add_fusion.place, s32[32,896]{1,0:T(8,128)S(1)} %copy-done.8, s32[32,896]{1,0:T(8,128)S(1)} %copy-done.9, f32[80,128]{1,0:T(8,128)S(1)} %get-tuple-element.55.heat, ...), custom_call_target="tpu_custom_call" | custom-call | bytes 21000000 | tf_op jit(solution)/shard_map/pallas_call | solution.py:566
  49.6 3.2 %collective-permute-done.3.n1 = f32[672,128]{1,0:T(8,128)S(1)} collective-permute-done((f32[672,128]{1,0:T(8,128)}, f32[672,128]{1,0:T(8,128)S(1)}, u32[]{:S(2)}, u32[]{:S(2)}) %collective-permute-start.3) | collective-permute-done | bytes 344096 | tf_op jit(solution)/shard_map/ppermute | solution.py:517
  52.8 3.1 %collective-permute-done.4.n2 = f32[672,128]{1,0:T(8,128)S(1)} collective-permute-done((f32[672,128]{1,0:T(8,128)}, f32[672,128]{1,0:T(8,128)S(1)}, u32[]{:S(2)}, u32[]{:S(2)}) %collective-permute-start.4) | collective-permute-done | bytes 344096 | tf_op jit(solution)/shard_map/ppermute | solution.py:517
  55.8 4.2 %collective-permute-done.5.n3 = f32[672,128]{1,0:T(8,128)S(1)} collective-permute-done((f32[672,128]{1,0:T(8,128)S(1)}, f32[672,128]{1,0:T(8,128)S(1)}, u32[]{:S(2)}, u32[]{:S(2)}) %collective-permute-start.5) | collective-permute-done | bytes 344096 | tf_op jit(solution)/shard_map/ppermute | solution.py:517
  60.1 14.0 %shard_map.163 = (f32[432,128]{1,0:T(8,128)S(1)}, bf16[192,1152]{1,0:T(8,128)(2,1)S(1)}, bf16[192,1152]{1,0:T(8,128)(2,1)S(1)}) custom-call(f32[624,128]{1,0:T(8,128)S(1)} %copy-done.3, f32[624,128]{1,0:T(8,128)S(1)} %collective-permute-done.m1, f32[624,128]{1,0:T(8,128)S(1)} %collective-permute-done.1.m2, f32[624,128]{1,0:T(8,128)S(1)} %collective-permute-done.2.m3, ...), custom_call_target="tpu_custom_call" | custom-call | bytes 39000000 | tf_op jit(solution)/shard_map/pallas_call | solution.py:573
  74.1 1.3 %collective-permute-start.16 = (f32[432,128]{1,0:T(8,128)S(1)}, f32[432,128]{1,0:T(8,128)S(1)}, u32[]{:S(2)}, u32[]{:S(2)}) collective-permute-start(f32[432,128]{1,0:T(8,128)S(1)} %get-tuple-element.62), channel_id=1, source_target_pairs={{0,2},{1,3},{2,0},{3,1},{4,6},{5,7},{6,4},{7,5},{8,10},{9,11},{10,... | collective-permute-start | bytes 663560 | tf_op jit(solution)/shard_map/ppermute | solution.py:517
  75.5 1.8 %shard_map.164 = (f32[432,128]{1,0:T(8,128)S(1)}, f32[432,128]{1,0:T(8,128)S(1)}) custom-call(bf16[192,1152]{1,0:T(8,128)(2,1)S(1)} %get-tuple-element.58.top.behind, bf16[192,1152]{1,0:T(8,128)(2,1)S(1)} %get-tuple-element.59.rest, bf16[1152,1152]{1,0:T(8,128)(2,1)S(1)} %get-tuple-element.52.bh, bf16[1152,1152]{1,0:T(8,128)(2,1)S(1)} %get-tuple-element.53.bl), custom_call_target="tpu_custom_call" | custom-call | bytes 6000000 | tf_op jit(solution)/shard_map/pallas_call | solution.py:583
  77.2 1.9 %collective-permute-start.15 = (f32[432,128]{1,0:T(8,128)S(1)}, f32[432,128]{1,0:T(8,128)S(1)}, u32[]{:S(2)}, u32[]{:S(2)}) collective-permute-start(f32[432,128]{1,0:T(8,128)S(1)} %get-tuple-element.61), channel_id=1, source_target_pairs={{0,3},{1,0},{2,1},{3,2},{4,7},{5,4},{6,5},{7,6},{8,11},{9,8},{10,9... | collective-permute-start | bytes 663560 | tf_op jit(solution)/shard_map/ppermute | solution.py:517
  79.2 1.0 %collective-permute-start.14 = (f32[432,128]{1,0:T(8,128)S(1)}, f32[432,128]{1,0:T(8,128)S(1)}, u32[]{:S(2)}, u32[]{:S(2)}) collective-permute-start(f32[432,128]{1,0:T(8,128)S(1)} %get-tuple-element.60.behind), channel_id=1, source_target_pairs={{0,1},{1,2},{2,3},{3,0},{4,5},{5,6},{6,7},{7,4},{8,9},{9,10},{10,1... | collective-permute-start | bytes 663560 | tf_op jit(solution)/shard_map/ppermute | solution.py:517
  80.2 6.5 %collective-permute-start.17 = (f32[4,896]{1,0:T(4,128)S(1)}, f32[4,896]{1,0:T(4,128)S(1)}, u32[]{:S(2)}, u32[]{:S(2)}) collective-permute-start(f32[4,896]{1,0:T(4,128)S(1)} %get-tuple-element.57.after), channel_id=1, source_target_pairs={{4,8},{8,4},{12,16},{16,12},{20,24},{24,20},{28,32},{32,28},{36,40... | collective-permute-start | bytes 43016 | tf_op jit(solution)/shard_map/ppermute | solution.py:520
  86.6 2.5 %collective-permute-done.17.x0 = f32[4,896]{1,0:T(4,128)S(1)} collective-permute-done((f32[4,896]{1,0:T(4,128)S(1)}, f32[4,896]{1,0:T(4,128)S(1)}, u32[]{:S(2)}, u32[]{:S(2)}) %collective-permute-start.17) | collective-permute-done | bytes 14368 | tf_op jit(solution)/shard_map/ppermute | solution.py:520
  89.1 0.6 shard_map.168
  89.8 1.0 %collective-permute-start.19 = (f32[40,4]{1,0:T(8,128)S(1)}, f32[40,4]{1,0:T(8,128)S(1)}, u32[]{:S(2)}, u32[]{:S(2)}) collective-permute-start(f32[40,4]{1,0:T(8,128)S(1)} %get-tuple-element.70), channel_id=1, source_target_pairs={{0,3},{1,0},{2,1},{3,2},{4,7},{5,4},{6,5},{7,6},{8,11},{9,8},{10,9... | collective-permute-start | bytes 1928 | tf_op jit(solution)/shard_map/ppermute | solution.py:517
  90.8 1.0 %collective-permute-start.20 = (f32[40,4]{1,0:T(8,128)S(1)}, f32[40,4]{1,0:T(8,128)S(1)}, u32[]{:S(2)}, u32[]{:S(2)}) collective-permute-start(f32[40,4]{1,0:T(8,128)S(1)} %get-tuple-element.71), channel_id=1, source_target_pairs={{0,1},{1,2},{2,3},{3,0},{4,5},{5,6},{6,7},{7,4},{8,9},{9,10},{10,1... | collective-permute-start | bytes 1928 | tf_op jit(solution)/shard_map/ppermute | solution.py:517
  91.8 1.0 shard_map.165.w0
  92.8 0.4 collective-permute-done.19.air_east
  93.1 2.0 %shard_map.169 = f32[4,32,896]{2,1,0:T(8,128)} custom-call(f32[4,32,896]{2,1,0:T(8,128)S(1)} %copy-done, s32[32,896]{1,0:T(8,128)S(1)} %copy-done.1, f32[32,896]{1,0:T(8,128)S(1)} %get-tuple-element.63.heat, f32[32,896]{1,0:T(8,128)S(1)} %get-tuple-element.64.speed, f32[384,128]{1,0:T(8,128)S(1)} %get-tuple-element.65.before, ...), custom_call_target="tpu_custom_call" | custom-call | bytes 9000000 | tf_op jit(solution)/shard_map/pallas_call | solution.py:591
  95.2 1.5 %shard_map.166.half = f32[32,24,288]{2,1,0:T(8,128)} custom-call(s32[2]{0:T(128)S(1)} %pad_add_fusion.place, f32[432,128]{1,0:T(8,128)S(1)} %shard_map.165.w0, f32[432,128]{1,0:T(8,128)S(1)} %collective-permute-done.16.w2), custom_call_target="tpu_custom_call" | custom-call | bytes 3000000 | tf_op jit(solution)/shard_map/pallas_call | solution.py:598
  96.7 1.5 %shard_map.167 = f32[32,24,288]{2,1,0:T(8,128)} custom-call(s32[2]{0:T(128)S(1)} %pad_add_fusion.place, f32[432,128]{1,0:T(8,128)S(1)} %collective-permute-done.14.w1, f32[432,128]{1,0:T(8,128)S(1)} %collective-permute-done.15.w3, f32[32,24,288]{2,1,0:T(8,128)} %shard_map.166.half), custom_call_target="tpu_custom_call", output_to_operand_aliasing={{}: (3, {})} | custom-call | bytes 3000000 | tf_op jit(solution)/shard_map/pallas_call | solution.py:601
  (46 shorter events, 0.2 us)
Async XLA Ops:
  0.6 15.9 %copy-start.4 = (f32[36,1152]{1,0:T(8,128)S(1)}, f32[36,1152]{1,0:T(8,128)}, u32[]{:S(2)}) copy-start(f32[36,1152]{1,0:T(8,128)} %constant.50.clone.with_sin) | copy-start | bytes 497668
  0.6 15.9 %copy-start.5 = (f32[36,1152]{1,0:T(8,128)S(1)}, f32[36,1152]{1,0:T(8,128)}, u32[]{:S(2)}) copy-start(f32[36,1152]{1,0:T(8,128)} %constant.49.clone.with_cos) | copy-start | bytes 497668
  0.7 15.9 %copy-start.6 = (f32[32,1152]{1,0:T(8,128)S(1)}, f32[32,1152]{1,0:T(8,128)}, u32[]{:S(2)}) copy-start(f32[32,1152]{1,0:T(8,128)} %constant.52.clone.sine) | copy-start | bytes 442372
  0.7 15.9 %copy-start.7 = (f32[32,1152]{1,0:T(8,128)S(1)}, f32[32,1152]{1,0:T(8,128)}, u32[]{:S(2)}) copy-start(f32[32,1152]{1,0:T(8,128)} %constant.51.clone.cosine) | copy-start | bytes 442372
  0.7 20.5 %copy-start.1 = (s32[32,896]{1,0:T(8,128)S(1)}, s32[32,896]{1,0:T(8,128)}, u32[]{:S(2)}) copy-start(s32[32,896]{1,0:T(8,128)} %mask.3) | copy-start | bytes 344068
  0.7 20.5 %copy-start = (f32[4,32,896]{2,1,0:T(8,128)S(1)}, f32[4,32,896]{2,1,0:T(8,128)}, u32[]{:S(2)}) copy-start(f32[4,32,896]{2,1,0:T(8,128)} %t.3) | copy-start | bytes 1376260
  0.7 17.4 %copy-start.14 = (s32[192]{0:T(256)S(1)}, s32[192]{0:T(256)}, u32[]{:S(2)}) copy-start(s32[192]{0:T(256)} %param.22) | copy-start | bytes 2308
  5.1 29.2 %copy-start.16 = (f32[624,128]{1,0:T(8,128)S(1)}, f32[624,128]{1,0:T(8,128)}, u32[]{:S(2)}) copy-start(f32[624,128]{1,0:T(8,128)} %get-tuple-element.40) | copy-start | bytes 958468
  5.1 33.1 %copy-start.15 = (f32[672,128]{1,0:T(8,128)S(1)}, f32[672,128]{1,0:T(8,128)}, u32[]{:S(2)}) copy-start(f32[672,128]{1,0:T(8,128)} %get-tuple-element.44) | copy-start | bytes 1032196
  5.1 35.0 %copy-start.11 = (f32[1152]{0:T(1024)S(1)}, f32[1152]{0:T(1024)}, u32[]{:S(2)}) copy-start(f32[1152]{0:T(1024)} %constant.66) | copy-start | bytes 13828
  5.1 35.0 %copy-start.12 = (f32[1152]{0:T(1024)S(1)}, f32[1152]{0:T(1024)}, u32[]{:S(2)}) copy-start(f32[1152]{0:T(1024)} %constant.65) | copy-start | bytes 13828
  5.2 35.0 %copy-start.13 = (pred[1152]{0:T(1024)(128)(4,1)S(1)}, pred[1152]{0:T(1024)(128)(4,1)}, u32[]{:S(2)}) copy-start(pred[1152]{0:T(1024)(128)(4,1)} %constant.63) | copy-start | bytes 3460
  5.2 15.0 %collective-permute-start.6 = (f32[384,128]{1,0:T(8,128)}, f32[384,128]{1,0:T(8,128)S(1)}, u32[]{:S(2)}, u32[]{:S(2)}) collective-permute-start(f32[384,128]{1,0:T(8,128)} %get-tuple-element.45), channel_id=1, source_target_pairs={{4,8},{8,4},{12,16},{16,12},{20,24},{24,20},{28,32},{32,28},{36,40... | collective-permute-start | bytes 589832 | tf_op jit(solution)/shard_map/ppermute | solution.py:520
  15.4 5.8 %collective-permute-start.7 = (f32[384,128]{1,0:T(8,128)}, f32[384,128]{1,0:T(8,128)S(1)}, u32[]{:S(2)}, u32[]{:S(2)}) collective-permute-start(f32[384,128]{1,0:T(8,128)} %get-tuple-element.46), channel_id=1, source_target_pairs={{0,4},{4,0},{8,12},{12,8},{16,20},{20,16},{24,28},{28,24},{32,36},... | collective-permute-start | bytes 589832 | tf_op jit(solution)/shard_map/ppermute | solution.py:521
  15.5 22.7 %collective-permute-start = (f32[624,128]{1,0:T(8,128)}, f32[624,128]{1,0:T(8,128)S(1)}, u32[]{:S(2)}, u32[]{:S(2)}) collective-permute-start(f32[624,128]{1,0:T(8,128)} %get-tuple-element.38), channel_id=1, source_target_pairs={{0,3},{1,0},{2,1},{3,2},{4,7},{5,4},{6,5},{7,6},{8,11},{9,8},{10,9... | collective-permute-start | bytes 958472 | tf_op jit(solution)/shard_map/ppermute | solution.py:517
  21.2 0.9 copy-start.10
  23.0 4.1 %collective-permute-start.9 = (f32[144,128]{1,0:T(8,128)S(1)}, f32[144,128]{1,0:T(8,128)S(1)}, u32[]{:S(2)}, u32[]{:S(2)}) collective-permute-start(f32[144,128]{1,0:T(8,128)S(1)} %get-tuple-element.50), channel_id=1, source_target_pairs={{0,2},{1,3},{2,0},{3,1},{4,6},{5,7},{6,4},{7,5},{8,10},{9,11},{10,... | collective-permute-start | bytes 221192 | tf_op jit(solution)/shard_map/ppermute | solution.py:517
  23.5 7.7 %collective-permute-start.8 = (f32[184,128]{1,0:T(8,128)S(1)}, f32[184,128]{1,0:T(8,128)S(1)}, u32[]{:S(2)}, u32[]{:S(2)}) collective-permute-start(f32[184,128]{1,0:T(8,128)S(1)} %get-tuple-element.49), channel_id=1, source_target_pairs={{0,3},{1,0},{2,1},{3,2},{4,7},{5,4},{6,5},{7,6},{8,11},{9,8},{10,9... | collective-permute-start | bytes 282632 | tf_op jit(solution)/shard_map/ppermute | solution.py:517
  25.6 8.7 %collective-permute-start.13 = (f32[216,128]{1,0:T(8,128)S(1)}, f32[216,128]{1,0:T(8,128)S(1)}, u32[]{:S(2)}, u32[]{:S(2)}) collective-permute-start(f32[216,128]{1,0:T(8,128)S(1)} %get-tuple-element.54.w0), channel_id=1, source_target_pairs={{0,1},{1,2},{2,3},{3,0},{4,5},{5,6},{6,7},{7,4},{8,9},{9,10},{10,1... | collective-permute-start | bytes 331784 | tf_op jit(solution)/shard_map/ppermute | solution.py:517
  26.7 10.4 %collective-permute-start.12 = (f32[216,128]{1,0:T(8,128)S(1)}, f32[216,128]{1,0:T(8,128)S(1)}, u32[]{:S(2)}, u32[]{:S(2)}) collective-permute-start(f32[216,128]{1,0:T(8,128)S(1)} %get-tuple-element.54.w0), channel_id=1, source_target_pairs={{0,2},{1,3},{2,0},{3,1},{4,6},{5,7},{6,4},{7,5},{8,10},{9,11},{10,... | collective-permute-start | bytes 331784 | tf_op jit(solution)/shard_map/ppermute | solution.py:517
  27.1 10.0 %collective-permute-start.11 = (f32[216,128]{1,0:T(8,128)S(1)}, f32[216,128]{1,0:T(8,128)S(1)}, u32[]{:S(2)}, u32[]{:S(2)}) collective-permute-start(f32[216,128]{1,0:T(8,128)S(1)} %get-tuple-element.54.w0), channel_id=1, source_target_pairs={{0,3},{1,0},{2,1},{3,2},{4,7},{5,4},{6,5},{7,6},{8,11},{9,8},{10,9... | collective-permute-start | bytes 331784 | tf_op jit(solution)/shard_map/ppermute | solution.py:517
  31.2 2.7 %collective-permute-start.10 = (f32[184,128]{1,0:T(8,128)S(1)}, f32[184,128]{1,0:T(8,128)S(1)}, u32[]{:S(2)}, u32[]{:S(2)}) collective-permute-start(f32[184,128]{1,0:T(8,128)S(1)} %get-tuple-element.51), channel_id=1, source_target_pairs={{0,1},{1,2},{2,3},{3,0},{4,5},{5,6},{6,7},{7,4},{8,9},{9,10},{10,1... | collective-permute-start | bytes 282632 | tf_op jit(solution)/shard_map/ppermute | solution.py:517
  33.9 15.7 %collective-permute-start.1 = (f32[624,128]{1,0:T(8,128)}, f32[624,128]{1,0:T(8,128)S(1)}, u32[]{:S(2)}, u32[]{:S(2)}) collective-permute-start(f32[624,128]{1,0:T(8,128)} %get-tuple-element.39), channel_id=1, source_target_pairs={{0,2},{1,3},{2,0},{3,1},{4,6},{5,7},{6,4},{7,5},{8,10},{9,11},{10,... | collective-permute-start | bytes 958472 | tf_op jit(solution)/shard_map/ppermute | solution.py:517
  34.3 15.2 %collective-permute-start.2 = (f32[624,128]{1,0:T(8,128)S(1)}, f32[624,128]{1,0:T(8,128)S(1)}, u32[]{:S(2)}, u32[]{:S(2)}) collective-permute-start(f32[624,128]{1,0:T(8,128)S(1)} %copy-done.16), channel_id=1, source_target_pairs={{0,1},{1,2},{2,3},{3,0},{4,5},{5,6},{6,7},{7,4},{8,9},{9,10},{10,1... | collective-permute-start | bytes 958472 | tf_op jit(solution)/shard_map/ppermute | solution.py:517
  37.1 15.7 %collective-permute-start.3 = (f32[672,128]{1,0:T(8,128)}, f32[672,128]{1,0:T(8,128)S(1)}, u32[]{:S(2)}, u32[]{:S(2)}) collective-permute-start(f32[672,128]{1,0:T(8,128)} %get-tuple-element.42), channel_id=1, source_target_pairs={{0,3},{1,0},{2,1},{3,2},{4,7},{5,4},{6,5},{7,6},{8,11},{9,8},{10,9... | collective-permute-start | bytes 1032200 | tf_op jit(solution)/shard_map/ppermute | solution.py:517
  37.1 18.7 %collective-permute-start.4 = (f32[672,128]{1,0:T(8,128)}, f32[672,128]{1,0:T(8,128)S(1)}, u32[]{:S(2)}, u32[]{:S(2)}) collective-permute-start(f32[672,128]{1,0:T(8,128)} %get-tuple-element.43), channel_id=1, source_target_pairs={{0,2},{1,3},{2,0},{3,1},{4,6},{5,7},{6,4},{7,5},{8,10},{9,11},{10,... | collective-permute-start | bytes 1032200 | tf_op jit(solution)/shard_map/ppermute | solution.py:517
  38.2 21.9 %collective-permute-start.5 = (f32[672,128]{1,0:T(8,128)S(1)}, f32[672,128]{1,0:T(8,128)S(1)}, u32[]{:S(2)}, u32[]{:S(2)}) collective-permute-start(f32[672,128]{1,0:T(8,128)S(1)} %copy-done.15), channel_id=1, source_target_pairs={{0,1},{1,2},{2,3},{3,0},{4,5},{5,6},{6,7},{7,4},{8,9},{9,10},{10,1... | collective-permute-start | bytes 1032200 | tf_op jit(solution)/shard_map/ppermute | solution.py:517
  40.2 4.7 %copy-start.8 = (s32[32,896]{1,0:T(8,128)S(1)}, s32[32,896]{1,0:T(8,128)}, u32[]{:S(2)}) copy-start(s32[32,896]{1,0:T(8,128)} %rows.1) | copy-start | bytes 344068
  40.2 4.7 %copy-start.9 = (s32[32,896]{1,0:T(8,128)S(1)}, s32[32,896]{1,0:T(8,128)}, u32[]{:S(2)}) copy-start(s32[32,896]{1,0:T(8,128)} %cols.1) | copy-start | bytes 344068
  40.2 19.8 %copy-start.2 = (f32[672,128]{1,0:T(8,128)S(1)}, f32[672,128]{1,0:T(8,128)}, u32[]{:S(2)}) copy-start(f32[672,128]{1,0:T(8,128)} %get-tuple-element.41.n0) | copy-start | bytes 1032196
  40.3 19.8 %copy-start.3 = (f32[624,128]{1,0:T(8,128)S(1)}, f32[624,128]{1,0:T(8,128)}, u32[]{:S(2)}) copy-start(f32[624,128]{1,0:T(8,128)} %get-tuple-element.37.m0) | copy-start | bytes 958468
  74.1 21.0 %collective-permute-start.16 = (f32[432,128]{1,0:T(8,128)S(1)}, f32[432,128]{1,0:T(8,128)S(1)}, u32[]{:S(2)}, u32[]{:S(2)}) collective-permute-start(f32[432,128]{1,0:T(8,128)S(1)} %get-tuple-element.62), channel_id=1, source_target_pairs={{0,2},{1,3},{2,0},{3,1},{4,6},{5,7},{6,4},{7,5},{8,10},{9,11},{10,... | collective-permute-start | bytes 663560 | tf_op jit(solution)/shard_map/ppermute | solution.py:517
  77.2 19.4 %collective-permute-start.15 = (f32[432,128]{1,0:T(8,128)S(1)}, f32[432,128]{1,0:T(8,128)S(1)}, u32[]{:S(2)}, u32[]{:S(2)}) collective-permute-start(f32[432,128]{1,0:T(8,128)S(1)} %get-tuple-element.61), channel_id=1, source_target_pairs={{0,3},{1,0},{2,1},{3,2},{4,7},{5,4},{6,5},{7,6},{8,11},{9,8},{10,9... | collective-permute-start | bytes 663560 | tf_op jit(solution)/shard_map/ppermute | solution.py:517
  79.2 17.5 %collective-permute-start.14 = (f32[432,128]{1,0:T(8,128)S(1)}, f32[432,128]{1,0:T(8,128)S(1)}, u32[]{:S(2)}, u32[]{:S(2)}) collective-permute-start(f32[432,128]{1,0:T(8,128)S(1)} %get-tuple-element.60.behind), channel_id=1, source_target_pairs={{0,1},{1,2},{2,3},{3,0},{4,5},{5,6},{6,7},{7,4},{8,9},{9,10},{10,1... | collective-permute-start | bytes 663560 | tf_op jit(solution)/shard_map/ppermute | solution.py:517
  80.2 6.5 %collective-permute-start.18 = (f32[4,896]{1,0:T(4,128)S(1)}, f32[4,896]{1,0:T(4,128)S(1)}, u32[]{:S(2)}, u32[]{:S(2)}) collective-permute-start(f32[4,896]{1,0:T(4,128)S(1)} %get-tuple-element.67), channel_id=1, source_target_pairs={{0,4},{4,0},{8,12},{12,8},{16,20},{20,16},{24,28},{28,24},{32,36},... | collective-permute-start | bytes 43016 | tf_op jit(solution)/shard_map/ppermute | solution.py:521
  80.2 9.0 %collective-permute-start.17 = (f32[4,896]{1,0:T(4,128)S(1)}, f32[4,896]{1,0:T(4,128)S(1)}, u32[]{:S(2)}, u32[]{:S(2)}) collective-permute-start(f32[4,896]{1,0:T(4,128)S(1)} %get-tuple-element.57.after), channel_id=1, source_target_pairs={{4,8},{8,4},{12,16},{16,12},{20,24},{24,20},{28,32},{32,28},{36,40... | collective-permute-start | bytes 43016 | tf_op jit(solution)/shard_map/ppermute | solution.py:520
  89.8 3.4 %collective-permute-start.19 = (f32[40,4]{1,0:T(8,128)S(1)}, f32[40,4]{1,0:T(8,128)S(1)}, u32[]{:S(2)}, u32[]{:S(2)}) collective-permute-start(f32[40,4]{1,0:T(8,128)S(1)} %get-tuple-element.70), channel_id=1, source_target_pairs={{0,3},{1,0},{2,1},{3,2},{4,7},{5,4},{6,5},{7,6},{8,11},{9,8},{10,9... | collective-permute-start | bytes 1928 | tf_op jit(solution)/shard_map/ppermute | solution.py:517
  90.8 2.4 %collective-permute-start.20 = (f32[40,4]{1,0:T(8,128)S(1)}, f32[40,4]{1,0:T(8,128)S(1)}, u32[]{:S(2)}, u32[]{:S(2)}) collective-permute-start(f32[40,4]{1,0:T(8,128)S(1)} %get-tuple-element.71), channel_id=1, source_target_pairs={{0,1},{1,2},{2,3},{3,0},{4,5},{5,6},{6,7},{7,4},{8,9},{9,10},{10,1... | collective-permute-start | bytes 1928 | tf_op jit(solution)/shard_map/ppermute | solution.py:517

commit v4 on v3

--- a/solution.py
+++ b/solution.py
@@ -55,7 +55,7 @@
 
 
 LEVEL_AT, OCEAN_AT, SEA_AT, LAT_WIRE = 288, 312, 368, 384
-FIRST, SECOND = FT + 192, 2 * FT - 192
+FIRST, SECOND = FT + 240, 2 * FT - 240
 STRIP_AT, RIM_WIRE, WINDOW = 144, 184, 216
 TILES = OCOLS // 128
 THIRD, TABLE = 40, 80
@@ -65,8 +65,8 @@
     if f == 0:
         return ((first, 0), (first, 192), (first, 384))
     if f == 1:
-        return ((first, FT), (second, 0), (second, 192))
-    return ((second, 240), (second, 432), (second, 624))
+        return ((first, FT), (second, 0), (first, FT + 192))
+    return ((second, 192), (second, 384), (second, 576))
 
 
 def cross(place, a, b, first, second):

time: 99 us -> 99 us (level)
  no operation moved by 1% of the time
where the time goes in v4:
time: 99 us; the launch traced here: 98.3 us
  Pallas kernels  38.4 us (39%)
  starting transfers between devices  37 us (37%)
  waiting for transfers between devices  20.3 us (21%)
  between operations  1.14 us (1%)
  local copies, waits for them, and re-layouts  0.99 us (1%)
    ppermute x17, starting transfers between devices, along(): return lax.ppermute(x, 'lon', [(i, (i + s) % LONS) for i in range(LONS)])  20.3 us
    ppermute x2, starting transfers between devices, across(): got = lax.ppermute(first, 'lat', swaps[0])  16.7 us
    ppermute x17, waiting for transfers between devices, along(): return lax.ppermute(x, 'lon', [(i, (i + s) % LONS) for i in range(LONS)])  14.9 us
    pallas_call x1, Pallas kernels, per_device(): call(bulk_kernel, [sds(FT, 128)] + [sds(ROWS * LB, NLON, dtype=bf16)] * 2...  14 us
    pallas_call x1, Pallas kernels, per_device(): call(bottom_kernel, [sds(TABLE, 128)] * 2, n_in=7, cost=cost(8))  4.67 us
    pallas_call x1, Pallas kernels, per_device(): call(pick_kernel, [sds(OROWS, OCOLS)] * 2 + [sds(4, OCOLS)] * 2, smem=1,...  4.6 us
    pallas_call x1, Pallas kernels, per_device(): call(pack_kernel, [sds(FIRST, 128)] * 4 + [sds(SECOND, 128)] * 4 + [sds(L...  4.4 us
    ppermute x2, waiting for transfers between devices, across(): got = lax.ppermute(first, 'lat', swaps[0])  4.36 us
  transfers between devices with their start and end apart: 21, of which 9 were waited for; matrix products, arithmetic and copies ran while one was open for 0% of the time, Pallas kernels for 19%

profile of v4, /device:TPU:3, one launch (start us, length us, event | category | flops | bytes accessed | tf_op | source)
XLA Modules:
  0.0 98.3 jit_solution(13082517178867594471)
XLA Ops:
  0.6 0.0 copy-start.4
  0.6 0.0 copy-start.5
  0.7 0.0 copy-start.7
  0.7 4.4 %shard_map.158 = (f32[672,128]{1,0:T(8,128)}, f32[672,128]{1,0:T(8,128)}, f32[672,128]{1,0:T(8,128)}, f32[672,128]{1,0:T(8,128)}, f32[624,128]{1,0:T(8,128)}, /*...) custom-call(f32[32,24,288]{2,1,0:T(8,128)} %q_in.1, ...), custom_call_target="tpu_custom_call" | custom-call | bytes 15000000 | tf_op jit(solution)/shard_map/pallas_call | solution.py:523
  5.1 0.0 copy-start.11
  5.2 0.0 copy-start.12
  5.2 10.2 %collective-permute-start.6 = (f32[384,128]{1,0:T(8,128)}, f32[384,128]{1,0:T(8,128)S(1)}, u32[]{:S(2)}, u32[]{:S(2)}) collective-permute-start(f32[384,128]{1,0:T(8,128)} %get-tuple-element.45), channel_id=1, source_target_pairs={{4,8},{8,4},{12,16},{16,12},{20,24},{24,20},{28,32},{32,28},{36,40... | collective-permute-start | bytes 589832 | tf_op jit(solution)/shard_map/ppermute | solution.py:520
  15.4 0.1 collective-permute-start.7
  15.5 1.0 %collective-permute-start.3 = (f32[624,128]{1,0:T(8,128)}, f32[624,128]{1,0:T(8,128)S(1)}, u32[]{:S(2)}, u32[]{:S(2)}) collective-permute-start(f32[624,128]{1,0:T(8,128)} %get-tuple-element.42), channel_id=1, source_target_pairs={{0,3},{1,0},{2,1},{3,2},{4,7},{5,4},{6,5},{7,6},{8,11},{9,8},{10,9... | collective-permute-start | bytes 958472 | tf_op jit(solution)/shard_map/ppermute | solution.py:517
  16.6 1.5 %shard_map.160 = (bf16[1152,1152]{1,0:T(8,128)(2,1)S(1)}, bf16[1152,1152]{1,0:T(8,128)(2,1)S(1)}) custom-call(f32[36,1152]{1,0:T(8,128)S(1)} %copy-done.5, f32[36,1152]{1,0:T(8,128)S(1)} %copy-done.4, f32[32,1152]{1,0:T(8,128)S(1)} %copy-done.7, f32[32,1152]{1,0:T(8,128)S(1)} %copy-done.6), custom_call_target="tpu_custom_call" | custom-call | bytes 9000000 | tf_op jit(solution)/shard_map/pallas_call | solution.py:547
  18.1 0.2 compare_reduce_fusion
  18.3 0.1 pad_add_fusion.place
  18.3 1.9 %collective-permute-done.6.x0 = f32[384,128]{1,0:T(8,128)S(1)} collective-permute-done((f32[384,128]{1,0:T(8,128)}, f32[384,128]{1,0:T(8,128)S(1)}, u32[]{:S(2)}, u32[]{:S(2)}) %collective-permute-start.6) | collective-permute-done | bytes 196640 | tf_op jit(solution)/shard_map/ppermute | solution.py:520
  20.2 1.0 %collective-permute-done.7.x1 = f32[384,128]{1,0:T(8,128)S(1)} collective-permute-done((f32[384,128]{1,0:T(8,128)}, f32[384,128]{1,0:T(8,128)S(1)}, u32[]{:S(2)}, u32[]{:S(2)}) %collective-permute-start.7) | collective-permute-done | bytes 196640 | tf_op jit(solution)/shard_map/ppermute | solution.py:521
  21.2 0.9 copy-done.10
  22.1 0.9 shard_map.159
  23.0 0.5 collective-permute-start.9
  23.5 2.1 %collective-permute-start.8 = (f32[184,128]{1,0:T(8,128)S(1)}, f32[184,128]{1,0:T(8,128)S(1)}, u32[]{:S(2)}, u32[]{:S(2)}) collective-permute-start(f32[184,128]{1,0:T(8,128)S(1)} %get-tuple-element.49), channel_id=1, source_target_pairs={{0,3},{1,0},{2,1},{3,2},{4,7},{5,4},{6,5},{7,6},{8,11},{9,8},{10,9... | collective-permute-start | bytes 282632 | tf_op jit(solution)/shard_map/ppermute | solution.py:517
  25.6 1.0 %collective-permute-start.13 = (f32[216,128]{1,0:T(8,128)S(1)}, f32[216,128]{1,0:T(8,128)S(1)}, u32[]{:S(2)}, u32[]{:S(2)}) collective-permute-start(f32[216,128]{1,0:T(8,128)S(1)} %get-tuple-element.54.w0), channel_id=1, source_target_pairs={{0,1},{1,2},{2,3},{3,0},{4,5},{5,6},{6,7},{7,4},{8,9},{9,10},{10,1... | collective-permute-start | bytes 331784 | tf_op jit(solution)/shard_map/ppermute | solution.py:517
  26.7 0.4 collective-permute-start.12
  27.1 2.8 %collective-permute-start.11 = (f32[216,128]{1,0:T(8,128)S(1)}, f32[216,128]{1,0:T(8,128)S(1)}, u32[]{:S(2)}, u32[]{:S(2)}) collective-permute-start(f32[216,128]{1,0:T(8,128)S(1)} %get-tuple-element.54.w0), channel_id=1, source_target_pairs={{0,3},{1,0},{2,1},{3,2},{4,7},{5,4},{6,5},{7,6},{8,11},{9,8},{10,9... | collective-permute-start | bytes 331784 | tf_op jit(solution)/shard_map/ppermute | solution.py:517
  29.8 1.3 %collective-permute-done.8.h1.east = f32[184,128]{1,0:T(8,128)S(1)} collective-permute-done((f32[184,128]{1,0:T(8,128)S(1)}, f32[184,128]{1,0:T(8,128)S(1)}, u32[]{:S(2)}, u32[]{:S(2)}) %collective-permute-start.8) | collective-permute-done | bytes 94240 | tf_op jit(solution)/shard_map/ppermute | solution.py:517
  31.2 2.7 %collective-permute-done.10.h3.west = f32[184,128]{1,0:T(8,128)S(1)} collective-permute-done((f32[184,128]{1,0:T(8,128)S(1)}, f32[184,128]{1,0:T(8,128)S(1)}, u32[]{:S(2)}, u32[]{:S(2)}) %collective-permute-start.10) | collective-permute-done | bytes 94240 | tf_op jit(solution)/shard_map/ppermute | solution.py:517
  33.9 0.5 collective-permute-start.4
  34.4 2.8 %collective-permute-start.5 = (f32[624,128]{1,0:T(8,128)S(1)}, f32[624,128]{1,0:T(8,128)S(1)}, u32[]{:S(2)}, u32[]{:S(2)}) collective-permute-start(f32[624,128]{1,0:T(8,128)S(1)} %copy-done.16), channel_id=1, source_target_pairs={{0,1},{1,2},{2,3},{3,0},{4,5},{5,6},{6,7},{7,4},{8,9},{9,10},{10,1... | collective-permute-start | bytes 958472 | tf_op jit(solution)/shard_map/ppermute | solution.py:517
  37.1 1.0 %collective-permute-start.1 = (f32[672,128]{1,0:T(8,128)}, f32[672,128]{1,0:T(8,128)S(1)}, u32[]{:S(2)}, u32[]{:S(2)}) collective-permute-start(f32[672,128]{1,0:T(8,128)} %get-tuple-element.39), channel_id=1, source_target_pairs={{0,2},{1,3},{2,0},{3,1},{4,6},{5,7},{6,4},{7,5},{8,10},{9,11},{10,... | collective-permute-start | bytes 1032200 | tf_op jit(solution)/shard_map/ppermute | solution.py:517
  38.2 1.9 %collective-permute-start.2 = (f32[672,128]{1,0:T(8,128)S(1)}, f32[672,128]{1,0:T(8,128)S(1)}, u32[]{:S(2)}, u32[]{:S(2)}) collective-permute-start(f32[672,128]{1,0:T(8,128)S(1)} %copy-done.15), channel_id=1, source_target_pairs={{0,1},{1,2},{2,3},{3,0},{4,5},{5,6},{6,7},{7,4},{8,9},{9,10},{10,1... | collective-permute-start | bytes 1032200 | tf_op jit(solution)/shard_map/ppermute | solution.py:517
  40.1 0.1 fusion.3.damp
  40.3 4.7 %shard_map.161 = (f32[80,128]{1,0:T(8,128)S(1)}, f32[80,128]{1,0:T(8,128)S(1)}) custom-call(f32[216,128]{1,0:T(8,128)S(1)} %get-tuple-element.54.w0, f32[216,128]{1,0:T(8,128)S(1)} %collective-permute-done.11.w1, f32[216,128]{1,0:T(8,128)S(1)} %collective-permute-done.12.w2, f32[216,128]{1,0:T(8,128)S(1)} %collective-permute-done.13.w3, ...), custom_call_target="tpu_custom_call" | custom-call | bytes 24000000 | tf_op jit(solution)/shard_map/pallas_call | solution.py:565
  45.0 4.6 %shard_map.162 = (f32[32,896]{1,0:T(8,128)S(1)}, f32[32,896]{1,0:T(8,128)S(1)}, f32[4,896]{1,0:T(4,128)S(1)}, f32[4,896]{1,0:T(4,128)S(1)}) custom-call(s32[2]{0:T(128)S(1)} %pad_add_fusion.place, s32[32,896]{1,0:T(8,128)S(1)} %copy-done.8, s32[32,896]{1,0:T(8,128)S(1)} %copy-done.9, f32[80,128]{1,0:T(8,128)S(1)} %get-tuple-element.55.heat, ...), custom_call_target="tpu_custom_call" | custom-call | bytes 21000000 | tf_op jit(solution)/shard_map/pallas_call | solution.py:566
  49.6 3.2 %collective-permute-done.m1 = f32[672,128]{1,0:T(8,128)S(1)} collective-permute-done((f32[672,128]{1,0:T(8,128)}, f32[672,128]{1,0:T(8,128)S(1)}, u32[]{:S(2)}, u32[]{:S(2)}) %collective-permute-start) | collective-permute-done | bytes 344096 | tf_op jit(solution)/shard_map/ppermute | solution.py:517
  52.8 3.1 %collective-permute-done.1.m2 = f32[672,128]{1,0:T(8,128)S(1)} collective-permute-done((f32[672,128]{1,0:T(8,128)}, f32[672,128]{1,0:T(8,128)S(1)}, u32[]{:S(2)}, u32[]{:S(2)}) %collective-permute-start.1) | collective-permute-done | bytes 344096 | tf_op jit(solution)/shard_map/ppermute | solution.py:517
  55.8 4.2 %collective-permute-done.2.m3 = f32[672,128]{1,0:T(8,128)S(1)} collective-permute-done((f32[672,128]{1,0:T(8,128)S(1)}, f32[672,128]{1,0:T(8,128)S(1)}, u32[]{:S(2)}, u32[]{:S(2)}) %collective-permute-start.2) | collective-permute-done | bytes 344096 | tf_op jit(solution)/shard_map/ppermute | solution.py:517
  60.1 14.0 %shard_map.163 = (f32[432,128]{1,0:T(8,128)S(1)}, bf16[192,1152]{1,0:T(8,128)(2,1)S(1)}, bf16[192,1152]{1,0:T(8,128)(2,1)S(1)}) custom-call(f32[672,128]{1,0:T(8,128)S(1)} %copy-done.2, f32[672,128]{1,0:T(8,128)S(1)} %collective-permute-done.m1, f32[672,128]{1,0:T(8,128)S(1)} %collective-permute-done.1.m2, f32[672,128]{1,0:T(8,128)S(1)} %collective-permute-done.2.m3, ...), custom_call_target="tpu_custom_call" | custom-call | bytes 39000000 | tf_op jit(solution)/shard_map/pallas_call | solution.py:573
  74.1 1.3 %collective-permute-start.16 = (f32[432,128]{1,0:T(8,128)S(1)}, f32[432,128]{1,0:T(8,128)S(1)}, u32[]{:S(2)}, u32[]{:S(2)}) collective-permute-start(f32[432,128]{1,0:T(8,128)S(1)} %get-tuple-element.62), channel_id=1, source_target_pairs={{0,2},{1,3},{2,0},{3,1},{4,6},{5,7},{6,4},{7,5},{8,10},{9,11},{10,... | collective-permute-start | bytes 663560 | tf_op jit(solution)/shard_map/ppermute | solution.py:517
  75.5 1.8 %shard_map.164 = (f32[432,128]{1,0:T(8,128)S(1)}, f32[432,128]{1,0:T(8,128)S(1)}) custom-call(bf16[192,1152]{1,0:T(8,128)(2,1)S(1)} %get-tuple-element.58.top.behind, bf16[192,1152]{1,0:T(8,128)(2,1)S(1)} %get-tuple-element.59.rest, bf16[1152,1152]{1,0:T(8,128)(2,1)S(1)} %get-tuple-element.52.bh, bf16[1152,1152]{1,0:T(8,128)(2,1)S(1)} %get-tuple-element.53.bl), custom_call_target="tpu_custom_call" | custom-call | bytes 6000000 | tf_op jit(solution)/shard_map/pallas_call | solution.py:583
  77.2 1.9 %collective-permute-start.15 = (f32[432,128]{1,0:T(8,128)S(1)}, f32[432,128]{1,0:T(8,128)S(1)}, u32[]{:S(2)}, u32[]{:S(2)}) collective-permute-start(f32[432,128]{1,0:T(8,128)S(1)} %get-tuple-element.61), channel_id=1, source_target_pairs={{0,3},{1,0},{2,1},{3,2},{4,7},{5,4},{6,5},{7,6},{8,11},{9,8},{10,9... | collective-permute-start | bytes 663560 | tf_op jit(solution)/shard_map/ppermute | solution.py:517
  79.2 1.0 %collective-permute-start.14 = (f32[432,128]{1,0:T(8,128)S(1)}, f32[432,128]{1,0:T(8,128)S(1)}, u32[]{:S(2)}, u32[]{:S(2)}) collective-permute-start(f32[432,128]{1,0:T(8,128)S(1)} %get-tuple-element.60.behind), channel_id=1, source_target_pairs={{0,1},{1,2},{2,3},{3,0},{4,5},{5,6},{6,7},{7,4},{8,9},{9,10},{10,1... | collective-permute-start | bytes 663560 | tf_op jit(solution)/shard_map/ppermute | solution.py:517
  80.2 6.5 %collective-permute-start.17 = (f32[4,896]{1,0:T(4,128)S(1)}, f32[4,896]{1,0:T(4,128)S(1)}, u32[]{:S(2)}, u32[]{:S(2)}) collective-permute-start(f32[4,896]{1,0:T(4,128)S(1)} %get-tuple-element.57.after), channel_id=1, source_target_pairs={{4,8},{8,4},{12,16},{16,12},{20,24},{24,20},{28,32},{32,28},{36,40... | collective-permute-start | bytes 43016 | tf_op jit(solution)/shard_map/ppermute | solution.py:520
  86.6 2.5 %collective-permute-done.17.x0 = f32[4,896]{1,0:T(4,128)S(1)} collective-permute-done((f32[4,896]{1,0:T(4,128)S(1)}, f32[4,896]{1,0:T(4,128)S(1)}, u32[]{:S(2)}, u32[]{:S(2)}) %collective-permute-start.17) | collective-permute-done | bytes 14368 | tf_op jit(solution)/shard_map/ppermute | solution.py:520
  89.1 0.6 shard_map.168
  89.7 1.0 %collective-permute-start.19 = (f32[40,4]{1,0:T(8,128)S(1)}, f32[40,4]{1,0:T(8,128)S(1)}, u32[]{:S(2)}, u32[]{:S(2)}) collective-permute-start(f32[40,4]{1,0:T(8,128)S(1)} %get-tuple-element.70), channel_id=1, source_target_pairs={{0,3},{1,0},{2,1},{3,2},{4,7},{5,4},{6,5},{7,6},{8,11},{9,8},{10,9... | collective-permute-start | bytes 1928 | tf_op jit(solution)/shard_map/ppermute | solution.py:517
  90.8 1.0 %collective-permute-start.20 = (f32[40,4]{1,0:T(8,128)S(1)}, f32[40,4]{1,0:T(8,128)S(1)}, u32[]{:S(2)}, u32[]{:S(2)}) collective-permute-start(f32[40,4]{1,0:T(8,128)S(1)} %get-tuple-element.71), channel_id=1, source_target_pairs={{0,1},{1,2},{2,3},{3,0},{4,5},{5,6},{6,7},{7,4},{8,9},{9,10},{10,1... | collective-permute-start | bytes 1928 | tf_op jit(solution)/shard_map/ppermute | solution.py:517
  91.8 1.0 shard_map.165.w0
  92.8 0.4 collective-permute-done.19.air_east
  93.1 2.0 %shard_map.169 = f32[4,32,896]{2,1,0:T(8,128)} custom-call(f32[4,32,896]{2,1,0:T(8,128)S(1)} %copy-done, s32[32,896]{1,0:T(8,128)S(1)} %copy-done.1, f32[32,896]{1,0:T(8,128)S(1)} %get-tuple-element.63.heat, f32[32,896]{1,0:T(8,128)S(1)} %get-tuple-element.64.speed, f32[384,128]{1,0:T(8,128)S(1)} %get-tuple-element.65.before, ...), custom_call_target="tpu_custom_call" | custom-call | bytes 9000000 | tf_op jit(solution)/shard_map/pallas_call | solution.py:591
  95.2 1.5 %shard_map.166.half = f32[32,24,288]{2,1,0:T(8,128)} custom-call(s32[2]{0:T(128)S(1)} %pad_add_fusion.place, f32[432,128]{1,0:T(8,128)S(1)} %shard_map.165.w0, f32[432,128]{1,0:T(8,128)S(1)} %collective-permute-done.16.w2), custom_call_target="tpu_custom_call" | custom-call | bytes 3000000 | tf_op jit(solution)/shard_map/pallas_call | solution.py:598
  96.7 1.5 %shard_map.167 = f32[32,24,288]{2,1,0:T(8,128)} custom-call(s32[2]{0:T(128)S(1)} %pad_add_fusion.place, f32[432,128]{1,0:T(8,128)S(1)} %collective-permute-done.14.w1, f32[432,128]{1,0:T(8,128)S(1)} %collective-permute-done.15.w3, f32[32,24,288]{2,1,0:T(8,128)} %shard_map.166.half), custom_call_target="tpu_custom_call", output_to_operand_aliasing={{}: (3, {})} | custom-call | bytes 3000000 | tf_op jit(solution)/shard_map/pallas_call | solution.py:601
  (46 shorter events, 0.2 us)
Async XLA Ops:
  0.6 15.9 %copy-start.4 = (f32[36,1152]{1,0:T(8,128)S(1)}, f32[36,1152]{1,0:T(8,128)}, u32[]{:S(2)}) copy-start(f32[36,1152]{1,0:T(8,128)} %constant.50.clone.with_sin) | copy-start | bytes 497668
  0.6 15.9 %copy-start.5 = (f32[36,1152]{1,0:T(8,128)S(1)}, f32[36,1152]{1,0:T(8,128)}, u32[]{:S(2)}) copy-start(f32[36,1152]{1,0:T(8,128)} %constant.49.clone.with_cos) | copy-start | bytes 497668
  0.7 15.9 %copy-start.6 = (f32[32,1152]{1,0:T(8,128)S(1)}, f32[32,1152]{1,0:T(8,128)}, u32[]{:S(2)}) copy-start(f32[32,1152]{1,0:T(8,128)} %constant.52.clone.sine) | copy-start | bytes 442372
  0.7 15.9 %copy-start.7 = (f32[32,1152]{1,0:T(8,128)S(1)}, f32[32,1152]{1,0:T(8,128)}, u32[]{:S(2)}) copy-start(f32[32,1152]{1,0:T(8,128)} %constant.51.clone.cosine) | copy-start | bytes 442372
  0.7 20.5 %copy-start.1 = (s32[32,896]{1,0:T(8,128)S(1)}, s32[32,896]{1,0:T(8,128)}, u32[]{:S(2)}) copy-start(s32[32,896]{1,0:T(8,128)} %mask.3) | copy-start | bytes 344068
  0.7 20.5 %copy-start = (f32[4,32,896]{2,1,0:T(8,128)S(1)}, f32[4,32,896]{2,1,0:T(8,128)}, u32[]{:S(2)}) copy-start(f32[4,32,896]{2,1,0:T(8,128)} %t.3) | copy-start | bytes 1376260
  0.7 17.4 %copy-start.14 = (s32[192]{0:T(256)S(1)}, s32[192]{0:T(256)}, u32[]{:S(2)}) copy-start(s32[192]{0:T(256)} %param.22) | copy-start | bytes 2308
  5.1 29.2 %copy-start.16 = (f32[624,128]{1,0:T(8,128)S(1)}, f32[624,128]{1,0:T(8,128)}, u32[]{:S(2)}) copy-start(f32[624,128]{1,0:T(8,128)} %get-tuple-element.44) | copy-start | bytes 958468
  5.1 33.0 %copy-start.15 = (f32[672,128]{1,0:T(8,128)S(1)}, f32[672,128]{1,0:T(8,128)}, u32[]{:S(2)}) copy-start(f32[672,128]{1,0:T(8,128)} %get-tuple-element.40) | copy-start | bytes 1032196
  5.1 35.0 %copy-start.11 = (f32[1152]{0:T(1024)S(1)}, f32[1152]{0:T(1024)}, u32[]{:S(2)}) copy-start(f32[1152]{0:T(1024)} %constant.66) | copy-start | bytes 13828
  5.2 35.0 %copy-start.12 = (f32[1152]{0:T(1024)S(1)}, f32[1152]{0:T(1024)}, u32[]{:S(2)}) copy-start(f32[1152]{0:T(1024)} %constant.65) | copy-start | bytes 13828
  5.2 35.0 %copy-start.13 = (pred[1152]{0:T(1024)(128)(4,1)S(1)}, pred[1152]{0:T(1024)(128)(4,1)}, u32[]{:S(2)}) copy-start(pred[1152]{0:T(1024)(128)(4,1)} %constant.63) | copy-start | bytes 3460
  5.2 15.0 %collective-permute-start.6 = (f32[384,128]{1,0:T(8,128)}, f32[384,128]{1,0:T(8,128)S(1)}, u32[]{:S(2)}, u32[]{:S(2)}) collective-permute-start(f32[384,128]{1,0:T(8,128)} %get-tuple-element.45), channel_id=1, source_target_pairs={{4,8},{8,4},{12,16},{16,12},{20,24},{24,20},{28,32},{32,28},{36,40... | collective-permute-start | bytes 589832 | tf_op jit(solution)/shard_map/ppermute | solution.py:520
  15.4 5.8 %collective-permute-start.7 = (f32[384,128]{1,0:T(8,128)}, f32[384,128]{1,0:T(8,128)S(1)}, u32[]{:S(2)}, u32[]{:S(2)}) collective-permute-start(f32[384,128]{1,0:T(8,128)} %get-tuple-element.46), channel_id=1, source_target_pairs={{0,4},{4,0},{8,12},{12,8},{16,20},{20,16},{24,28},{28,24},{32,36},... | collective-permute-start | bytes 589832 | tf_op jit(solution)/shard_map/ppermute | solution.py:521
  15.5 22.7 %collective-permute-start.3 = (f32[624,128]{1,0:T(8,128)}, f32[624,128]{1,0:T(8,128)S(1)}, u32[]{:S(2)}, u32[]{:S(2)}) collective-permute-start(f32[624,128]{1,0:T(8,128)} %get-tuple-element.42), channel_id=1, source_target_pairs={{0,3},{1,0},{2,1},{3,2},{4,7},{5,4},{6,5},{7,6},{8,11},{9,8},{10,9... | collective-permute-start | bytes 958472 | tf_op jit(solution)/shard_map/ppermute | solution.py:517
  21.2 0.9 copy-start.10
  23.0 4.1 %collective-permute-start.9 = (f32[144,128]{1,0:T(8,128)S(1)}, f32[144,128]{1,0:T(8,128)S(1)}, u32[]{:S(2)}, u32[]{:S(2)}) collective-permute-start(f32[144,128]{1,0:T(8,128)S(1)} %get-tuple-element.50), channel_id=1, source_target_pairs={{0,2},{1,3},{2,0},{3,1},{4,6},{5,7},{6,4},{7,5},{8,10},{9,11},{10,... | collective-permute-start | bytes 221192 | tf_op jit(solution)/shard_map/ppermute | solution.py:517
  23.5 7.7 %collective-permute-start.8 = (f32[184,128]{1,0:T(8,128)S(1)}, f32[184,128]{1,0:T(8,128)S(1)}, u32[]{:S(2)}, u32[]{:S(2)}) collective-permute-start(f32[184,128]{1,0:T(8,128)S(1)} %get-tuple-element.49), channel_id=1, source_target_pairs={{0,3},{1,0},{2,1},{3,2},{4,7},{5,4},{6,5},{7,6},{8,11},{9,8},{10,9... | collective-permute-start | bytes 282632 | tf_op jit(solution)/shard_map/ppermute | solution.py:517
  25.6 8.7 %collective-permute-start.13 = (f32[216,128]{1,0:T(8,128)S(1)}, f32[216,128]{1,0:T(8,128)S(1)}, u32[]{:S(2)}, u32[]{:S(2)}) collective-permute-start(f32[216,128]{1,0:T(8,128)S(1)} %get-tuple-element.54.w0), channel_id=1, source_target_pairs={{0,1},{1,2},{2,3},{3,0},{4,5},{5,6},{6,7},{7,4},{8,9},{9,10},{10,1... | collective-permute-start | bytes 331784 | tf_op jit(solution)/shard_map/ppermute | solution.py:517
  26.7 10.4 %collective-permute-start.12 = (f32[216,128]{1,0:T(8,128)S(1)}, f32[216,128]{1,0:T(8,128)S(1)}, u32[]{:S(2)}, u32[]{:S(2)}) collective-permute-start(f32[216,128]{1,0:T(8,128)S(1)} %get-tuple-element.54.w0), channel_id=1, source_target_pairs={{0,2},{1,3},{2,0},{3,1},{4,6},{5,7},{6,4},{7,5},{8,10},{9,11},{10,... | collective-permute-start | bytes 331784 | tf_op jit(solution)/shard_map/ppermute | solution.py:517
  27.1 10.0 %collective-permute-start.11 = (f32[216,128]{1,0:T(8,128)S(1)}, f32[216,128]{1,0:T(8,128)S(1)}, u32[]{:S(2)}, u32[]{:S(2)}) collective-permute-start(f32[216,128]{1,0:T(8,128)S(1)} %get-tuple-element.54.w0), channel_id=1, source_target_pairs={{0,3},{1,0},{2,1},{3,2},{4,7},{5,4},{6,5},{7,6},{8,11},{9,8},{10,9... | collective-permute-start | bytes 331784 | tf_op jit(solution)/shard_map/ppermute | solution.py:517
  31.2 2.7 %collective-permute-start.10 = (f32[184,128]{1,0:T(8,128)S(1)}, f32[184,128]{1,0:T(8,128)S(1)}, u32[]{:S(2)}, u32[]{:S(2)}) collective-permute-start(f32[184,128]{1,0:T(8,128)S(1)} %get-tuple-element.51), channel_id=1, source_target_pairs={{0,1},{1,2},{2,3},{3,0},{4,5},{5,6},{6,7},{7,4},{8,9},{9,10},{10,1... | collective-permute-start | bytes 282632 | tf_op jit(solution)/shard_map/ppermute | solution.py:517
  33.9 15.7 %collective-permute-start.4 = (f32[624,128]{1,0:T(8,128)}, f32[624,128]{1,0:T(8,128)S(1)}, u32[]{:S(2)}, u32[]{:S(2)}) collective-permute-start(f32[624,128]{1,0:T(8,128)} %get-tuple-element.43), channel_id=1, source_target_pairs={{0,2},{1,3},{2,0},{3,1},{4,6},{5,7},{6,4},{7,5},{8,10},{9,11},{10,... | collective-permute-start | bytes 958472 | tf_op jit(solution)/shard_map/ppermute | solution.py:517
  34.4 15.2 %collective-permute-start.5 = (f32[624,128]{1,0:T(8,128)S(1)}, f32[624,128]{1,0:T(8,128)S(1)}, u32[]{:S(2)}, u32[]{:S(2)}) collective-permute-start(f32[624,128]{1,0:T(8,128)S(1)} %copy-done.16), channel_id=1, source_target_pairs={{0,1},{1,2},{2,3},{3,0},{4,5},{5,6},{6,7},{7,4},{8,9},{9,10},{10,1... | collective-permute-start | bytes 958472 | tf_op jit(solution)/shard_map/ppermute | solution.py:517
  37.1 15.7 %collective-permute-start = (f32[672,128]{1,0:T(8,128)}, f32[672,128]{1,0:T(8,128)S(1)}, u32[]{:S(2)}, u32[]{:S(2)}) collective-permute-start(f32[672,128]{1,0:T(8,128)} %get-tuple-element.38), channel_id=1, source_target_pairs={{0,3},{1,0},{2,1},{3,2},{4,7},{5,4},{6,5},{7,6},{8,11},{9,8},{10,9... | collective-permute-start | bytes 1032200 | tf_op jit(solution)/shard_map/ppermute | solution.py:517
  37.1 18.7 %collective-permute-start.1 = (f32[672,128]{1,0:T(8,128)}, f32[672,128]{1,0:T(8,128)S(1)}, u32[]{:S(2)}, u32[]{:S(2)}) collective-permute-start(f32[672,128]{1,0:T(8,128)} %get-tuple-element.39), channel_id=1, source_target_pairs={{0,2},{1,3},{2,0},{3,1},{4,6},{5,7},{6,4},{7,5},{8,10},{9,11},{10,... | collective-permute-start | bytes 1032200 | tf_op jit(solution)/shard_map/ppermute | solution.py:517
  38.2 21.9 %collective-permute-start.2 = (f32[672,128]{1,0:T(8,128)S(1)}, f32[672,128]{1,0:T(8,128)S(1)}, u32[]{:S(2)}, u32[]{:S(2)}) collective-permute-start(f32[672,128]{1,0:T(8,128)S(1)} %copy-done.15), channel_id=1, source_target_pairs={{0,1},{1,2},{2,3},{3,0},{4,5},{5,6},{6,7},{7,4},{8,9},{9,10},{10,1... | collective-permute-start | bytes 1032200 | tf_op jit(solution)/shard_map/ppermute | solution.py:517
  40.2 4.7 %copy-start.8 = (s32[32,896]{1,0:T(8,128)S(1)}, s32[32,896]{1,0:T(8,128)}, u32[]{:S(2)}) copy-start(s32[32,896]{1,0:T(8,128)} %rows.1) | copy-start | bytes 344068
  40.2 4.7 %copy-start.9 = (s32[32,896]{1,0:T(8,128)S(1)}, s32[32,896]{1,0:T(8,128)}, u32[]{:S(2)}) copy-start(s32[32,896]{1,0:T(8,128)} %cols.1) | copy-start | bytes 344068
  40.3 19.8 %copy-start.2 = (f32[672,128]{1,0:T(8,128)S(1)}, f32[672,128]{1,0:T(8,128)}, u32[]{:S(2)}) copy-start(f32[672,128]{1,0:T(8,128)} %get-tuple-element.37.m0) | copy-start | bytes 1032196
  40.3 19.8 %copy-start.3 = (f32[624,128]{1,0:T(8,128)S(1)}, f32[624,128]{1,0:T(8,128)}, u32[]{:S(2)}) copy-start(f32[624,128]{1,0:T(8,128)} %get-tuple-element.41.n0) | copy-start | bytes 958468
  74.1 21.0 %collective-permute-start.16 = (f32[432,128]{1,0:T(8,128)S(1)}, f32[432,128]{1,0:T(8,128)S(1)}, u32[]{:S(2)}, u32[]{:S(2)}) collective-permute-start(f32[432,128]{1,0:T(8,128)S(1)} %get-tuple-element.62), channel_id=1, source_target_pairs={{0,2},{1,3},{2,0},{3,1},{4,6},{5,7},{6,4},{7,5},{8,10},{9,11},{10,... | collective-permute-start | bytes 663560 | tf_op jit(solution)/shard_map/ppermute | solution.py:517
  77.2 19.4 %collective-permute-start.15 = (f32[432,128]{1,0:T(8,128)S(1)}, f32[432,128]{1,0:T(8,128)S(1)}, u32[]{:S(2)}, u32[]{:S(2)}) collective-permute-start(f32[432,128]{1,0:T(8,128)S(1)} %get-tuple-element.61), channel_id=1, source_target_pairs={{0,3},{1,0},{2,1},{3,2},{4,7},{5,4},{6,5},{7,6},{8,11},{9,8},{10,9... | collective-permute-start | bytes 663560 | tf_op jit(solution)/shard_map/ppermute | solution.py:517
  79.2 17.5 %collective-permute-start.14 = (f32[432,128]{1,0:T(8,128)S(1)}, f32[432,128]{1,0:T(8,128)S(1)}, u32[]{:S(2)}, u32[]{:S(2)}) collective-permute-start(f32[432,128]{1,0:T(8,128)S(1)} %get-tuple-element.60.behind), channel_id=1, source_target_pairs={{0,1},{1,2},{2,3},{3,0},{4,5},{5,6},{6,7},{7,4},{8,9},{9,10},{10,1... | collective-permute-start | bytes 663560 | tf_op jit(solution)/shard_map/ppermute | solution.py:517
  80.2 6.5 %collective-permute-start.18 = (f32[4,896]{1,0:T(4,128)S(1)}, f32[4,896]{1,0:T(4,128)S(1)}, u32[]{:S(2)}, u32[]{:S(2)}) collective-permute-start(f32[4,896]{1,0:T(4,128)S(1)} %get-tuple-element.67), channel_id=1, source_target_pairs={{0,4},{4,0},{8,12},{12,8},{16,20},{20,16},{24,28},{28,24},{32,36},... | collective-permute-start | bytes 43016 | tf_op jit(solution)/shard_map/ppermute | solution.py:521
  80.2 9.0 %collective-permute-start.17 = (f32[4,896]{1,0:T(4,128)S(1)}, f32[4,896]{1,0:T(4,128)S(1)}, u32[]{:S(2)}, u32[]{:S(2)}) collective-permute-start(f32[4,896]{1,0:T(4,128)S(1)} %get-tuple-element.57.after), channel_id=1, source_target_pairs={{4,8},{8,4},{12,16},{16,12},{20,24},{24,20},{28,32},{32,28},{36,40... | collective-permute-start | bytes 43016 | tf_op jit(solution)/shard_map/ppermute | solution.py:520
  89.7 3.4 %collective-permute-start.19 = (f32[40,4]{1,0:T(8,128)S(1)}, f32[40,4]{1,0:T(8,128)S(1)}, u32[]{:S(2)}, u32[]{:S(2)}) collective-permute-start(f32[40,4]{1,0:T(8,128)S(1)} %get-tuple-element.70), channel_id=1, source_target_pairs={{0,3},{1,0},{2,1},{3,2},{4,7},{5,4},{6,5},{7,6},{8,11},{9,8},{10,9... | collective-permute-start | bytes 1928 | tf_op jit(solution)/shard_map/ppermute | solution.py:517
  90.8 2.4 %collective-permute-start.20 = (f32[40,4]{1,0:T(8,128)S(1)}, f32[40,4]{1,0:T(8,128)S(1)}, u32[]{:S(2)}, u32[]{:S(2)}) collective-permute-start(f32[40,4]{1,0:T(8,128)S(1)} %get-tuple-element.71), channel_id=1, source_target_pairs={{0,1},{1,2},{2,3},{3,0},{4,5},{5,6},{6,7},{7,4},{8,9},{9,10},{10,1... | collective-permute-start | bytes 1928 | tf_op jit(solution)/shard_map/ppermute | solution.py:517
